TPU v7x, 32 devices: a whole 2x2x4 slice. The times are simulated.
32 devices in a mesh: grp: 4 (over y, x), dom: 8 (over z, core).
Axes of the slice: x: 2, y: 2, z: 4, core: 2. Of those that a mesh axis runs over, the one named last changes fastest.
Arguments:
- u_int: bfloat16 [16384, 192], P(('grp', 'dom')), may hold values from -1.59375 to 1.59375
- u_if: bfloat16 [5632, 192], P('dom'), may hold values from -1.59375 to 1.59375
- load_int: float32 [16384, 192], P(('grp', 'dom')), may hold values from -6 to 6
- load_if: float32 [5632, 192], P('dom'), may hold values from -6 to 6
- conn: int32 [65536, 8], P(('grp', 'dom')), may hold values from 0 to 1343
- send_map: int32 [128, 32], P(('grp', 'dom')), may hold values from 0 to 1215
- counts: int32 [32], P(('grp', 'dom')), may hold values from 256 to 2048, as said below
- elem_size: float32 [65536], P(('grp', 'dom')), may hold values from 0.7 to 1.4
- stiffness: float32 [65536], P(('grp', 'dom')), may hold values from 0.5 to 2
- yield_stress: float32 [65536], P(('grp', 'dom')), may hold values from 0.5 to 2
- relax_rate: float32 [65536], P(('grp', 'dom')), may hold values from 0.02 to 0.5
- stress_init: float32 [48, 65536], P(None, ('grp', 'dom')), may hold values from -6 to 6
- kinv_int: bfloat16 [49152, 1536], P(('grp', 'dom')), may hold values from -0.15625 to 0.15625
- sinv: bfloat16 [16896, 16896], P('grp', 'dom'), may hold values from -0.0625 to 0.0625
Outputs:
- du_int: float32 [16384, 192], P(('grp', 'dom'))
- du_if: float32 [5632, 192], P(('grp', 'dom'))
- stress_end: float32 [48, 65536], P(None, ('grp', 'dom'))
Inputs may be any that keep to these rules, and one draw needn't show every extreme that they name: `counts`: every partition has at least 256 live elements and some partition has exactly 2048.
All inputs are finite; a program needn't handle non-finite values.
Results may differ from a plain program's by a relative error of at most 0.0046.
Values may be sent and summed in bfloat16 or wider, within the bound.
No kernel may reach another device: no remote copies, remote signals or barrier semaphores. Data moves between devices by JAX's collectives and lax.ppermute only.
A program may use at most 128 MiB of HBM per device.

v0:
```python
import math

import jax
import jax.numpy as jnp
import numpy as np
from jax import lax
from jax.sharding import PartitionSpec as P

TIMES = 32


POISSON = 0.3
HIGHEST = lax.Precision.HIGHEST


def passed_along(shard, axis, by):
    peers = lax.axis_size(axis)
    return lax.ppermute(shard, axis, [(i, (i + by) % peers) for i in range(peers)])


def strain_table():
    gauss = 1.0 / math.sqrt(3.0)
    table = np.zeros((6, 8, 8, 3))
    for point in range(8):
        coords = [((point >> bit & 1) * 2 - 1) * gauss for bit in range(3)]
        for corner in range(8):
            signs = [(corner >> bit & 1) * 2 - 1 for bit in range(3)]
            deriv = []
            for axis in range(3):
                value = signs[axis] / 8.0
                for other in range(3):
                    if other != axis:
                        value = value * (1.0 + signs[other] * coords[other])
                deriv.append(value)
            table[0, point, corner, 0] = deriv[0]
            table[1, point, corner, 1] = deriv[1]
            table[2, point, corner, 2] = deriv[2]
            table[3, point, corner, 0] = deriv[1]
            table[3, point, corner, 1] = deriv[0]
            table[4, point, corner, 1] = deriv[2]
            table[4, point, corner, 2] = deriv[1]
            table[5, point, corner, 2] = deriv[0]
            table[5, point, corner, 0] = deriv[2]
    return jnp.asarray(table.reshape(48, 24), jnp.float32).astype(jnp.bfloat16)


def time_tables(times, fourier):
    theta = 2.0 * math.pi * (np.arange(times) + 0.3) / times
    synthesis = np.zeros((fourier, times))
    for column in range(fourier):
        harmonic = column // 2
        if column % 2 == 0:
            synthesis[column] = np.cos(harmonic * theta)
        else:
            synthesis[column] = np.sin((harmonic + 1) * theta)
    analysis = synthesis.T * (2.0 / times)
    analysis[:, 0] = 1.0 / times
    return (jnp.asarray(synthesis, jnp.float32), jnp.asarray(analysis, jnp.float32))


def element_update(rows, conn_dev, count, size_e, stiff_e, yield_e, rate_e, stress_zero):
    table = strain_table().reshape(48, 8, 3)
    width = rows.shape[1]
    fourier = width // 3
    buffer_rows = rows.shape[0]
    synthesis, analysis = time_tables(TIMES, fourier)
    elems = conn_dev.shape[0]
    columns = jnp.transpose(rows)
    corner_index = jnp.transpose(conn_dev).reshape(-1)
    gathered = jnp.take(columns, corner_index, axis=1).reshape(3, fourier, 8, elems)
    strain_hat = jnp.einsum("qai,ifae->qfe", table, gathered, preferred_element_type=jnp.float32)
    strain = jnp.einsum("fm,qfe->mqe", synthesis, strain_hat, precision=HIGHEST) * (2.0 / size_e)
    delta = strain - jnp.roll(strain, 1, axis=0)
    delta = delta.reshape(delta.shape[0], 6, 8, elems)
    lame_first = POISSON / ((1.0 + POISSON) * (1.0 - 2.0 * POISSON))
    shear_mod = 1.0 / (2.0 * (1.0 + POISSON))
    coef = jnp.asarray(
        np.array([2.0 * shear_mod] * 3 + [shear_mod] * 3).reshape(6, 1, 1), jnp.float32
    )
    normal_mask = jnp.asarray(
        np.array([1.0, 1.0, 1.0, 0.0, 0.0, 0.0]).reshape(6, 1, 1), jnp.float32
    )
    stress_start = stress_zero.reshape(6, 8, elems)

    def advance(stress, step_delta):
        trace = step_delta[0] + step_delta[1] + step_delta[2]
        increment = coef * step_delta + lame_first * normal_mask * trace[None]
        stress = stress + stiff_e * increment - rate_e * yield_e * jnp.tanh(stress / yield_e)
        return (stress, stress)

    final, history = lax.scan(advance, stress_start, delta, unroll=8)
    live = (jnp.arange(elems) < count).astype(jnp.float32)
    history = history.reshape(history.shape[0], 48, elems)
    stress_hat = jnp.einsum("mf,mqe->fqe", analysis, history, precision=HIGHEST)
    forces = jnp.einsum("qai,fqe->ifae", table.astype(jnp.float32), stress_hat, precision=HIGHEST)
    forces = forces * (size_e * size_e * 0.25 * live)
    forces = forces.reshape(width, 8 * elems)
    assembled = jnp.zeros((width, buffer_rows), jnp.float32).at[:, corner_index].add(forces)
    return (final.reshape(48, elems) * live, jnp.transpose(assembled))


def per_device(
    u_int,
    u_if,
    load_int,
    load_if,
    conn,
    send_map,
    counts,
    elem_size,
    stiffness,
    yield_stress,
    relax_rate,
    stress_init,
    kinv_int,
    sinv,
):
    width = u_int.shape[1]
    fourier = width // 3
    int_nodes = u_int.shape[0]
    neighbours = send_map.shape[0]
    slots = send_map.shape[1]
    reach = neighbours // 2
    offsets = list(range(-reach, 0)) + list(range(1, reach + 1))
    local = jnp.concatenate([u_int, u_if], axis=0)
    local_rows = local.shape[0]
    blocks = jnp.take(local, send_map.reshape(-1), axis=0).reshape(neighbours, slots, width)
    halo = jnp.stack(
        [
            passed_along(blocks[slot_index], "dom", offsets[slot_index])
            for slot_index in range(neighbours)
        ],
        axis=0,
    )
    buffer = jnp.concatenate([local, halo.reshape(neighbours * slots, width)], axis=0)
    stress_end, assembled = element_update(
        buffer, conn, counts[0], elem_size, stiffness, yield_stress, relax_rate, stress_init
    )
    owned = assembled[:local_rows]
    back = assembled[local_rows:].reshape(neighbours, slots, width)
    returned = jnp.stack(
        [
            passed_along(back[slot_index], "dom", -offsets[slot_index])
            for slot_index in range(neighbours)
        ],
        axis=0,
    )
    owned = owned + jax.ops.segment_sum(
        returned.reshape(neighbours * slots, width), send_map.reshape(-1), num_segments=local_rows
    )
    r_int = load_int - owned[:int_nodes]
    group_force = lax.psum(owned[int_nodes:], "grp")
    r_if = load_if - group_force
    rhs_int = r_int.astype(jnp.bfloat16).reshape(3 * int_nodes, fourier)
    rhs_if = r_if.astype(jnp.bfloat16).reshape(3 * r_if.shape[0], fourier)
    dom_count = lax.axis_size("dom")
    out_rows = sinv.shape[0] // 3 // dom_count
    du_if = lax.psum_scatter(
        jnp.dot(sinv, rhs_if, preferred_element_type=jnp.float32).reshape(
            out_rows * lax.axis_size("dom"), width
        ),
        "dom",
        scatter_dimension=0,
        tiled=True,
    )
    du_int = jnp.dot(kinv_int, rhs_int, preferred_element_type=jnp.float32).reshape(
        int_nodes, width
    )
    return (du_int, du_if, stress_end)


def solution(mesh):
    return jax.shard_map(
        per_device,
        mesh=mesh,
        in_specs=(
            P(("grp", "dom"), None),
            P("dom", None),
            P(("grp", "dom"), None),
            P("dom", None),
            P(("grp", "dom"), None),
            P(("grp", "dom"), None),
            P(("grp", "dom")),
            P(("grp", "dom")),
            P(("grp", "dom")),
            P(("grp", "dom")),
            P(("grp", "dom")),
            P(None, ("grp", "dom")),
            P(("grp", "dom"), None),
            P("grp", "dom"),
        ),
        out_specs=(P(("grp", "dom"), None), P(("grp", "dom"), None), P(None, ("grp", "dom"))),
        check_vma=False,
    )
```

profile of v0, /device:TPU:0, one launch (start us, length us, event | category | flops | bytes accessed | tf_op | source)
XLA Modules:
  0.0 602.3 jit_solution(17403107908922040519)
XLA Ops:
  8.7 1.1 copy.32
  9.9 1.1 copy.31
  12.1 5.1 collective-permute-start
  21.5 1.3 broadcast_divide_fusion
  23.7 64.9 %gather_fusion.1 = bf16[16384,192]{1,0:T(8,128)(2,1)} fusion(bf16[192,1344]{0,1:T(8,128)(2,1)S(1)} %maximum_bitcast_fusion, s32[16384]{0:T(1024)S(1)} %broadcast_clamp_fusion), kind=kCustom, calls=%fused_computation.1 | custom fusion | bytes 12648448 | tf_op jit(solution)/shard_map/jit(_take)/gather | solution.py:70
  88.6 10.1 %copy.33 = bf16[192,16384]{1,0:T(8,128)(2,1)} copy(bf16[192,16384]{0,1:T(8,128)(2,1)} %bitcast.275) | data formatting | bytes 12582912 | tf_op jit(solution)/shard_map/jit(_take)/gather | solution.py:70
  98.8 7.8 %copy.83 = bf16[24,8,8,2048]{3,2,1,0:T(8,128)(2,1)S(1)} copy(bf16[24,8,8,2048]{3,1,2,0:T(8,128)(2,1)} %bitcast.276) | data formatting | bytes 12582912
  106.6 10.1 %convolution_bitcast_fusion = f32[48,64,2048,1]{2,0,3,1:T(8,128)} fusion(pred[8,2048]{1,0:T(8,128)(4,1)S(1)} %compare_and_fusion, bf16[48,8,3,1]{0,1,2,3:T(8,128)(2,1)S(1)} %copy-done.19, bf16[3,64,8,2048]{3,2,1,0:T(8,128)(2,1)S(1)} %bitcast.268), kind=kOutput, calls=%fused_computation.128 | convolution fusion | flops 305135616 | bytes 31475968 | tf_op jit(solution)/shard_map/qai,ifae->qfe/dot_general | solution.py:71
  116.7 38.1 %multiply_bitcast_fusion.1 = f32[32,48,2048]{2,0,1:T(8,128)S(1)} fusion(f32[2048]{0:T(1024)S(1)} %get-tuple-element.225, f32[64,32,1]{0,1,2:T(8,128)S(1)} %copy-done.22, f32[48,64,2048,1]{2,0,3,1:T(8,128)} %convolution_bitcast_fusion), kind=kOutput, calls=%fused_computation.126 | convolution fusion | flops 2419064832 | bytes 37765120 | tf_op jit(solution)/shard_map/fm,qfe->mqe/dot_general | solution.py:72
  155.2 6.0 %maximum_subtract_fusion = f32[32,48,2048]{2,0,1:T(8,128)} fusion(f32[32,48,2048]{2,0,1:T(8,128)S(1)} %multiply_bitcast_fusion.1, f32[31,48,2048]{2,0,1:T(8,128)S(1)} %bitcast.269, f32[1,48,2048]{2,0,1:T(1,128)S(1)} %slice.355), kind=kLoop, calls=%fused_computation.122 | loop fusion | flops 6291456 | bytes 37748736 | tf_op jit(solution)/shard_map/sub | solution.py:73
  161.3 121.9 %while.15 = (s32[]{:T(128)}, f32[6,8,2048]{2,1,0:T(8,128)S(1)}, f32[4,8,6,8,2048]{4,3,2,1,0:T(8,128)}, f32[2048]{0:T(1024)}, f32[4,8,6,8,2048]{4,1,0,3,2:T(8,128...) while((s32[]{:T(128)}, f32[6,8,2048]{2,1,0:T(8,128)S(1)}, ...), condition=%wide.region_1.2_spmd.clone, body=%wide.region_0.1_spmd.sunk.clone.sunk | while | flops 9699336 | bytes 34575964 | solution.py:91
  161.5 8.0 %constant_dynamic-slice_fusion.34 = (f32[1,1,1,8,2048]{4,1,0,3,2:T(1,128)}, f32[1,1,1,8,2048]{4,1,0,3,2:T(1,128)}, f32[1,1,1,8,2048]{4,1,0,3,2:T(1,128)}, f32[1,...) fusion(f32[4,8,6,8,2048]{4,1,0,3,2:T(8,128)} %get-tuple-element, ...), kind=kLoop, calls=%fused_computation.104.clone.1 | loop fusion | bytes 3145760 | tf_op jit(solution)/shard_map/while/body/eval_jaxpr/slice | solution.py:86
  170.2 12.2 %constant_dynamic-slice_fusion.35 = (f32[1,1,6,8,2048]{4,1,0,3,2:T(1,128)S(1)}, f32[1,1,6,8,2048]{4,1,0,3,2:T(1,128)S(1)}, f32[1,1,6,8,2048]{4,1,0,3,2:T(1,128)S...) fusion(f32[4,8,6,8,2048]{4,1,0,3,2:T(8,128)} %get-tuple-element, ...), kind=kLoop, calls=%fused_computation.100.clone.1 | loop fusion | bytes 6291488 | tf_op jit(solution)/shard_map/while/body/slice | solution.py:91
  182.5 1.3 bitcast_dynamic-update-slice_fusion.18
  183.8 1.3 bitcast_dynamic-update-slice_fusion.19
  185.2 1.1 fusion.89
  186.3 1.0 bitcast_dynamic-update-slice_fusion.20
  187.2 1.2 bitcast_dynamic-update-slice_fusion.21
  190.2 1.8 bitcast_dynamic-update-slice_fusion.26
  192.0 7.5 %constant_dynamic-slice_fusion.34 = (f32[1,1,1,8,2048]{4,1,0,3,2:T(1,128)}, f32[1,1,1,8,2048]{4,1,0,3,2:T(1,128)}, f32[1,1,1,8,2048]{4,1,0,3,2:T(1,128)}, f32[1,...) fusion(f32[4,8,6,8,2048]{4,1,0,3,2:T(8,128)} %get-tuple-element, ...), kind=kLoop, calls=%fused_computation.104.clone.1 | loop fusion | bytes 3145760 | tf_op jit(solution)/shard_map/while/body/eval_jaxpr/slice | solution.py:86
  200.3 12.6 %constant_dynamic-slice_fusion.35 = (f32[1,1,6,8,2048]{4,1,0,3,2:T(1,128)S(1)}, f32[1,1,6,8,2048]{4,1,0,3,2:T(1,128)S(1)}, f32[1,1,6,8,2048]{4,1,0,3,2:T(1,128)S...) fusion(f32[4,8,6,8,2048]{4,1,0,3,2:T(8,128)} %get-tuple-element, ...), kind=kLoop, calls=%fused_computation.100.clone.1 | loop fusion | bytes 6291488 | tf_op jit(solution)/shard_map/while/body/slice | solution.py:91
  213.1 1.3 bitcast_dynamic-update-slice_fusion.18
  214.4 1.3 bitcast_dynamic-update-slice_fusion.19
  215.7 1.1 fusion.89
  216.8 1.0 bitcast_dynamic-update-slice_fusion.20
  217.8 1.2 bitcast_dynamic-update-slice_fusion.21
  220.8 1.9 bitcast_dynamic-update-slice_fusion.26
  222.7 7.8 %constant_dynamic-slice_fusion.34 = (f32[1,1,1,8,2048]{4,1,0,3,2:T(1,128)}, f32[1,1,1,8,2048]{4,1,0,3,2:T(1,128)}, f32[1,1,1,8,2048]{4,1,0,3,2:T(1,128)}, f32[1,...) fusion(f32[4,8,6,8,2048]{4,1,0,3,2:T(8,128)} %get-tuple-element, ...), kind=kLoop, calls=%fused_computation.104.clone.1 | loop fusion | bytes 3145760 | tf_op jit(solution)/shard_map/while/body/eval_jaxpr/slice | solution.py:86
  231.2 12.4 %constant_dynamic-slice_fusion.35 = (f32[1,1,6,8,2048]{4,1,0,3,2:T(1,128)S(1)}, f32[1,1,6,8,2048]{4,1,0,3,2:T(1,128)S(1)}, f32[1,1,6,8,2048]{4,1,0,3,2:T(1,128)S...) fusion(f32[4,8,6,8,2048]{4,1,0,3,2:T(8,128)} %get-tuple-element, ...), kind=kLoop, calls=%fused_computation.100.clone.1 | loop fusion | bytes 6291488 | tf_op jit(solution)/shard_map/while/body/slice | solution.py:91
  243.7 1.3 bitcast_dynamic-update-slice_fusion.18
  245.0 1.3 bitcast_dynamic-update-slice_fusion.19
  246.4 1.1 fusion.89
  247.5 1.0 bitcast_dynamic-update-slice_fusion.20
  248.4 1.2 bitcast_dynamic-update-slice_fusion.21
  251.4 1.9 bitcast_dynamic-update-slice_fusion.26
  253.3 7.7 %constant_dynamic-slice_fusion.34 = (f32[1,1,1,8,2048]{4,1,0,3,2:T(1,128)}, f32[1,1,1,8,2048]{4,1,0,3,2:T(1,128)}, f32[1,1,1,8,2048]{4,1,0,3,2:T(1,128)}, f32[1,...) fusion(f32[4,8,6,8,2048]{4,1,0,3,2:T(8,128)} %get-tuple-element, ...), kind=kLoop, calls=%fused_computation.104.clone.1 | loop fusion | bytes 3145760 | tf_op jit(solution)/shard_map/while/body/eval_jaxpr/slice | solution.py:86
  261.7 11.7 %constant_dynamic-slice_fusion.35 = (f32[1,1,6,8,2048]{4,1,0,3,2:T(1,128)S(1)}, f32[1,1,6,8,2048]{4,1,0,3,2:T(1,128)S(1)}, f32[1,1,6,8,2048]{4,1,0,3,2:T(1,128)S...) fusion(f32[4,8,6,8,2048]{4,1,0,3,2:T(8,128)} %get-tuple-element, ...), kind=kLoop, calls=%fused_computation.100.clone.1 | loop fusion | bytes 6291488 | tf_op jit(solution)/shard_map/while/body/slice | solution.py:91
  273.6 1.3 bitcast_dynamic-update-slice_fusion.18
  274.9 1.3 bitcast_dynamic-update-slice_fusion.19
  276.2 1.1 fusion.89
  277.4 1.0 bitcast_dynamic-update-slice_fusion.20
  278.3 1.2 bitcast_dynamic-update-slice_fusion.21
  281.3 1.9 bitcast_dynamic-update-slice_fusion.26
  283.2 34.2 %fusion.55 = f32[64,48,2048,1]{2,0,1,3:T(8,128)} fusion(f32[32,64,1]{1,0,2:T(8,128)} %constant.84, f32[32,48,2048]{2,1,0:T(8,128)} %bitcast.274), kind=kOutput, calls=%fused_computation.127 | convolution fusion | flops 2415919104 | bytes 37756928 | tf_op jit(solution)/shard_map/mf,mqe->fqe/dot_general | solution.py:94
  317.4 31.7 %multiply_bitcast_fusion = f32[3,64,8,2048]{3,2,0,1:T(8,128)} fusion(f32[2048]{0:T(1024)S(1)} %copy-done.21, bf16[48,8,3,1]{0,1,2,3:T(8,128)(2,1)S(1)} %copy-done.20, f32[64,48,2048,1]{2,0,1,3:T(8,128)} %fusion.55), kind=kOutput, calls=%fused_computation.125 | convolution fusion | flops 1815085056 | bytes 37759232 | tf_op jit(solution)/shard_map/qai,fqe->ifae/dot_general | solution.py:95
  349.1 11.3 %copy.35 = f32[3,64,8,2048]{3,2,1,0:T(8,128)} copy(f32[3,64,8,2048]{3,2,0,1:T(8,128)} %multiply_bitcast_fusion) | data formatting | bytes 25165824 | tf_op jit(solution)/shard_map/mul | solution.py:96
  360.4 21.3 %copy.84 = f32[24,8,8,2048]{3,1,2,0:T(8,128)} copy(f32[24,8,8,2048]{3,2,1,0:T(8,128)} %bitcast.273) | data formatting | bytes 25165824
  381.7 14.7 %copy.36 = f32[16384,192]{1,0:T(8,128)} copy(f32[16384,192]{0,1:T(8,128)} %bitcast.272) | data formatting | bytes 25165824 | tf_op jit(solution)/shard_map/reshape | solution.py:97
  396.4 88.5 %scatter_custom_fusion = f32[192,1344]{0,1:T(8,128)S(1)} fusion(s32[16384]{0:T(1024)} %bitcast.291, f32[16384,192]{1,0:T(8,128)} %copy.36, f32[]{:T(128)} %constant.63.clone.1), kind=kCustom, calls=%fused_computation.136 | custom fusion | flops 3145728 | bytes 1032704 | tf_op jit(solution)/shard_map/scatter-add | solution.py:98
  485.1 3.4 collective-permute-start.6
  488.6 2.0 collective-permute-start.7
  490.7 1.8 collective-permute-done.7
  492.5 1.7 scatter_fusion
  494.3 0.9 slice.363
  495.3 1.3 copy.39
  496.6 47.9 %all-reduce.2.cloned.1.call-done = f32[704,192]{1,0:T(8,128)} async-done(((f32[704,192]{1,0:T(8,128)}), f32[704,192]{1,0:T(8,128)}) %all-reduce.2.cloned.1.call-update) | async-done | bytes 540688 | tf_op jit(solution)/shard_map/psum | solution.py:152
  544.5 1.2 subtract_convert_fusion
  545.7 1.1 reshape.410
  546.8 9.2 %convolution_bitcast_fusion.1 = f32[4224,64]{0,1:T(8,128)S(1)} fusion(bf16[2112,64]{1,0:T(8,128)(2,1)} %reshape.410, bf16[4224,2112]{0,1:T(8,128)(2,1)} %param.34), kind=kOutput, calls=%fused_computation.131 | convolution fusion | flops 1141899264 | bytes 19193856 | tf_op jit(solution)/shard_map/dot_general | solution.py:159
  556.0 1.9 copy.40
  557.9 3.0 reshape.411
  562.2 3.9 convolution_bitcast_fusion.2
  566.7 0.9 copy.41
  567.6 27.4 %reduce-scatter.2.cloned.1.call-done = f32[176,192]{1,0:T(8,128)} async-done(((f32[1408,192]{1,0:T(8,128)}), f32[176,192]{1,0:T(8,128)}) %reduce-scatter.2.cloned.1.call-update) | async-done | bytes 135184 | tf_op jit(solution)/shard_map/reduce_scatter | solution.py:158
  (212 shorter events, 19.7 us)
Async XLA Ops:
  7.2 537.3 %all-reduce.2.cloned.1.call-start = ((), (), s32[]{:S(2)}) async-start(), calls=%async_computation.1 | async-start | bytes 1441792 | tf_op jit(solution)/shard_map/psum | solution.py:152
  12.1 11.5 %collective-permute-start = (bf16[32,192]{1,0:T(8,128)(2,1)S(1)}, bf16[32,192]{1,0:T(8,128)(2,1)S(1)}, u32[]{:S(2)}, u32[]{:S(2)}) collective-permute-start(bf16[32,192]{1,0:T(8,128)(2,1)S(1)} %get-tuple-element.221), channel_id=1, source_target_pairs={{0,6},{1,7},{2,0},{3,1},{4,2},{5,3},{6,4},{7,5},{8,14},{9,15},{10,... | collective-permute-start | bytes 36872 | tf_op jit(solution)/shard_map/ppermute | solution.py:18
  17.2 6.4 %collective-permute-start.1 = (bf16[32,192]{1,0:T(8,128)(2,1)S(1)}, bf16[32,192]{1,0:T(8,128)(2,1)S(1)}, u32[]{:S(2)}, u32[]{:S(2)}) collective-permute-start(bf16[32,192]{1,0:T(8,128)(2,1)S(1)} %get-tuple-element.224), channel_id=1, source_target_pairs={{0,7},{1,0},{2,1},{3,2},{4,3},{5,4},{6,5},{7,6},{8,15},{9,8},{10,9... | collective-permute-start | bytes 36872 | tf_op jit(solution)/shard_map/ppermute | solution.py:18
  17.2 6.4 %collective-permute-start.2 = (bf16[32,192]{1,0:T(8,128)(2,1)S(1)}, bf16[32,192]{1,0:T(8,128)(2,1)S(1)}, u32[]{:S(2)}, u32[]{:S(2)}) collective-permute-start(bf16[32,192]{1,0:T(8,128)(2,1)S(1)} %get-tuple-element.223), channel_id=1, source_target_pairs={{0,1},{1,2},{2,3},{3,4},{4,5},{5,6},{6,7},{7,0},{8,9},{9,10},{10,1... | collective-permute-start | bytes 36872 | tf_op jit(solution)/shard_map/ppermute | solution.py:18
  17.7 5.9 collective-permute-start.3
  98.8 7.8 %copy-start.19 = (bf16[48,8,3,1]{0,1,2,3:T(8,128)(2,1)S(1)}, bf16[48,8,3,1]{0,1,2,3:T(8,128)(2,1)}, u32[]{:S(2)}) copy-start(bf16[48,8,3,1]{0,1,2,3:T(8,128)(2,1)} %constant.85) | copy-start | bytes 6916
  106.5 10.1 %copy-start.22 = (f32[64,32,1]{0,1,2:T(8,128)S(1)}, f32[64,32,1]{0,1,2:T(8,128)}, u32[]{:S(2)}) copy-start(f32[64,32,1]{0,1,2:T(8,128)} %constant.86) | copy-start | bytes 24580
  155.2 6.1 %copy-start = (f32[48,2048]{1,0:T(8,128)S(1)}, f32[48,2048]{1,0:T(8,128)}, u32[]{:S(2)}) copy-start(f32[48,2048]{1,0:T(8,128)} %param.32) | copy-start | bytes 1179652
  155.2 6.1 %copy-start.1 = (f32[2048]{0:T(1024)S(1)}, f32[2048]{0:T(1024)}, u32[]{:S(2)}) copy-start(f32[2048]{0:T(1024)} %param.30) | copy-start | bytes 24580
  182.4 6.0 %copy-start.9 = (f32[1,1,1,8,2048]{4,1,0,3,2:T(1,128)S(1)}, f32[1,1,1,8,2048]{4,1,0,3,2:T(1,128)}, u32[]{:S(2)}) copy-start(f32[1,1,1,8,2048]{4,1,0,3,2:T(1,128)} %get-tuple-element.342) | copy-start | bytes 196612 | tf_op jit(solution)/shard_map/while
  182.4 6.0 %copy-start.10 = (f32[1,1,1,8,2048]{4,1,0,3,2:T(1,128)S(1)}, f32[1,1,1,8,2048]{4,1,0,3,2:T(1,128)}, u32[]{:S(2)}) copy-start(f32[1,1,1,8,2048]{4,1,0,3,2:T(1,128)} %get-tuple-element.343) | copy-start | bytes 196612 | tf_op jit(solution)/shard_map/while
  182.4 6.0 %copy-start.11 = (f32[1,1,1,8,2048]{4,1,0,3,2:T(1,128)S(1)}, f32[1,1,1,8,2048]{4,1,0,3,2:T(1,128)}, u32[]{:S(2)}) copy-start(f32[1,1,1,8,2048]{4,1,0,3,2:T(1,128)} %get-tuple-element.344) | copy-start | bytes 196612 | tf_op jit(solution)/shard_map/while
  182.4 6.0 %copy-start.12 = (f32[1,1,1,8,2048]{4,1,0,3,2:T(1,128)S(1)}, f32[1,1,1,8,2048]{4,1,0,3,2:T(1,128)}, u32[]{:S(2)}) copy-start(f32[1,1,1,8,2048]{4,1,0,3,2:T(1,128)} %get-tuple-element.345) | copy-start | bytes 196612 | tf_op jit(solution)/shard_map/while
  182.4 6.0 %copy-start.13 = (f32[1,1,1,8,2048]{4,1,0,3,2:T(1,128)S(1)}, f32[1,1,1,8,2048]{4,1,0,3,2:T(1,128)}, u32[]{:S(2)}) copy-start(f32[1,1,1,8,2048]{4,1,0,3,2:T(1,128)} %get-tuple-element.346) | copy-start | bytes 196612 | tf_op jit(solution)/shard_map/while
  182.4 6.0 %copy-start.14 = (f32[1,1,1,8,2048]{4,1,0,3,2:T(1,128)S(1)}, f32[1,1,1,8,2048]{4,1,0,3,2:T(1,128)}, u32[]{:S(2)}) copy-start(f32[1,1,1,8,2048]{4,1,0,3,2:T(1,128)} %get-tuple-element.347) | copy-start | bytes 196612 | tf_op jit(solution)/shard_map/while
  182.4 6.2 %copy-start.2 = (f32[2048]{0:T(1024)S(1)}, f32[2048]{0:T(1024)}, u32[]{:S(2)}) copy-start(f32[2048]{0:T(1024)} %get-tuple-element.405) | copy-start | bytes 24580 | tf_op jit(solution)/shard_map/while
  182.5 6.2 %copy-start.15 = (f32[6]{0:T(128)S(1)}, f32[6]{0:T(128)}, u32[]{:S(2)}) copy-start(f32[6]{0:T(128)} %get-tuple-element.418) | copy-start | bytes 76 | tf_op jit(solution)/shard_map/while
  182.5 6.2 %copy-start.16 = (f32[6]{0:T(128)S(1)}, f32[6]{0:T(128)}, u32[]{:S(2)}) copy-start(f32[6]{0:T(128)} %get-tuple-element.419) | copy-start | bytes 76 | tf_op jit(solution)/shard_map/while
  182.5 6.8 %copy-start.3 = (f32[1,1,1,8,2048]{4,1,0,3,2:T(1,128)S(1)}, f32[1,1,1,8,2048]{4,1,0,3,2:T(1,128)}, u32[]{:S(2)}) copy-start(f32[1,1,1,8,2048]{4,1,0,3,2:T(1,128)} %get-tuple-element.356) | copy-start | bytes 196612 | tf_op jit(solution)/shard_map/while
  182.5 6.8 %copy-start.4 = (f32[1,1,1,8,2048]{4,1,0,3,2:T(1,128)S(1)}, f32[1,1,1,8,2048]{4,1,0,3,2:T(1,128)}, u32[]{:S(2)}) copy-start(f32[1,1,1,8,2048]{4,1,0,3,2:T(1,128)} %get-tuple-element.355) | copy-start | bytes 196612 | tf_op jit(solution)/shard_map/while
  182.5 6.8 %copy-start.5 = (f32[1,1,1,8,2048]{4,1,0,3,2:T(1,128)S(1)}, f32[1,1,1,8,2048]{4,1,0,3,2:T(1,128)}, u32[]{:S(2)}) copy-start(f32[1,1,1,8,2048]{4,1,0,3,2:T(1,128)} %get-tuple-element.357) | copy-start | bytes 196612 | tf_op jit(solution)/shard_map/while
  182.5 6.8 %copy-start.6 = (f32[1,1,1,8,2048]{4,1,0,3,2:T(1,128)S(1)}, f32[1,1,1,8,2048]{4,1,0,3,2:T(1,128)}, u32[]{:S(2)}) copy-start(f32[1,1,1,8,2048]{4,1,0,3,2:T(1,128)} %get-tuple-element.358) | copy-start | bytes 196612 | tf_op jit(solution)/shard_map/while
  182.5 6.8 %copy-start.7 = (f32[1,1,1,8,2048]{4,1,0,3,2:T(1,128)S(1)}, f32[1,1,1,8,2048]{4,1,0,3,2:T(1,128)}, u32[]{:S(2)}) copy-start(f32[1,1,1,8,2048]{4,1,0,3,2:T(1,128)} %get-tuple-element.359) | copy-start | bytes 196612 | tf_op jit(solution)/shard_map/while
  182.5 6.8 %copy-start.8 = (f32[1,1,1,8,2048]{4,1,0,3,2:T(1,128)S(1)}, f32[1,1,1,8,2048]{4,1,0,3,2:T(1,128)}, u32[]{:S(2)}) copy-start(f32[1,1,1,8,2048]{4,1,0,3,2:T(1,128)} %get-tuple-element.354) | copy-start | bytes 196612 | tf_op jit(solution)/shard_map/while
  212.9 6.0 %copy-start.9 = (f32[1,1,1,8,2048]{4,1,0,3,2:T(1,128)S(1)}, f32[1,1,1,8,2048]{4,1,0,3,2:T(1,128)}, u32[]{:S(2)}) copy-start(f32[1,1,1,8,2048]{4,1,0,3,2:T(1,128)} %get-tuple-element.342) | copy-start | bytes 196612 | tf_op jit(solution)/shard_map/while
  212.9 6.0 %copy-start.10 = (f32[1,1,1,8,2048]{4,1,0,3,2:T(1,128)S(1)}, f32[1,1,1,8,2048]{4,1,0,3,2:T(1,128)}, u32[]{:S(2)}) copy-start(f32[1,1,1,8,2048]{4,1,0,3,2:T(1,128)} %get-tuple-element.343) | copy-start | bytes 196612 | tf_op jit(solution)/shard_map/while
  213.0 6.0 %copy-start.11 = (f32[1,1,1,8,2048]{4,1,0,3,2:T(1,128)S(1)}, f32[1,1,1,8,2048]{4,1,0,3,2:T(1,128)}, u32[]{:S(2)}) copy-start(f32[1,1,1,8,2048]{4,1,0,3,2:T(1,128)} %get-tuple-element.344) | copy-start | bytes 196612 | tf_op jit(solution)/shard_map/while
  213.0 6.0 %copy-start.12 = (f32[1,1,1,8,2048]{4,1,0,3,2:T(1,128)S(1)}, f32[1,1,1,8,2048]{4,1,0,3,2:T(1,128)}, u32[]{:S(2)}) copy-start(f32[1,1,1,8,2048]{4,1,0,3,2:T(1,128)} %get-tuple-element.345) | copy-start | bytes 196612 | tf_op jit(solution)/shard_map/while
  213.0 6.0 %copy-start.13 = (f32[1,1,1,8,2048]{4,1,0,3,2:T(1,128)S(1)}, f32[1,1,1,8,2048]{4,1,0,3,2:T(1,128)}, u32[]{:S(2)}) copy-start(f32[1,1,1,8,2048]{4,1,0,3,2:T(1,128)} %get-tuple-element.346) | copy-start | bytes 196612 | tf_op jit(solution)/shard_map/while
  213.0 6.2 %copy-start.2 = (f32[2048]{0:T(1024)S(1)}, f32[2048]{0:T(1024)}, u32[]{:S(2)}) copy-start(f32[2048]{0:T(1024)} %get-tuple-element.405) | copy-start | bytes 24580 | tf_op jit(solution)/shard_map/while
  213.0 6.2 %copy-start.15 = (f32[6]{0:T(128)S(1)}, f32[6]{0:T(128)}, u32[]{:S(2)}) copy-start(f32[6]{0:T(128)} %get-tuple-element.418) | copy-start | bytes 76 | tf_op jit(solution)/shard_map/while
  213.0 6.2 %copy-start.16 = (f32[6]{0:T(128)S(1)}, f32[6]{0:T(128)}, u32[]{:S(2)}) copy-start(f32[6]{0:T(128)} %get-tuple-element.419) | copy-start | bytes 76 | tf_op jit(solution)/shard_map/while
  213.0 6.8 %copy-start.3 = (f32[1,1,1,8,2048]{4,1,0,3,2:T(1,128)S(1)}, f32[1,1,1,8,2048]{4,1,0,3,2:T(1,128)}, u32[]{:S(2)}) copy-start(f32[1,1,1,8,2048]{4,1,0,3,2:T(1,128)} %get-tuple-element.356) | copy-start | bytes 196612 | tf_op jit(solution)/shard_map/while
  213.0 6.8 %copy-start.4 = (f32[1,1,1,8,2048]{4,1,0,3,2:T(1,128)S(1)}, f32[1,1,1,8,2048]{4,1,0,3,2:T(1,128)}, u32[]{:S(2)}) copy-start(f32[1,1,1,8,2048]{4,1,0,3,2:T(1,128)} %get-tuple-element.355) | copy-start | bytes 196612 | tf_op jit(solution)/shard_map/while
  213.1 6.8 %copy-start.5 = (f32[1,1,1,8,2048]{4,1,0,3,2:T(1,128)S(1)}, f32[1,1,1,8,2048]{4,1,0,3,2:T(1,128)}, u32[]{:S(2)}) copy-start(f32[1,1,1,8,2048]{4,1,0,3,2:T(1,128)} %get-tuple-element.357) | copy-start | bytes 196612 | tf_op jit(solution)/shard_map/while
  213.1 6.8 %copy-start.6 = (f32[1,1,1,8,2048]{4,1,0,3,2:T(1,128)S(1)}, f32[1,1,1,8,2048]{4,1,0,3,2:T(1,128)}, u32[]{:S(2)}) copy-start(f32[1,1,1,8,2048]{4,1,0,3,2:T(1,128)} %get-tuple-element.358) | copy-start | bytes 196612 | tf_op jit(solution)/shard_map/while
  213.1 6.8 %copy-start.7 = (f32[1,1,1,8,2048]{4,1,0,3,2:T(1,128)S(1)}, f32[1,1,1,8,2048]{4,1,0,3,2:T(1,128)}, u32[]{:S(2)}) copy-start(f32[1,1,1,8,2048]{4,1,0,3,2:T(1,128)} %get-tuple-element.359) | copy-start | bytes 196612 | tf_op jit(solution)/shard_map/while
  213.1 6.8 %copy-start.8 = (f32[1,1,1,8,2048]{4,1,0,3,2:T(1,128)S(1)}, f32[1,1,1,8,2048]{4,1,0,3,2:T(1,128)}, u32[]{:S(2)}) copy-start(f32[1,1,1,8,2048]{4,1,0,3,2:T(1,128)} %get-tuple-element.354) | copy-start | bytes 196612 | tf_op jit(solution)/shard_map/while
  243.6 6.2 %copy-start.2 = (f32[2048]{0:T(1024)S(1)}, f32[2048]{0:T(1024)}, u32[]{:S(2)}) copy-start(f32[2048]{0:T(1024)} %get-tuple-element.405) | copy-start | bytes 24580 | tf_op jit(solution)/shard_map/while
  243.7 6.2 %copy-start.15 = (f32[6]{0:T(128)S(1)}, f32[6]{0:T(128)}, u32[]{:S(2)}) copy-start(f32[6]{0:T(128)} %get-tuple-element.418) | copy-start | bytes 76 | tf_op jit(solution)/shard_map/while
  243.7 6.2 %copy-start.16 = (f32[6]{0:T(128)S(1)}, f32[6]{0:T(128)}, u32[]{:S(2)}) copy-start(f32[6]{0:T(128)} %get-tuple-element.419) | copy-start | bytes 76 | tf_op jit(solution)/shard_map/while
  243.7 6.8 %copy-start.3 = (f32[1,1,1,8,2048]{4,1,0,3,2:T(1,128)S(1)}, f32[1,1,1,8,2048]{4,1,0,3,2:T(1,128)}, u32[]{:S(2)}) copy-start(f32[1,1,1,8,2048]{4,1,0,3,2:T(1,128)} %get-tuple-element.356) | copy-start | bytes 196612 | tf_op jit(solution)/shard_map/while
  243.7 6.8 %copy-start.4 = (f32[1,1,1,8,2048]{4,1,0,3,2:T(1,128)S(1)}, f32[1,1,1,8,2048]{4,1,0,3,2:T(1,128)}, u32[]{:S(2)}) copy-start(f32[1,1,1,8,2048]{4,1,0,3,2:T(1,128)} %get-tuple-element.355) | copy-start | bytes 196612 | tf_op jit(solution)/shard_map/while
  243.7 6.8 %copy-start.5 = (f32[1,1,1,8,2048]{4,1,0,3,2:T(1,128)S(1)}, f32[1,1,1,8,2048]{4,1,0,3,2:T(1,128)}, u32[]{:S(2)}) copy-start(f32[1,1,1,8,2048]{4,1,0,3,2:T(1,128)} %get-tuple-element.357) | copy-start | bytes 196612 | tf_op jit(solution)/shard_map/while
  243.7 6.8 %copy-start.6 = (f32[1,1,1,8,2048]{4,1,0,3,2:T(1,128)S(1)}, f32[1,1,1,8,2048]{4,1,0,3,2:T(1,128)}, u32[]{:S(2)}) copy-start(f32[1,1,1,8,2048]{4,1,0,3,2:T(1,128)} %get-tuple-element.358) | copy-start | bytes 196612 | tf_op jit(solution)/shard_map/while
  243.7 6.8 %copy-start.7 = (f32[1,1,1,8,2048]{4,1,0,3,2:T(1,128)S(1)}, f32[1,1,1,8,2048]{4,1,0,3,2:T(1,128)}, u32[]{:S(2)}) copy-start(f32[1,1,1,8,2048]{4,1,0,3,2:T(1,128)} %get-tuple-element.359) | copy-start | bytes 196612 | tf_op jit(solution)/shard_map/while
  243.7 6.8 %copy-start.8 = (f32[1,1,1,8,2048]{4,1,0,3,2:T(1,128)S(1)}, f32[1,1,1,8,2048]{4,1,0,3,2:T(1,128)}, u32[]{:S(2)}) copy-start(f32[1,1,1,8,2048]{4,1,0,3,2:T(1,128)} %get-tuple-element.354) | copy-start | bytes 196612 | tf_op jit(solution)/shard_map/while
  273.5 6.2 %copy-start.2 = (f32[2048]{0:T(1024)S(1)}, f32[2048]{0:T(1024)}, u32[]{:S(2)}) copy-start(f32[2048]{0:T(1024)} %get-tuple-element.405) | copy-start | bytes 24580 | tf_op jit(solution)/shard_map/while
  273.5 6.2 %copy-start.15 = (f32[6]{0:T(128)S(1)}, f32[6]{0:T(128)}, u32[]{:S(2)}) copy-start(f32[6]{0:T(128)} %get-tuple-element.418) | copy-start | bytes 76 | tf_op jit(solution)/shard_map/while
  273.6 6.2 %copy-start.16 = (f32[6]{0:T(128)S(1)}, f32[6]{0:T(128)}, u32[]{:S(2)}) copy-start(f32[6]{0:T(128)} %get-tuple-element.419) | copy-start | bytes 76 | tf_op jit(solution)/shard_map/while
  273.6 6.8 %copy-start.3 = (f32[1,1,1,8,2048]{4,1,0,3,2:T(1,128)S(1)}, f32[1,1,1,8,2048]{4,1,0,3,2:T(1,128)}, u32[]{:S(2)}) copy-start(f32[1,1,1,8,2048]{4,1,0,3,2:T(1,128)} %get-tuple-element.356) | copy-start | bytes 196612 | tf_op jit(solution)/shard_map/while
  273.6 6.8 %copy-start.4 = (f32[1,1,1,8,2048]{4,1,0,3,2:T(1,128)S(1)}, f32[1,1,1,8,2048]{4,1,0,3,2:T(1,128)}, u32[]{:S(2)}) copy-start(f32[1,1,1,8,2048]{4,1,0,3,2:T(1,128)} %get-tuple-element.355) | copy-start | bytes 196612 | tf_op jit(solution)/shard_map/while
  273.6 6.8 %copy-start.5 = (f32[1,1,1,8,2048]{4,1,0,3,2:T(1,128)S(1)}, f32[1,1,1,8,2048]{4,1,0,3,2:T(1,128)}, u32[]{:S(2)}) copy-start(f32[1,1,1,8,2048]{4,1,0,3,2:T(1,128)} %get-tuple-element.357) | copy-start | bytes 196612 | tf_op jit(solution)/shard_map/while
  273.6 6.8 %copy-start.6 = (f32[1,1,1,8,2048]{4,1,0,3,2:T(1,128)S(1)}, f32[1,1,1,8,2048]{4,1,0,3,2:T(1,128)}, u32[]{:S(2)}) copy-start(f32[1,1,1,8,2048]{4,1,0,3,2:T(1,128)} %get-tuple-element.358) | copy-start | bytes 196612 | tf_op jit(solution)/shard_map/while
  273.6 6.8 %copy-start.7 = (f32[1,1,1,8,2048]{4,1,0,3,2:T(1,128)S(1)}, f32[1,1,1,8,2048]{4,1,0,3,2:T(1,128)}, u32[]{:S(2)}) copy-start(f32[1,1,1,8,2048]{4,1,0,3,2:T(1,128)} %get-tuple-element.359) | copy-start | bytes 196612 | tf_op jit(solution)/shard_map/while
  273.6 6.8 %copy-start.8 = (f32[1,1,1,8,2048]{4,1,0,3,2:T(1,128)S(1)}, f32[1,1,1,8,2048]{4,1,0,3,2:T(1,128)}, u32[]{:S(2)}) copy-start(f32[1,1,1,8,2048]{4,1,0,3,2:T(1,128)} %get-tuple-element.354) | copy-start | bytes 196612 | tf_op jit(solution)/shard_map/while
  283.2 34.2 %copy-start.20 = (bf16[48,8,3,1]{0,1,2,3:T(8,128)(2,1)S(1)}, bf16[48,8,3,1]{0,1,2,3:T(8,128)(2,1)}, u32[]{:S(2)}) copy-start(bf16[48,8,3,1]{0,1,2,3:T(8,128)(2,1)} %constant.85) | copy-start | bytes 6916
  283.2 34.2 %copy-start.21 = (f32[2048]{0:T(1024)S(1)}, f32[2048]{0:T(1024)}, u32[]{:S(2)}) copy-start(f32[2048]{0:T(1024)} %get-tuple-element.226) | copy-start | bytes 24580
  381.7 110.8 %copy-start.24 = (s32[128]{0:T(128)S(1)}, s32[128]{0:T(128)}, u32[]{:S(2)}) copy-start(s32[128]{0:T(128)} %copy-done.23) | copy-start | bytes 1540
  484.9 5.8 collective-permute-start.4
  485.0 5.7 collective-permute-start.5
  485.1 5.5 collective-permute-start.6
  488.6 3.9 collective-permute-start.7
  495.2 99.8 %reduce-scatter.2.cloned.1.call-start = ((), (), s32[]{:S(2)}) async-start(), calls=%async_computation.2 | async-start | bytes 1622016 | tf_op jit(solution)/shard_map/reduce_scatter | solution.py:158
  (16 other events, 86.3 us)
Sparse Core Ops, SparseCore 0:
  495.3 49.1 all-reduce.1
  561.0 33.9 reduce-scatter.1
where the time goes:
time: 611 us; the launch traced here: 602 us
  local copies, waits for them, and re-layouts  235 us (38%)
  other arithmetic  135 us (22%)
  matrix products  127 us (21%)
  waiting for transfers between devices  77.2 us (13%)
  between operations  15.4 us (3%)
  starting transfers between devices  12 us (2%)
    scatter-add x1, other arithmetic, element_update(): jnp.zeros((width, buffer_rows), jnp.float32).at[:, corner_index].add(forces)  88.5 us
    gather x2, local copies, waits for them, and re-layouts, element_update(): jnp.take(columns, corner_index, axis=1).reshape(3, fourier, 8, elems)  75 us
    slice x4, local copies, waits for them, and re-layouts, element_update(): final, history = lax.scan(advance, stress_start, delta, unroll=8)  48.8 us
    psum x1, waiting for transfers between devices, per_device(): group_force = lax.psum(owned[int_nodes:], 'grp')  47.9 us
    dot_general x1, matrix products, element_update(): jnp.einsum('fm,qfe->mqe', synthesis, strain_hat, precision=HIGHEST)  38.1 us
    unnamed x28, local copies, waits for them, and re-layouts  35.3 us
    dot_general x1, matrix products, element_update(): stress_hat = jnp.einsum('mf,mqe->fqe', analysis, history, precision=HIGHEST)  34.2 us
    dot_general x1, matrix products, element_update(): jnp.einsum('qai,fqe->ifae', table.astype(jnp.float32), stress_hat, precis...  31.7 us
  transfers between devices with their start and end apart: 10, of which 4 were waited for; matrix products, arithmetic and copies ran while one was open for 2% of the time, Pallas kernels for 0%

commit v1 on v0

v1 whole, which is shorter than its diff:
```python
import functools
import math

import jax
import jax.numpy as jnp
import numpy as np
from jax import lax
from jax.experimental import pallas as pl
from jax.experimental.pallas import tpu as pltpu
from jax.sharding import PartitionSpec as P

TIMES = 32
POISSON = 0.3
LAME = POISSON / ((1.0 + POISSON) * (1.0 - 2.0 * POISSON))
SHEAR = 1.0 / (2.0 * (1.0 + POISSON))
HIGHEST = lax.Precision.HIGHEST
STEPS = 8
GROUPS = TIMES // STEPS
ROWS = 3 * TIMES
NT = (((1,), (1,)), ((), ()))
BF16 = jnp.bfloat16
F32 = jnp.float32


def strain_table():
    gauss = 1.0 / math.sqrt(3.0)
    table = np.zeros((6, 8, 8, 3))
    for point in range(8):
        coords = [((point >> bit & 1) * 2 - 1) * gauss for bit in range(3)]
        for corner in range(8):
            signs = [(corner >> bit & 1) * 2 - 1 for bit in range(3)]
            deriv = []
            for axis in range(3):
                value = signs[axis] / 8.0
                for other in range(3):
                    if other != axis:
                        value = value * (1.0 + signs[other] * coords[other])
                deriv.append(value)
            table[0, point, corner, 0] = deriv[0]
            table[1, point, corner, 1] = deriv[1]
            table[2, point, corner, 2] = deriv[2]
            table[3, point, corner, 0] = deriv[1]
            table[3, point, corner, 1] = deriv[0]
            table[4, point, corner, 1] = deriv[2]
            table[4, point, corner, 2] = deriv[1]
            table[5, point, corner, 2] = deriv[0]
            table[5, point, corner, 0] = deriv[2]
    return table.reshape(48, 24).astype(np.float32)


def time_tables(fourier):
    theta = 2.0 * math.pi * (np.arange(TIMES) + 0.3) / TIMES
    synthesis = np.zeros((fourier, TIMES))
    for column in range(fourier):
        harmonic = column // 2
        if column % 2 == 0:
            synthesis[column] = np.cos(harmonic * theta)
        else:
            synthesis[column] = np.sin((harmonic + 1) * theta)
    analysis = synthesis.T * (2.0 / TIMES)
    analysis[:, 0] = 1.0 / TIMES
    return synthesis.astype(np.float32), analysis.astype(np.float32)


def constants(fourier):
    synthesis, analysis = time_tables(fourier)
    differences = synthesis.astype(np.float64) - np.roll(synthesis.astype(np.float64), 1, axis=1)
    synth = np.zeros((GROUPS, 3, STEPS, 3, fourier))
    anal = np.zeros((GROUPS, 3, STEPS, 3, fourier))
    for comp in range(3):
        synth[:, comp, :, comp, :] = differences.T.reshape(GROUPS, STEPS, fourier)
        anal[:, comp, :, comp, :] = analysis.reshape(GROUPS, STEPS, fourier)
    synth = synth.reshape(ROWS, 3 * fourier).astype(np.float32)
    table = strain_table().reshape(48, 8, 3)
    strain = np.zeros((STEPS, 48, 8, 2, 3, STEPS), np.float32)
    force = np.zeros((8, 3, STEPS, STEPS, 48), np.float32)
    for step in range(STEPS):
        for half in range(2):
            strain[step, :, :, half, :, step] = table
        force[:, :, step, step, :] = table.transpose(1, 2, 0)
    high = jnp.asarray(synth).astype(BF16)
    low = (jnp.asarray(synth) - high.astype(F32)).astype(BF16)
    return (
        high,
        low,
        jnp.asarray(strain.reshape(STEPS * 48, 16 * 3 * STEPS)).astype(BF16),
        jnp.asarray(force.reshape(24 * STEPS, STEPS * 48)).astype(BF16),
        jnp.asarray(anal.reshape(ROWS, 3 * fourier), F32),
    )


def up(n, to):
    return -(-n // to) * to


def element_kernel(
    count_ref, int_ref, if_ref, *refs, neighbours, chunk, own, padded
):
    halo_refs = refs[:neighbours]
    conn_ref, par_ref, init_ref, high_ref, low_ref, strain_ref, force_ref = refs[neighbours : neighbours + 7]
    end_ref, pint_ref, pif_ref, back_ref, nodes, onehot, corners, forces, history, total = refs[neighbours + 7 :]
    index = pl.program_id(0)
    n_int, n_if, slots = int_ref.shape[0], if_ref.shape[0], halo_refs[0].shape[0]
    halo_at = up(own, 128)

    @pl.when(index == 0)
    def _():
        nodes[...] = jnp.zeros_like(nodes)
        halo = jnp.concatenate([ref[...].astype(F32) for ref in halo_refs], axis=0).astype(BF16)
        pieces = ((0, n_int, int_ref[...]), (n_int, n_if, if_ref[...]), (halo_at, neighbours * slots, halo))
        for start, length, rows in pieces:
            value = lax.dot_general(high_ref[...], rows, NT, preferred_element_type=F32)
            value = value + lax.dot_general(low_ref[...], rows, NT, preferred_element_type=F32)
            upper = value.astype(BF16).astype(F32)
            lower = value - upper
            for group in range(GROUPS):
                part = slice(group * 3 * STEPS, (group + 1) * 3 * STEPS)
                nodes[group * 6 * STEPS : (group + 1) * 6 * STEPS, start : start + length] = jnp.concatenate(
                    [upper[part], lower[part]], axis=0
                ).astype(BF16)
        total[...] = jnp.zeros_like(total)

    live = index * chunk < count_ref[0]

    @pl.when(jnp.logical_not(live))
    def _():
        end_ref[...] = jnp.zeros_like(end_ref)

    @pl.when(live)
    def _():
        @pl.loop(0, 8)
        def _(corner):
            node = conn_ref[pl.ds(corner, 1), :]
            node = node + jnp.where(node >= own, halo_at - own, 0)
            hot = jnp.where(lax.broadcasted_iota(jnp.int32, (padded, chunk), 0) == node, 1.0, 0.0).astype(BF16)
            onehot[corner] = hot
            found = jnp.dot(nodes[...], hot, preferred_element_type=F32).astype(BF16)
            rows = pl.ds(pl.multiple_of(corner * 6 * STEPS, 16), 6 * STEPS)
            for group in range(GROUPS):
                corners[group, rows, :] = found[group * 6 * STEPS : (group + 1) * 6 * STEPS]

        size, limit, rate = par_ref[0:1, :], par_ref[2:3, :], par_ref[3:4, :]
        modulus = par_ref[1:2, :] * (2.0 / size)

        def wide(row):
            return jnp.broadcast_to(row, (8, chunk))

        twice_shear, shear, lame = wide(modulus * (2.0 * SHEAR)), wide(modulus * SHEAR), wide(modulus * LAME)
        inverse, relax = wide(1.0 / limit), wide(rate * limit)
        slot = index * chunk + lax.broadcasted_iota(jnp.int32, (1, chunk), 1)
        alive = jnp.where(slot < count_ref[0], 1.0, 0.0)
        scale = jnp.broadcast_to(size * size * 0.25 * alive, (3 * STEPS, chunk))

        def advance(group, stress):
            delta = jnp.dot(strain_ref[...], corners[group], preferred_element_type=F32)
            for step in range(STEPS):
                d = [delta[step * 48 + comp * 8 : step * 48 + comp * 8 + 8] for comp in range(6)]
                trace = lame * (d[0] + d[1] + d[2])
                stress = tuple(
                    s
                    + (twice_shear * d[comp] + trace if comp < 3 else shear * d[comp])
                    - relax * jnp.tanh(s * inverse)
                    for comp, s in enumerate(stress)
                )
                history[step * 48 : (step + 1) * 48, :] = jnp.concatenate(stress, axis=0).astype(BF16)
            force = jnp.dot(force_ref[...], history[...], preferred_element_type=F32)
            rows = pl.ds(pl.multiple_of(group * 3 * STEPS, 8), 3 * STEPS)
            for corner in range(8):
                part = force[corner * 3 * STEPS : (corner + 1) * 3 * STEPS]
                forces[rows, corner * chunk : (corner + 1) * chunk] = part * scale
            return stress

        stress = tuple(init_ref[comp * 8 : comp * 8 + 8, :] for comp in range(6))
        stress = lax.fori_loop(0, GROUPS, advance, stress)
        for comp in range(6):
            end_ref[comp * 8 : comp * 8 + 8, :] = stress[comp] * alive
        half = padded // 2

        @pl.loop(0, 2)
        def _(block):
            rows = pl.ds(pl.multiple_of(block * half, 16), half)
            sums = None
            for corner in range(8):
                part = forces[:, corner * chunk : (corner + 1) * chunk].astype(BF16)
                term = lax.dot_general(onehot[corner, rows, :], part, NT, preferred_element_type=F32)
                sums = term if sums is None else sums + term
            total[rows, :] += sums

    @pl.when(index == pl.num_programs(0) - 1)
    def _():
        pint_ref[...] = total[:n_int]
        pif_ref[...] = total[n_int:own]
        for slot_index in range(neighbours):
            start = halo_at + slot_index * slots
            back_ref[slot_index] = total[start : start + slots]


def whole(shape):
    return pl.BlockSpec(shape, lambda *_: (0,) * len(shape))


def element_phase(u_int, u_if, halos, conn, count, params, stress_init, tables):
    elems = conn.shape[1]
    chunk = 256
    own = u_int.shape[0] + u_if.shape[0]
    neighbours, slots = len(halos), halos[0].shape[0]
    padded = up(own, 128) + up(neighbours * slots, 128)
    n_rows = stress_init.shape[0]

    def columns(rows):
        return pl.BlockSpec((rows, chunk), lambda c, *_: (0, c))

    synth_high, synth_low, strain, force = tables[:4]
    return pl.pallas_call(
        functools.partial(element_kernel, neighbours=neighbours, chunk=chunk, own=own, padded=padded),
        grid_spec=pltpu.PrefetchScalarGridSpec(
            num_scalar_prefetch=1,
            grid=(elems // chunk,),
            in_specs=[whole(u_int.shape), whole(u_if.shape)]
            + [whole(h.shape) for h in halos]
            + [columns(8), columns(4), columns(n_rows)]
            + [whole(t.shape) for t in tables[:4]],
            out_specs=[
                columns(n_rows),
                whole((u_int.shape[0], ROWS)),
                whole((u_if.shape[0], ROWS)),
                whole((neighbours, slots, ROWS)),
            ],
            scratch_shapes=[
                pltpu.VMEM((2 * ROWS, padded), BF16),
                pltpu.VMEM((8, padded, chunk), BF16),
                pltpu.VMEM((GROUPS, 48 * STEPS, chunk), BF16),
                pltpu.VMEM((ROWS, 8 * chunk), F32),
                pltpu.VMEM((48 * STEPS, chunk), BF16),
                pltpu.VMEM((padded, ROWS), F32),
            ],
        ),
        out_shape=[
            jax.ShapeDtypeStruct(stress_init.shape, F32),
            jax.ShapeDtypeStruct((u_int.shape[0], ROWS), F32),
            jax.ShapeDtypeStruct((u_if.shape[0], ROWS), F32),
            jax.ShapeDtypeStruct((neighbours, slots, ROWS), F32),
        ],
        compiler_params=pltpu.CompilerParams(vmem_limit_bytes=32 << 20),
        name="elements",
    )(count, u_int, u_if, *halos, conn, params, stress_init, *tables[:4])


def added_back(own, map_ref, returned, first):
    for slot_index, ref in enumerate(returned):
        hot = (
            lax.broadcasted_iota(jnp.int32, (own.shape[0], ref.shape[0]), 0) + first
            == map_ref[slot_index : slot_index + 1, :]
        )
        hot = jnp.where(hot, 1.0, 0.0).astype(BF16)
        value = ref[...]
        high = value.astype(BF16)
        low = (value - high.astype(F32)).astype(BF16)
        own = own + jnp.dot(hot, high, preferred_element_type=F32) + jnp.dot(hot, low, preferred_element_type=F32)
    return own


def interface_kernel(own_ref, map_ref, *refs, first):
    returned, (a_ref, b_ref) = refs[:-2], refs[-2:]
    value = added_back(own_ref[...], map_ref, returned, first)
    half = a_ref.shape[0]
    a_ref[...] = value[:half]
    b_ref[...] = value[half:]


def interleaved(value, scratch):
    nodes, width = value.shape
    fourier = width // 3
    for comp in range(3):
        scratch[pl.ds(comp, nodes, stride=3), :] = value[:, comp * fourier : (comp + 1) * fourier]
    return scratch[...]


def separated(value, scratch):
    scratch[...] = value
    nodes = value.shape[0] // 3
    return jnp.concatenate([scratch[pl.ds(comp, nodes, stride=3), :] for comp in range(3)], axis=1)


def interior_kernel(own_ref, map_ref, *refs):
    returned = refs[:-6]
    load_ref, anal_ref, kinv_ref, du_ref, scratch, _ = refs[-6:]
    value = added_back(own_ref[...], map_ref, returned, 0)
    force = jnp.dot(value, anal_ref[...], precision=HIGHEST, preferred_element_type=F32)
    rhs = interleaved(load_ref[...] - force, scratch).astype(BF16)
    du = jnp.dot(kinv_ref[...], rhs, preferred_element_type=F32)
    du_ref[...] = separated(du, scratch)


def rhs_kernel(load_ref, own_a, got_a, own_b, got_b, anal_ref, rhs_ref, scratch):
    half = own_a.shape[0]
    total = jnp.concatenate([own_a[...] + got_a[...], own_b[...] + got_b[...]], axis=0)
    force = jnp.dot(total, anal_ref[...], precision=HIGHEST, preferred_element_type=F32)
    rhs_ref[...] = interleaved(load_ref[...] - force, scratch).astype(BF16)


def solve_kernel(order_ref, sinv_ref, rhs_ref, out_ref):
    value = jnp.dot(sinv_ref[0], rhs_ref[...], preferred_element_type=F32)
    half = value.shape[0] // 2
    out_ref[0] = jnp.concatenate([value[:half], value[half:]], axis=1).astype(out_ref.dtype)


def solve_blocks(order, sinv, rhs, peers, dtype):
    rows = sinv.shape[0] // peers
    fourier = rhs.shape[1]
    count = order.shape[0]
    return pl.pallas_call(
        solve_kernel,
        grid_spec=pltpu.PrefetchScalarGridSpec(
            num_scalar_prefetch=1,
            grid=(count,),
            in_specs=[
                pl.BlockSpec((1, rows, sinv.shape[1]), lambda j, order: (order[j], 0, 0)),
                whole(rhs.shape),
            ],
            out_specs=pl.BlockSpec((1, rows // 2, 2 * fourier), lambda j, order: (j, 0, 0)),
        ),
        out_shape=jax.ShapeDtypeStruct((count, rows // 2, 2 * fourier), dtype),
        cost_estimate=pl.CostEstimate(
            flops=2 * count * rows * sinv.shape[1] * fourier,
            bytes_accessed=2 * count * rows * sinv.shape[1],
            transcendentals=0,
        ),
        name="interface_solve",
    )(order, sinv.reshape(peers, rows, sinv.shape[1]), rhs)


def last_kernel(mine_ref, got_ref, out_ref, scratch):
    value = mine_ref[0] + got_ref[0].astype(F32)
    half = value.shape[0]
    fourier = value.shape[1] // 2
    out_ref[...] = separated(jnp.concatenate([value[:, :fourier], value[:, fourier:]], axis=0), scratch)


def swapped(shard, axis, bit):
    peers = lax.axis_size(axis)
    return lax.ppermute(shard, axis, [(i, i ^ bit) for i in range(peers)])


def passed_along(shard, axis, by):
    peers = lax.axis_size(axis)
    return lax.ppermute(shard, axis, [(i, (i + by) % peers) for i in range(peers)])


def per_device(
    u_int,
    u_if,
    load_int,
    load_if,
    conn,
    send_map,
    counts,
    elem_size,
    stiffness,
    yield_stress,
    relax_rate,
    stress_init,
    kinv_int,
    sinv,
):
    width = u_int.shape[1]
    fourier = width // 3
    n_int, n_if = u_int.shape[0], u_if.shape[0]
    neighbours, slots = send_map.shape
    reach = neighbours // 2
    offsets = list(range(-reach, 0)) + list(range(1, reach + 1))
    tables = constants(fourier)
    analysis = tables[4]

    local = jnp.concatenate([u_int, u_if], axis=0)
    blocks = jnp.take(local, send_map.reshape(-1), axis=0).reshape(neighbours, slots, width)
    halos = [passed_along(blocks[j], "dom", offsets[j]) for j in range(neighbours)]
    params = jnp.stack([elem_size, stiffness, yield_stress, relax_rate], axis=0)
    stress_end, p_int, p_if, back = element_phase(
        u_int, u_if, halos, conn.T, counts, params, stress_init, tables
    )
    returned = [passed_along(back[j], "dom", -offsets[j]) for j in range(neighbours)]

    half = n_if // 2
    part_a, part_b = pl.pallas_call(
        functools.partial(interface_kernel, first=n_int),
        out_shape=[jax.ShapeDtypeStruct((half, ROWS), F32), jax.ShapeDtypeStruct((n_if - half, ROWS), F32)],
        name="interface_forces",
    )(p_if, send_map, *returned)

    bits = [1 << b for b in range(lax.axis_size("grp").bit_length() - 1)]
    got_a = got_b = None
    for bit_a, bit_b in zip(bits, bits[::-1]):
        if got_a is not None:
            part_a, part_b = part_a + got_a, part_b + got_b
        got_a, got_b = swapped(part_a, "grp", bit_a), swapped(part_b, "grp", bit_b)

    du_int = pl.pallas_call(
        interior_kernel,
        out_shape=jax.ShapeDtypeStruct((n_int, width), F32),
        scratch_shapes=[pltpu.VMEM((3 * n_int, fourier), F32), pltpu.VMEM((8, 128), F32)],
        cost_estimate=pl.CostEstimate(
            flops=2 * kinv_int.size * fourier, bytes_accessed=2 * kinv_int.size, transcendentals=0
        ),
        name="interior_solve",
    )(p_int, send_map, *returned, load_int, analysis, kinv_int)

    rhs = pl.pallas_call(
        rhs_kernel,
        out_shape=jax.ShapeDtypeStruct((3 * n_if, fourier), BF16),
        scratch_shapes=[pltpu.VMEM((3 * n_if, fourier), F32)],
        name="interface_rhs",
    )(load_if, part_a, got_a, part_b, got_b, analysis)

    peers = lax.axis_size("dom")
    me = lax.axis_index("dom").astype(jnp.int32)
    levels = peers.bit_length() - 1
    away = [j for j in range(peers) if j & 1]
    near = [j for j in range(peers) if not j & 1]
    sent = solve_blocks(me ^ jnp.asarray(away, jnp.int32), sinv, rhs, peers, F32)
    got = swapped(sent, "dom", 1)
    mine = solve_blocks(me ^ jnp.asarray(near, jnp.int32), sinv, rhs, peers, F32)
    for level in range(1, levels):
        both = (mine + got).reshape(peers >> (level + 1), 2, *mine.shape[1:])
        mine = both[:, 0]
        got = swapped(both[:, 1], "dom", 1 << level)
    rows = sinv.shape[0] // peers
    du_if = pl.pallas_call(
        last_kernel,
        out_shape=jax.ShapeDtypeStruct((rows // 3, width), F32),
        scratch_shapes=[pltpu.VMEM((rows, fourier), F32)],
        name="interface_result",
    )(mine, got)
    return (du_int, du_if, stress_end)


def solution(mesh):
    return jax.shard_map(
        per_device,
        mesh=mesh,
        in_specs=(
            P(("grp", "dom"), None),
            P("dom", None),
            P(("grp", "dom"), None),
            P("dom", None),
            P(("grp", "dom"), None),
            P(("grp", "dom"), None),
            P(("grp", "dom")),
            P(("grp", "dom")),
            P(("grp", "dom")),
            P(("grp", "dom")),
            P(("grp", "dom")),
            P(None, ("grp", "dom")),
            P(("grp", "dom"), None),
            P("grp", "dom"),
        ),
        out_specs=(P(("grp", "dom"), None), P(("grp", "dom"), None), P(None, ("grp", "dom"))),
        check_vma=False,
    )
```

time: 611 us -> 166 us (0.27); the launches traced: 602 us -> 163 us
  local copies, waits for them, and re-layouts: 235 us -> 42.7 us
  other arithmetic: 135 us -> 3.22 us
  matrix products: 127 us -> 0 us
  waiting for transfers between devices: 77.2 us -> 18.9 us
  Pallas kernels: 0 us -> 46 us
  starting transfers between devices: 12 us -> 51.1 us
  between operations: 15.4 us -> 1.49 us
    dot_general x6 -> x0, matrix products: 127 us -> none  [the longest x1 38.1 us: element_update(): jnp.einsum('fm,qfe->mqe', synthesis, strain_hat, precision=HIGHEST)]
    scatter-add x2 -> x0, other arithmetic: 90.2 us -> none  [the longest x1 88.5 us: element_update(): jnp.zeros((width, buffer_rows), jnp.float32).at[:, corner_index].add(forces)]
    slice x13 -> x1, local copies, waits for them, and re-layouts: 81.3 us -> 0.01 us  [per_device(): blocks[j]]
    gather x2 -> x0, local copies, waits for them, and re-layouts: 75 us -> none  [element_update(): jnp.take(columns, corner_index, axis=1).reshape(3, fourier, 8, elems)]
    psum x1 -> x0, waiting for transfers between devices: 47.9 us -> none  [per_device(): group_force = lax.psum(owned[int_nodes:], 'grp')]
    pallas_call x0 -> x7, Pallas kernels: none -> 46 us  [the longest x1 16.8 us: element_phase(): pl.pallas_call(functools.partial(element_kernel, neighbours=neighbours, c...]
    ppermute x8, starting transfers between devices: 11.9 us -> 42.1 us  [passed_along(): lax.ppermute(shard, axis, [(i, (i + by) % peers) for i in range(peers)])]
    reduce_scatter x1 -> x0, waiting for transfers between devices: 27.4 us -> none  [per_device(): lax.psum_scatter(jnp.dot(sinv, rhs_if, preferred_element_type=jnp.float32...]
  transfers between devices with their start and end apart: 10 -> 15, of which waited for: 4 -> 7; matrix products, arithmetic and copies ran while one was open for 2% -> 18% of each run, Pallas kernels for 0% -> 9%
where the time goes in v1:
time: 166 us; the launch traced here: 163 us
  starting transfers between devices  51.1 us (31%)
  Pallas kernels  46 us (28%)
  local copies, waits for them, and re-layouts  42.7 us (26%)
  waiting for transfers between devices  18.9 us (11%)
  other arithmetic  3.22 us (2%)
    ppermute x8, starting transfers between devices, passed_along(): lax.ppermute(shard, axis, [(i, (i + by) % peers) for i in range(peers)])  42.1 us
    unnamed x50, local copies, waits for them, and re-layouts  39.5 us
    pallas_call x1, Pallas kernels, element_phase(): pl.pallas_call(functools.partial(element_kernel, neighbours=neighbours, c...  16.8 us
    pallas_call x2, Pallas kernels, solve_blocks(): pl.pallas_call(solve_kernel, grid_spec=pltpu.PrefetchScalarGridSpec(num_s...  15.3 us
    ppermute x7, waiting for transfers between devices, swapped(): return lax.ppermute(shard, axis, [(i, i ^ bit) for i in range(peers)])  12.2 us
    ppermute x7, starting transfers between devices, swapped(): return lax.ppermute(shard, axis, [(i, i ^ bit) for i in range(peers)])  9.09 us
    ppermute x8, waiting for transfers between devices, passed_along(): lax.ppermute(shard, axis, [(i, (i + by) % peers) for i in range(peers)])  6.74 us
    pallas_call x1, Pallas kernels, per_device(): pl.pallas_call(interior_kernel, out_shape=jax.ShapeDtypeStruct((n_int, wi...  6.73 us
  transfers between devices with their start and end apart: 15, of which 7 were waited for; matrix products, arithmetic and copies ran while one was open for 18% of the time, Pallas kernels for 9%

profile of v1, /device:TPU:0, one launch (start us, length us, event | category | flops | bytes accessed | tf_op | source)
XLA Modules:
  0.0 163.4 jit_solution(9488553292136460370)
XLA Ops:
  0.6 0.8 reshape.65
  1.5 0.8 reshape.64
  2.2 1.1 copy.34.if_ref
  3.4 1.1 copy.33.int_ref
  4.5 0.1 pad_maximum_fusion
  4.6 0.8 gather_fusion
  5.4 0.1 broadcast_select_fusion
  5.5 5.1 %collective-permute-start = (bf16[32,192]{1,0:T(8,128)(2,1)S(1)}, bf16[32,192]{1,0:T(8,128)(2,1)S(1)}, u32[]{:S(2)}, u32[]{:S(2)}) collective-permute-start(bf16[32,192]{1,0:T(8,128)(2,1)S(1)} %get-tuple-element.30), channel_id=1, source_target_pairs={{0,6},{1,7},{2,0},{3,1},{4,2},{5,3},{6,4},{7,5},{8,14},{9,15},{10,... | collective-permute-start | bytes 36872 | tf_op jit(solution)/shard_map/ppermute | solution.py:347
  10.7 0.0 collective-permute-start.1
  10.7 0.5 collective-permute-start.2
  11.2 0.7 collective-permute-start.3
  11.9 0.8 pad_maximum_fusion.1.refs_5_
  13.3 0.0 collective-permute-done.refs_0_
  13.3 0.0 collective-permute-done.1.refs_1_
  13.3 2.3 %collective-permute-done.2.refs_2_ = bf16[32,192]{1,0:T(8,128)(2,1)S(1)} collective-permute-done((bf16[32,192]{1,0:T(8,128)(2,1)S(1)}, bf16[32,192]{1,0:T(8,128)(2,1)S(1)}, u32[]{:S(2)}, u32[]{:S(2)}) %collective-permute-start.2) | collective-permute-done | bytes 12320 | tf_op jit(solution)/shard_map/ppermute | solution.py:347
  15.6 1.1 collective-permute-done.3.refs_3_
  16.7 1.0 copy-done
  17.7 1.0 copy-done.2
  18.7 0.9 copy-done.4
  19.6 0.8 copy-done.5
  20.4 0.8 copy-done.6
  21.2 0.8 copy-done.7
  22.0 16.8 %elements.1 = (f32[48,2048]{1,0:T(8,128)}, f32[512,96]{1,0:T(8,128)S(1)}, f32[704,96]{1,0:T(8,128)S(1)}, f32[4,32,96]{2,1,0:T(8,128)S(1)}) custom-call(s32[1]{0:T(128)S(6)} %copy.43.count_ref, bf16[512,192]{1,0:T(8,128)(2,1)S(1)} %copy.33.int_ref, bf16[704,192]{1,0:T(8,128)(2,1)S(1)} %copy.34.if_ref, bf16[32,192]{1,0:T(8,128)(2,1)S(1)} %collective-permute-done.refs_0_, ...), custom_call_target="tpu_custom_call" | custom-call | tf_op jit(solution)/shard_map/elements/pallas_call | solution.py:214
  38.9 0.7 copy-done.1
  39.6 0.7 copy-done.3
  40.3 12.0 %collective-permute-start.4 = (f32[32,96]{1,0:T(8,128)S(1)}, f32[32,96]{1,0:T(8,128)S(1)}, u32[]{:S(2)}, u32[]{:S(2)}) collective-permute-start(f32[32,96]{1,0:T(8,128)S(1)} %get-tuple-element.26), channel_id=1, source_target_pairs={{0,2},{1,3},{2,4},{3,5},{4,6},{5,7},{6,0},{7,1},{8,10},{9,11},{10,... | collective-permute-start | bytes 36872 | tf_op jit(solution)/shard_map/ppermute | solution.py:347
  52.3 20.2 %collective-permute-start.5 = (f32[32,96]{1,0:T(8,128)S(1)}, f32[32,96]{1,0:T(8,128)S(1)}, u32[]{:S(2)}, u32[]{:S(2)}) collective-permute-start(f32[32,96]{1,0:T(8,128)S(1)} %get-tuple-element.25), channel_id=1, source_target_pairs={{0,1},{1,2},{2,3},{3,4},{4,5},{5,6},{6,7},{7,0},{8,9},{9,10},{10,1... | collective-permute-start | bytes 36872 | tf_op jit(solution)/shard_map/ppermute | solution.py:347
  72.6 3.1 %collective-permute-start.6 = (f32[32,96]{1,0:T(8,128)S(1)}, f32[32,96]{1,0:T(8,128)S(1)}, u32[]{:S(2)}, u32[]{:S(2)}) collective-permute-start(f32[32,96]{1,0:T(8,128)S(1)} %get-tuple-element.24), channel_id=1, source_target_pairs={{0,7},{1,0},{2,1},{3,2},{4,3},{5,4},{6,5},{7,6},{8,15},{9,8},{10,9... | collective-permute-start | bytes 36872 | tf_op jit(solution)/shard_map/ppermute | solution.py:347
  75.7 0.4 collective-permute-start.7
  76.1 0.0 collective-permute-done.4.refs_0_
  76.1 1.2 collective-permute-done.5.refs_1_
  77.3 0.0 collective-permute-done.6.refs_2_
  77.3 2.1 %collective-permute-done.7.refs_3_ = f32[32,96]{1,0:T(8,128)S(1)} collective-permute-done((f32[32,96]{1,0:T(8,128)S(1)}, f32[32,96]{1,0:T(8,128)S(1)}, u32[]{:S(2)}, u32[]{:S(2)}) %collective-permute-start.7) | collective-permute-done | bytes 12320 | tf_op jit(solution)/shard_map/ppermute | solution.py:347
  79.4 0.6 copy-done.20
  80.0 2.2 %interface_forces.1 = (f32[352,96]{1,0:T(8,128)}, f32[352,96]{1,0:T(8,128)}) custom-call(f32[704,96]{1,0:T(8,128)} %copy-done.1, s32[4,32]{1,0:T(4,128)} %map_ref.3, f32[32,96]{1,0:T(8,128)} %copy-done.17, f32[32,96]{1,0:T(8,128)} %copy-done.18, f32[32,96]{1,0:T(8,128)} %copy-done.19, f32[32,96]{1,0:T(8,128)} %copy-done.20), custom_call_target="tpu_custom_call" | custom-call | tf_op jit(solution)/shard_map/interface_forces/pallas_call | solution.py:385
  82.2 0.0 collective-permute-start.10
  82.2 5.8 %collective-permute-start.8 = (f32[352,96]{1,0:T(8,128)}, f32[352,96]{1,0:T(8,128)S(1)}, u32[]{:S(2)}, u32[]{:S(2)}) collective-permute-start(f32[352,96]{1,0:T(8,128)} %get-tuple-element.12), channel_id=1, source_target_pairs={{0,8},{8,0},{16,24},{24,16},{1,9},{9,1},{17,25},{25,17},{2,10},{10... | collective-permute-start | bytes 405512 | tf_op jit(solution)/shard_map/ppermute | solution.py:342
  88.1 1.1 copy.37.load_ref
  89.2 24.0 %copy.36 = bf16[4224,2112]{1,0:T(8,128)(2,1)} copy(bf16[4224,2112]{0,1:T(8,128)(2,1)} %param.33) | data formatting | bytes 35684352 | tf_op args[13]
  113.2 0.0 collective-permute-done.10
  113.3 0.1 collective-permute-start.11
  113.4 0.0 collective-permute-done.8
  113.4 0.0 copy-start.9
  113.4 0.1 collective-permute-start.9
  113.5 0.5 broadcast_xor_fusion.order_ref
  114.0 4.9 %collective-permute-done.11.got_b = f32[352,96]{1,0:T(8,128)S(1)} collective-permute-done((f32[352,96]{1,0:T(8,128)S(1)}, f32[352,96]{1,0:T(8,128)S(1)}, u32[]{:S(2)}, u32[]{:S(2)}) %collective-permute-start.11) | collective-permute-done | bytes 135200 | tf_op jit(solution)/shard_map/ppermute | solution.py:342
  118.9 0.1 collective-permute-done.9.got_a
  119.0 0.5 copy-done.14
  119.6 0.7 copy-done.15
  120.2 3.1 %interface_rhs.1.rhs_ref = bf16[2112,64]{1,0:T(8,128)(2,1)} custom-call(f32[704,192]{1,0:T(8,128)} %copy.37.load_ref, f32[352,96]{1,0:T(8,128)} %copy-done.9, f32[352,96]{1,0:T(8,128)} %copy-done.15, f32[352,96]{1,0:T(8,128)} %copy-done.8, f32[352,96]{1,0:T(8,128)} %copy-done.14, f32[96,192]{1,0:T(8,128)} %constant.36.clone.refs_5_.anal_ref), custom_call_target="tpu_custom_call" | custom-call | tf_op jit(solution)/shard_map/interface_rhs/pallas_call | solution.py:408
  123.3 7.6 %interface_solve.3 = f32[4,264,128]{2,1,0:T(8,128)} custom-call(s32[4]{0:T(128)} %broadcast_xor_fusion.order_ref, bf16[8,528,2112]{2,1,0:T(8,128)(2,1)} %bitcast.36, bf16[2112,64]{1,0:T(8,128)(2,1)} %interface_rhs.1.rhs_ref), custom_call_target="tpu_custom_call" | custom-call | flops 570949632 | bytes 8921088 | tf_op jit(solution)/shard_map/interface_solve/pallas_call | solution.py:312
  130.9 0.0 collective-permute-start.12
  130.9 0.5 multiply_xor_fusion.order_ref
  131.4 7.7 %interface_solve.2 = f32[4,264,128]{2,1,0:T(8,128)} custom-call(s32[4]{0:T(128)} %multiply_xor_fusion.order_ref, bf16[8,528,2112]{2,1,0:T(8,128)(2,1)} %bitcast.37, bf16[2112,64]{1,0:T(8,128)(2,1)} %interface_rhs.1.rhs_ref), custom_call_target="tpu_custom_call" | custom-call | flops 570949632 | bytes 8921088 | tf_op jit(solution)/shard_map/interface_solve/pallas_call | solution.py:312
  139.1 1.1 add.39
  140.2 1.9 %collective-permute-start.13 = (f32[2,264,128]{2,1,0:T(8,128)S(1)}, f32[2,264,128]{2,1,0:T(8,128)S(1)}, u32[]{:S(2)}, u32[]{:S(2)}) collective-permute-start(f32[2,264,128]{2,1,0:T(8,128)S(1)} %slice_bitcast_fusion), channel_id=1, source_target_pairs={{0,2},{1,3},{2,0},{3,1},{4,6},{5,7},{6,4},{7,5},{8,10},{9,11},{10,... | collective-permute-start | bytes 811016 | tf_op jit(solution)/shard_map/ppermute | solution.py:342
  142.1 7.2 %collective-permute-done.13 = f32[2,264,128]{2,1,0:T(8,128)S(1)} collective-permute-done((f32[2,264,128]{2,1,0:T(8,128)S(1)}, f32[2,264,128]{2,1,0:T(8,128)S(1)}, u32[]{:S(2)}, u32[]{:S(2)}) %collective-permute-start.13) | collective-permute-done | bytes 270368 | tf_op jit(solution)/shard_map/ppermute | solution.py:342
  149.3 0.7 slice_bitcast_fusion.2
  150.0 1.2 collective-permute-start.14
  151.2 1.0 copy.35.refs_4_
  152.2 6.7 %interior_solve.1 = f32[512,192]{1,0:T(8,128)} custom-call(f32[512,96]{1,0:T(8,128)} %copy-done.3, s32[4,32]{1,0:T(4,128)} %map_ref.3, f32[32,96]{1,0:T(8,128)} %copy-done.17, f32[32,96]{1,0:T(8,128)} %copy-done.18, f32[32,96]{1,0:T(8,128)} %copy-done.19, f32[32,96]{1,0:T(8,128)} %copy-done.20, f32[512,192]{1,0:T(8,128)} %copy.35.refs_4_, ...), custom_call_target="tpu_custom_call" | custom-call | flops 301989888 | bytes 4718592 | tf_op jit(solution)/shard_map/interior_solve/pallas_call | solution.py:398
  158.9 2.0 %copy.40 = f32[512,192]{0,1:T(8,128)} copy(f32[512,192]{1,0:T(8,128)} %interior_solve.1) | data formatting | bytes 786432
  160.9 0.6 copy-done.16
  161.6 1.8 %interface_result.1 = f32[176,192]{1,0:T(8,128)} custom-call(f32[1,264,128]{2,1,0:T(8,128)} %get-tuple-element.22.mine_ref, f32[1,264,128]{2,1,0:T(8,128)} %copy-done.16), custom_call_target="tpu_custom_call" | custom-call | tf_op jit(solution)/shard_map/interface_result/pallas_call | solution.py:428
  (42 shorter events, 0.2 us)
Async XLA Ops:
  0.6 87.5 %copy-start.10 = (f32[704,192]{0,1:T(8,128)S(1)}, f32[704,192]{0,1:T(8,128)}, u32[]{:S(2)}) copy-start(f32[704,192]{0,1:T(8,128)} %param.23) | copy-start | bytes 1622020
  5.5 7.8 %collective-permute-start = (bf16[32,192]{1,0:T(8,128)(2,1)S(1)}, bf16[32,192]{1,0:T(8,128)(2,1)S(1)}, u32[]{:S(2)}, u32[]{:S(2)}) collective-permute-start(bf16[32,192]{1,0:T(8,128)(2,1)S(1)} %get-tuple-element.30), channel_id=1, source_target_pairs={{0,6},{1,7},{2,0},{3,1},{4,2},{5,3},{6,4},{7,5},{8,14},{9,15},{10,... | collective-permute-start | bytes 36872 | tf_op jit(solution)/shard_map/ppermute | solution.py:347
  10.7 2.6 %collective-permute-start.1 = (bf16[32,192]{1,0:T(8,128)(2,1)S(1)}, bf16[32,192]{1,0:T(8,128)(2,1)S(1)}, u32[]{:S(2)}, u32[]{:S(2)}) collective-permute-start(bf16[32,192]{1,0:T(8,128)(2,1)S(1)} %get-tuple-element.29), channel_id=1, source_target_pairs={{0,7},{1,0},{2,1},{3,2},{4,3},{5,4},{6,5},{7,6},{8,15},{9,8},{10,9... | collective-permute-start | bytes 36872 | tf_op jit(solution)/shard_map/ppermute | solution.py:347
  10.7 5.0 %collective-permute-start.2 = (bf16[32,192]{1,0:T(8,128)(2,1)S(1)}, bf16[32,192]{1,0:T(8,128)(2,1)S(1)}, u32[]{:S(2)}, u32[]{:S(2)}) collective-permute-start(bf16[32,192]{1,0:T(8,128)(2,1)S(1)} %get-tuple-element.28), channel_id=1, source_target_pairs={{0,1},{1,2},{2,3},{3,4},{4,5},{5,6},{6,7},{7,0},{8,9},{9,10},{10,1... | collective-permute-start | bytes 36872 | tf_op jit(solution)/shard_map/ppermute | solution.py:347
  11.2 5.5 %collective-permute-start.3 = (bf16[32,192]{1,0:T(8,128)(2,1)S(1)}, bf16[32,192]{1,0:T(8,128)(2,1)S(1)}, u32[]{:S(2)}, u32[]{:S(2)}) collective-permute-start(bf16[32,192]{1,0:T(8,128)(2,1)S(1)} %get-tuple-element.27), channel_id=1, source_target_pairs={{0,2},{1,3},{2,4},{3,5},{4,6},{5,7},{6,0},{7,1},{8,10},{9,11},{10,... | collective-permute-start | bytes 36872 | tf_op jit(solution)/shard_map/ppermute | solution.py:347
  16.7 1.0 copy-start
  17.7 1.0 copy-start.2
  18.7 0.9 copy-start.4
  19.6 0.8 copy-start.5
  20.4 0.8 copy-start.6
  21.2 0.8 copy-start.7
  38.9 0.7 copy-start.1
  39.6 0.7 copy-start.3
  40.3 35.7 %collective-permute-start.4 = (f32[32,96]{1,0:T(8,128)S(1)}, f32[32,96]{1,0:T(8,128)S(1)}, u32[]{:S(2)}, u32[]{:S(2)}) collective-permute-start(f32[32,96]{1,0:T(8,128)S(1)} %get-tuple-element.26), channel_id=1, source_target_pairs={{0,2},{1,3},{2,4},{3,5},{4,6},{5,7},{6,0},{7,1},{8,10},{9,11},{10,... | collective-permute-start | bytes 36872 | tf_op jit(solution)/shard_map/ppermute | solution.py:347
  52.3 24.9 %collective-permute-start.5 = (f32[32,96]{1,0:T(8,128)S(1)}, f32[32,96]{1,0:T(8,128)S(1)}, u32[]{:S(2)}, u32[]{:S(2)}) collective-permute-start(f32[32,96]{1,0:T(8,128)S(1)} %get-tuple-element.25), channel_id=1, source_target_pairs={{0,1},{1,2},{2,3},{3,4},{4,5},{5,6},{6,7},{7,0},{8,9},{9,10},{10,1... | collective-permute-start | bytes 36872 | tf_op jit(solution)/shard_map/ppermute | solution.py:347
  72.6 4.7 %collective-permute-start.6 = (f32[32,96]{1,0:T(8,128)S(1)}, f32[32,96]{1,0:T(8,128)S(1)}, u32[]{:S(2)}, u32[]{:S(2)}) collective-permute-start(f32[32,96]{1,0:T(8,128)S(1)} %get-tuple-element.24), channel_id=1, source_target_pairs={{0,7},{1,0},{2,1},{3,2},{4,3},{5,4},{6,5},{7,6},{8,15},{9,8},{10,9... | collective-permute-start | bytes 36872 | tf_op jit(solution)/shard_map/ppermute | solution.py:347
  75.7 3.7 %collective-permute-start.7 = (f32[32,96]{1,0:T(8,128)S(1)}, f32[32,96]{1,0:T(8,128)S(1)}, u32[]{:S(2)}, u32[]{:S(2)}) collective-permute-start(f32[32,96]{1,0:T(8,128)S(1)} %get-tuple-element.23), channel_id=1, source_target_pairs={{0,6},{1,7},{2,0},{3,1},{4,2},{5,3},{6,4},{7,5},{8,14},{9,15},{10,... | collective-permute-start | bytes 36872 | tf_op jit(solution)/shard_map/ppermute | solution.py:347
  76.1 3.3 %copy-start.17 = (f32[32,96]{1,0:T(8,128)}, f32[32,96]{1,0:T(8,128)S(1)}, u32[]{:S(2)}) copy-start(f32[32,96]{1,0:T(8,128)S(1)} %collective-permute-done.4.refs_0_) | copy-start | bytes 36868
  77.3 2.2 %copy-start.18 = (f32[32,96]{1,0:T(8,128)}, f32[32,96]{1,0:T(8,128)S(1)}, u32[]{:S(2)}) copy-start(f32[32,96]{1,0:T(8,128)S(1)} %collective-permute-done.5.refs_1_) | copy-start | bytes 36868
  77.3 2.2 %copy-start.19 = (f32[32,96]{1,0:T(8,128)}, f32[32,96]{1,0:T(8,128)S(1)}, u32[]{:S(2)}) copy-start(f32[32,96]{1,0:T(8,128)S(1)} %collective-permute-done.6.refs_2_) | copy-start | bytes 36868
  79.4 0.6 copy-start.20
  82.2 31.0 %collective-permute-start.10 = (f32[352,96]{1,0:T(8,128)}, f32[352,96]{1,0:T(8,128)S(1)}, u32[]{:S(2)}, u32[]{:S(2)}) collective-permute-start(f32[352,96]{1,0:T(8,128)} %get-tuple-element.13), channel_id=1, source_target_pairs={{0,16},{8,24},{16,0},{24,8},{1,17},{9,25},{17,1},{25,9},{2,18},{10... | collective-permute-start | bytes 405512 | tf_op jit(solution)/shard_map/ppermute | solution.py:342
  82.2 31.1 %collective-permute-start.8 = (f32[352,96]{1,0:T(8,128)}, f32[352,96]{1,0:T(8,128)S(1)}, u32[]{:S(2)}, u32[]{:S(2)}) collective-permute-start(f32[352,96]{1,0:T(8,128)} %get-tuple-element.12), channel_id=1, source_target_pairs={{0,8},{8,0},{16,24},{24,16},{1,9},{9,1},{17,25},{25,17},{2,10},{10... | collective-permute-start | bytes 405512 | tf_op jit(solution)/shard_map/ppermute | solution.py:342
  89.2 24.0 %copy-start.13 = (f32[352,96]{1,0:T(8,128)S(1)}, f32[352,96]{1,0:T(8,128)}, u32[]{:S(2)}) copy-start(f32[352,96]{1,0:T(8,128)} %get-tuple-element.13) | copy-start | bytes 405508
  89.2 24.1 %copy-start.12 = (f32[352,96]{1,0:T(8,128)S(1)}, f32[352,96]{1,0:T(8,128)}, u32[]{:S(2)}) copy-start(f32[352,96]{1,0:T(8,128)} %get-tuple-element.12) | copy-start | bytes 405508
  89.2 24.3 %copy-start.21 = (s32[4]{0:T(128)S(1)}, s32[4]{0:T(128)}, u32[]{:S(2)}) copy-start(s32[4]{0:T(128)} %constant.37.clone) | copy-start | bytes 52
  113.3 5.8 %copy-start.8 = (f32[352,96]{1,0:T(8,128)}, f32[352,96]{1,0:T(8,128)S(1)}, u32[]{:S(2)}) copy-start(f32[352,96]{1,0:T(8,128)S(1)} %add.38.own_b) | copy-start | bytes 405508
  113.3 5.6 %collective-permute-start.11 = (f32[352,96]{1,0:T(8,128)S(1)}, f32[352,96]{1,0:T(8,128)S(1)}, u32[]{:S(2)}, u32[]{:S(2)}) collective-permute-start(f32[352,96]{1,0:T(8,128)S(1)} %add.38.own_b), channel_id=1, source_target_pairs={{0,8},{8,0},{16,24},{24,16},{1,9},{9,1},{17,25},{25,17},{2,10},{10... | collective-permute-start | bytes 405512 | tf_op jit(solution)/shard_map/ppermute | solution.py:342
  113.4 5.6 %copy-start.9 = (f32[352,96]{1,0:T(8,128)}, f32[352,96]{1,0:T(8,128)S(1)}, u32[]{:S(2)}) copy-start(f32[352,96]{1,0:T(8,128)S(1)} %add.37.own_a) | copy-start | bytes 405508
  113.4 5.6 %collective-permute-start.9 = (f32[352,96]{1,0:T(8,128)S(1)}, f32[352,96]{1,0:T(8,128)S(1)}, u32[]{:S(2)}, u32[]{:S(2)}) collective-permute-start(f32[352,96]{1,0:T(8,128)S(1)} %add.37.own_a), channel_id=1, source_target_pairs={{0,16},{8,24},{16,0},{24,8},{1,17},{9,25},{17,1},{25,9},{2,18},{10... | collective-permute-start | bytes 405512 | tf_op jit(solution)/shard_map/ppermute | solution.py:342
  118.9 0.7 copy-start.14
  119.6 0.7 copy-start.15
  130.9 8.2 %collective-permute-start.12 = (f32[4,264,128]{2,1,0:T(8,128)}, f32[4,264,128]{2,1,0:T(8,128)S(1)}, u32[]{:S(2)}, u32[]{:S(2)}) collective-permute-start(f32[4,264,128]{2,1,0:T(8,128)} %interface_solve.3), channel_id=1, source_target_pairs={{0,1},{1,0},{2,3},{3,2},{4,5},{5,4},{6,7},{7,6},{8,9},{9,8},{10,11... | collective-permute-start | bytes 1622024 | tf_op jit(solution)/shard_map/ppermute | solution.py:342
  131.4 19.8 %copy-start.11 = (f32[512,192]{0,1:T(8,128)S(1)}, f32[512,192]{0,1:T(8,128)}, u32[]{:S(2)}) copy-start(f32[512,192]{0,1:T(8,128)} %param.22) | copy-start | bytes 1179652
  140.2 9.0 %collective-permute-start.13 = (f32[2,264,128]{2,1,0:T(8,128)S(1)}, f32[2,264,128]{2,1,0:T(8,128)S(1)}, u32[]{:S(2)}, u32[]{:S(2)}) collective-permute-start(f32[2,264,128]{2,1,0:T(8,128)S(1)} %slice_bitcast_fusion), channel_id=1, source_target_pairs={{0,2},{1,3},{2,0},{3,1},{4,6},{5,7},{6,4},{7,5},{8,10},{9,11},{10,... | collective-permute-start | bytes 811016 | tf_op jit(solution)/shard_map/ppermute | solution.py:342
  150.0 10.9 %collective-permute-start.14 = (f32[1,264,128]{2,1,0:T(8,128)S(1)}, f32[1,264,128]{2,1,0:T(8,128)S(1)}, u32[]{:S(2)}, u32[]{:S(2)}) collective-permute-start(f32[1,264,128]{2,1,0:T(8,128)S(1)} %get-tuple-element.21), channel_id=1, source_target_pairs={{0,4},{1,5},{2,6},{3,7},{4,0},{5,1},{6,2},{7,3},{8,12},{9,13},{10,... | collective-permute-start | bytes 405512 | tf_op jit(solution)/shard_map/ppermute | solution.py:342
  160.9 0.6 copy-start.16

commit v2 on v1

v2 whole, which is shorter than its diff:
```python
import functools
import math

import jax
import jax.numpy as jnp
import numpy as np
from jax import lax
from jax.experimental import pallas as pl
from jax.experimental.pallas import tpu as pltpu
from jax.sharding import PartitionSpec as P

TIMES = 32
POISSON = 0.3
LAME = POISSON / ((1.0 + POISSON) * (1.0 - 2.0 * POISSON))
SHEAR = 1.0 / (2.0 * (1.0 + POISSON))
HIGHEST = lax.Precision.HIGHEST
STEPS = 4
GROUPS = TIMES // STEPS
PART = 3 * STEPS
SLOT = 16
ROWS = GROUPS * SLOT
NT = (((1,), (1,)), ((), ()))
BF16 = jnp.bfloat16
F32 = jnp.float32


def strain_table():
    gauss = 1.0 / math.sqrt(3.0)
    table = np.zeros((6, 8, 8, 3))
    for point in range(8):
        coords = [((point >> bit & 1) * 2 - 1) * gauss for bit in range(3)]
        for corner in range(8):
            signs = [(corner >> bit & 1) * 2 - 1 for bit in range(3)]
            deriv = []
            for axis in range(3):
                value = signs[axis] / 8.0
                for other in range(3):
                    if other != axis:
                        value = value * (1.0 + signs[other] * coords[other])
                deriv.append(value)
            table[0, point, corner, 0] = deriv[0]
            table[1, point, corner, 1] = deriv[1]
            table[2, point, corner, 2] = deriv[2]
            table[3, point, corner, 0] = deriv[1]
            table[3, point, corner, 1] = deriv[0]
            table[4, point, corner, 1] = deriv[2]
            table[4, point, corner, 2] = deriv[1]
            table[5, point, corner, 2] = deriv[0]
            table[5, point, corner, 0] = deriv[2]
    return table.reshape(48, 24).astype(np.float32)


def time_tables(fourier):
    theta = 2.0 * math.pi * (np.arange(TIMES) + 0.3) / TIMES
    synthesis = np.zeros((fourier, TIMES))
    for column in range(fourier):
        harmonic = column // 2
        if column % 2 == 0:
            synthesis[column] = np.cos(harmonic * theta)
        else:
            synthesis[column] = np.sin((harmonic + 1) * theta)
    analysis = synthesis.T * (2.0 / TIMES)
    analysis[:, 0] = 1.0 / TIMES
    return synthesis.astype(np.float32), analysis.astype(np.float32)


def constants(fourier):
    synthesis, analysis = time_tables(fourier)
    differences = synthesis.astype(np.float64) - np.roll(synthesis.astype(np.float64), 1, axis=1)
    synth = np.zeros((GROUPS, 2, 3, STEPS, 3, fourier))
    anal = np.zeros((GROUPS, SLOT, 3, fourier))
    for comp in range(3):
        synth[:, :, comp, :, comp, :] = differences.T.reshape(GROUPS, 1, STEPS, fourier)
        anal[:, comp * STEPS : (comp + 1) * STEPS, comp, :] = analysis.reshape(GROUPS, STEPS, fourier)
    synth = jnp.asarray(synth.reshape(2 * GROUPS * PART, 3 * fourier), F32)
    table = strain_table().reshape(48, 8, 3)
    strain = np.zeros((STEPS, 48, 8, 2, 3, STEPS), np.float32)
    force = np.zeros((8, SLOT, STEPS, 48), np.float32)
    for step in range(STEPS):
        for half in range(2):
            strain[step, :, :, half, :, step] = table
        for comp in range(3):
            force[:, comp * STEPS + step, step, :] = table[:, :, comp].T
    high = synth.astype(BF16)
    low = (synth - high.astype(F32)).astype(BF16)
    return (
        high,
        low,
        jnp.asarray(strain.reshape(STEPS * 48, 16 * PART)).astype(BF16),
        jnp.asarray(force.reshape(8 * SLOT, STEPS * 48)).astype(BF16),
        jnp.asarray(anal.reshape(ROWS, 3 * fourier), F32),
    )


def up(n, to):
    return -(-n // to) * to


def element_kernel(*refs, neighbours, chunk, own, half):
    count_ref, int_ref, if_ref = refs[:3]
    halo_refs = refs[3 : 3 + neighbours]
    conn_ref, size_ref, stiff_ref, yield_ref, rate_ref, init_ref = refs[3 + neighbours : 9 + neighbours]
    high_ref, low_ref, strain_ref, force_ref = refs[9 + neighbours : 13 + neighbours]
    end_ref, pint_ref, pif_ref, back_ref = refs[13 + neighbours : 17 + neighbours]
    nodes, onehot, corners, forces, state, total = refs[17 + neighbours :]
    n_int, n_if, slots = int_ref.shape[1], if_ref.shape[1], halo_refs[0].shape[0]
    halo_at = up(own, 128)
    both = 2 * GROUPS * PART
    chunks = end_ref.shape[1] // chunk
    count = count_ref[0]
    used = lax.div(count + chunk - 1, chunk)

    nodes[...] = jnp.zeros_like(nodes)
    total[...] = jnp.zeros_like(total)
    halo = jnp.concatenate([ref[...].astype(F32) for ref in halo_refs], axis=0).astype(BF16)
    is_high = lax.rem(lax.broadcasted_iota(jnp.int32, (both, 1), 0), 2 * PART) < PART
    pieces = (
        (0, int_ref[...], (((1,), (0,)), ((), ()))),
        (n_int, if_ref[...], (((1,), (0,)), ((), ()))),
        (halo_at, halo, NT),
    )
    spans = []
    for start, rows, dims in pieces:
        value = lax.dot_general(high_ref[...], rows, dims, preferred_element_type=F32)
        value = value + lax.dot_general(low_ref[...], rows, dims, preferred_element_type=F32)
        upper = value.astype(BF16).astype(F32)
        value = jnp.where(is_high, upper, value - upper).astype(BF16)
        length = value.shape[1]
        cut = min(max(half - start, 0), length)
        if cut:
            nodes[:both, start : start + cut] = value[:, :cut]
        if cut < length:
            at = start + cut - half
            nodes[both:, at : at + length - cut] = value[:, cut:]

    def columns(c):
        return pl.ds(pl.multiple_of(c * chunk, chunk), chunk)

    def place(c, corner):
        node = conn_ref[pl.ds(corner, 1), columns(c)]
        node = node + jnp.where(node >= own, halo_at - own, 0)
        upper = node >= half
        return upper, node - jnp.where(upper, half, 0)

    def gather(c, corner):
        upper, node = place(c, corner)
        hot = jnp.where(lax.broadcasted_iota(jnp.int32, (half, chunk), 0) == node, 1.0, 0.0).astype(BF16)
        onehot[lax.rem(c, 3), corner] = hot
        found = jnp.dot(nodes[...], hot, preferred_element_type=F32)
        found = jnp.where(upper, found[both:], found[:both])
        rows = pl.ds(pl.multiple_of(corner * 2 * PART, 8), 2 * PART)
        for group in range(GROUPS):
            corners[lax.rem(c, 2), group, rows, :] = found[group * 2 * PART : (group + 1) * 2 * PART]

    def alive(c):
        slot = c * chunk + lax.broadcasted_iota(jnp.int32, (1, chunk), 1)
        return jnp.where(slot < count, 1.0, 0.0)

    def advance(c, group):
        at = columns(c)
        size, limit, rate = size_ref[:, at], yield_ref[:, at], rate_ref[:, at]
        modulus = stiff_ref[:, at] * (2.0 / size)

        def wide(row):
            return jnp.broadcast_to(row, (8, chunk))

        twice_shear, shear, lame = wide(modulus * (2.0 * SHEAR)), wide(modulus * SHEAR), wide(modulus * LAME)
        inverse, relax = wide(1.0 / limit), wide(rate * limit)
        scale = size * size * 0.25 * alive(c)
        corner_values = corners[lax.rem(c, 2), group].astype(BF16)
        delta = jnp.dot(strain_ref[...], corner_values, preferred_element_type=F32)
        stress = tuple(state[comp * 8 : comp * 8 + 8, :] for comp in range(6))
        history = []
        for step in range(STEPS):
            d = [delta[step * 48 + comp * 8 : step * 48 + comp * 8 + 8] for comp in range(6)]
            trace = lame * (d[0] + d[1] + d[2])
            stress = tuple(
                s + (twice_shear * d[comp] + trace if comp < 3 else shear * d[comp]) - relax * jnp.tanh(s * inverse)
                for comp, s in enumerate(stress)
            )
            history += list(stress)
        for comp in range(6):
            state[comp * 8 : comp * 8 + 8, :] = stress[comp]
        force = jnp.dot(force_ref[...], jnp.concatenate(history, axis=0).astype(BF16), preferred_element_type=F32)
        force = (force * scale).astype(BF16)
        rows = pl.ds(pl.multiple_of(group * SLOT, SLOT), SLOT)
        for corner in range(8):
            forces[lax.rem(c, 2), corner, rows, :] = force[corner * SLOT : (corner + 1) * SLOT]

    def scatter(c, corner):
        upper, _ = place(c, corner)
        part = forces[lax.rem(c, 2), corner].astype(F32)
        part = jnp.concatenate([jnp.where(upper, 0.0, part), jnp.where(upper, part, 0.0)], axis=0).astype(BF16)
        total[...] += lax.dot_general(onehot[lax.rem(c, 3), corner], part, NT, preferred_element_type=F32)

    turns = 4

    def stage(c, first, middle, last):
        if middle:
            state[...] = init_ref[:, columns(c)]

        @pl.loop(0, 8, step=turns)
        def _(turn):
            for k in range(turns) if last else ():
                scatter(c - 1, turn + k)
            for k in range(turns) if middle else ():
                advance(c, turn + k)
            for k in range(turns) if first else ():
                gather(c + 1, turn + k)

        if middle:
            end_ref[:, columns(c)] = state[...] * alive(c)

    stage(-1, True, False, False)

    @pl.when(used > 1)
    def _():
        stage(0, True, True, False)

        @pl.loop(1, used - 1)
        def _(c):
            stage(c, True, True, True)

        stage(used - 1, False, True, True)

    @pl.when(used == 1)
    def _():
        stage(0, False, True, False)

    stage(used, False, False, True)

    @pl.loop(used, chunks)
    def _(c):
        end_ref[:, columns(c)] = jnp.zeros((end_ref.shape[0], chunk), F32)

    def result(start, length):
        cut = min(max(half - start, 0), length)
        runs = []
        if cut:
            runs.append(total[start : start + cut, :ROWS])
        if cut < length:
            runs.append(total[start + cut - half : start + length - half, ROWS:])
        return runs[0] if len(runs) == 1 else jnp.concatenate(runs, axis=0)

    pint_ref[...] = result(0, n_int)
    pif_ref[...] = result(n_int, n_if)
    for slot_index in range(neighbours):
        back_ref[slot_index] = result(halo_at + slot_index * slots, slots)


def whole(shape):
    return pl.BlockSpec(shape, lambda *_: (0,) * len(shape))


def element_phase(count, u_int, u_if, halos, conn, params, stress_init, tables, interpret=False):
    chunk = 256
    n_int, n_if = u_int.shape[1], u_if.shape[1]
    own = n_int + n_if
    neighbours, slots = len(halos), halos[0].shape[0]
    half = up(up(own, 128) + neighbours * slots, 256) // 2
    half = up(half, 128)
    vmem = pl.BlockSpec(memory_space=pltpu.VMEM)
    inputs = [u_int, u_if, *halos, conn, *params, stress_init, *tables[:4]]
    return pl.pallas_call(
        functools.partial(element_kernel, neighbours=neighbours, chunk=chunk, own=own, half=half),
        in_specs=[pl.BlockSpec(memory_space=pltpu.SMEM)] + [vmem] * len(inputs),
        out_specs=[vmem] * 4,
        scratch_shapes=[
            pltpu.VMEM((4 * GROUPS * PART, half), BF16),
            pltpu.VMEM((3, 8, half, chunk), BF16),
            pltpu.VMEM((2, GROUPS, 16 * PART, chunk), F32),
            pltpu.VMEM((2, 8, ROWS, chunk), BF16),
            pltpu.VMEM((stress_init.shape[0], chunk), F32),
            pltpu.VMEM((half, 2 * ROWS), F32),
        ],
        out_shape=[
            jax.ShapeDtypeStruct(stress_init.shape, F32),
            jax.ShapeDtypeStruct((n_int, ROWS), F32),
            jax.ShapeDtypeStruct((n_if, ROWS), F32),
            jax.ShapeDtypeStruct((neighbours, slots, ROWS), F32),
        ],
        compiler_params=pltpu.CompilerParams(vmem_limit_bytes=60 << 20),
        name="elements",
        interpret=interpret,
    )(count, *inputs)


def send_kernel(int_ref, if_ref, map_ref, *out_refs):
    n_int, n_if = int_ref.shape[1], if_ref.shape[1]
    slots = map_ref.shape[1]
    for slot_index, out_ref in enumerate(out_refs):
        wanted = map_ref[slot_index : slot_index + 1, :]
        rows = None
        for first, ref in ((0, int_ref), (n_int, if_ref)):
            hot = lax.broadcasted_iota(jnp.int32, (ref.shape[1], slots), 0) + first == wanted
            hot = jnp.where(hot, 1.0, 0.0).astype(BF16)
            found = jnp.dot(ref[...], hot, preferred_element_type=F32)
            rows = found if rows is None else rows + found
        out_ref[...] = rows.T.astype(BF16)


def send_blocks(u_int, u_if, send_map):
    neighbours, slots = send_map.shape
    return pl.pallas_call(
        send_kernel,
        out_shape=[jax.ShapeDtypeStruct((slots, u_int.shape[0]), BF16)] * neighbours,
        name="halo_rows",
    )(u_int, u_if, send_map)


def added_back(own, map_ref, returned, first):
    for slot_index, ref in enumerate(returned):
        hot = (
            lax.broadcasted_iota(jnp.int32, (own.shape[0], ref.shape[0]), 0) + first
            == map_ref[slot_index : slot_index + 1, :]
        )
        hot = jnp.where(hot, 1.0, 0.0).astype(BF16)
        value = ref[...]
        high = value.astype(BF16)
        low = (value - high.astype(F32)).astype(BF16)
        own = own + jnp.dot(hot, high, preferred_element_type=F32) + jnp.dot(hot, low, preferred_element_type=F32)
    return own


def interface_kernel(own_ref, map_ref, *refs, first):
    returned, (a_ref, b_ref) = refs[:-2], refs[-2:]
    value = added_back(own_ref[...], map_ref, returned, first)
    half = a_ref.shape[0]
    a_ref[...] = value[:half]
    b_ref[...] = value[half:]


def interleaved(value, scratch):
    nodes, width = value.shape
    fourier = width // 3
    for comp in range(3):
        scratch[pl.ds(comp, nodes, stride=3), :] = value[:, comp * fourier : (comp + 1) * fourier]
    return scratch[...]


def separated(value, scratch):
    scratch[...] = value
    nodes = value.shape[0] // 3
    return jnp.concatenate([scratch[pl.ds(comp, nodes, stride=3), :] for comp in range(3)], axis=1)


def interior_kernel(own_ref, map_ref, *refs):
    returned = refs[:-5]
    load_ref, anal_ref, kinv_ref, du_ref, scratch = refs[-5:]
    value = added_back(own_ref[...], map_ref, returned, 0)
    force = jnp.dot(value, anal_ref[...], precision=HIGHEST, preferred_element_type=F32)
    rhs = interleaved(load_ref[...].T - force, scratch).astype(BF16)
    du = jnp.dot(kinv_ref[...], rhs, preferred_element_type=F32)
    du_ref[...] = separated(du, scratch).T


def solve_kernel(me_ref, load_ref, own_a, got_a, own_b, got_b, anal_ref, sinv_ref, *refs, peers):
    away_ref, near_ref, rhs, scratch, total, rows = refs
    index = pl.program_id(0)

    @pl.when(index == 0)
    def _():
        value = jnp.concatenate([own_a[...] + got_a[...], own_b[...] + got_b[...]], axis=0)
        force = jnp.dot(value, anal_ref[...], precision=HIGHEST, preferred_element_type=F32)
        right = interleaved(load_ref[...].T - force, scratch).T.astype(BF16)
        depth = rhs.shape[2]
        for block in range(rhs.shape[0]):
            rhs[block] = right[:, block * depth : (block + 1) * depth]

    term = jnp.dot(rhs[index], sinv_ref[...], preferred_element_type=F32)

    @pl.when(index == 0)
    def _():
        total[...] = term

    @pl.when(index > 0)
    def _():
        total[...] += term

    @pl.when(index == pl.num_programs(0) - 1)
    def _():
        rows[...] = total[...].T
        count = rows.shape[0] // peers
        for j in range(peers):
            at = (me_ref[0] ^ j) * count
            upper, lower = rows[pl.ds(at, count // 2), :], rows[pl.ds(at + count // 2, count // 2), :]
            out_ref = away_ref if j & 1 else near_ref
            out_ref[j // 2] = jnp.concatenate([upper, lower], axis=1).astype(out_ref.dtype)


def interface_solve(me, load, own_a, got_a, own_b, got_b, analysis, sinv, peers, dtype):
    depth_all, rows = sinv.shape
    blocks = next(b for b in (4, 3, 2, 1) if b == 1 or depth_all % (b * 16) == 0)
    depth = depth_all // blocks
    fourier = load.shape[0] // 3
    shape = (peers // 2, rows // peers // 2, 2 * fourier)
    small = [load, own_a, got_a, own_b, got_b, analysis]
    return pl.pallas_call(
        functools.partial(solve_kernel, peers=peers),
        grid_spec=pltpu.PrefetchScalarGridSpec(
            num_scalar_prefetch=1,
            grid=(blocks,),
            in_specs=[whole(x.shape) for x in small] + [pl.BlockSpec((depth, rows), lambda k, me: (k, 0))],
            out_specs=[whole(shape)] * 2,
            scratch_shapes=[
                pltpu.VMEM((blocks, fourier, depth), BF16),
                pltpu.VMEM((depth_all, fourier), F32),
                pltpu.VMEM((fourier, rows), F32),
                pltpu.VMEM((rows, fourier), F32),
            ],
        ),
        out_shape=[jax.ShapeDtypeStruct(shape, dtype), jax.ShapeDtypeStruct(shape, F32)],
        compiler_params=pltpu.CompilerParams(vmem_limit_bytes=40 << 20),
        name="interface_solve",
    )(me, *small, sinv)


def last_kernel(mine_ref, got_ref, out_ref, scratch):
    value = mine_ref[0] + got_ref[0].astype(F32)
    half = value.shape[0]
    fourier = value.shape[1] // 2
    out_ref[...] = separated(jnp.concatenate([value[:, :fourier], value[:, fourier:]], axis=0), scratch)


def swapped(shard, axis, bit):
    peers = lax.axis_size(axis)
    return lax.ppermute(shard, axis, [(i, i ^ bit) for i in range(peers)])


def passed_along(shard, axis, by):
    peers = lax.axis_size(axis)
    return lax.ppermute(shard, axis, [(i, (i + by) % peers) for i in range(peers)])


def per_device(
    u_int,
    u_if,
    load_int,
    load_if,
    conn,
    send_map,
    counts,
    elem_size,
    stiffness,
    yield_stress,
    relax_rate,
    stress_init,
    kinv_int,
    sinv,
):
    width = u_int.shape[1]
    fourier = width // 3
    n_int, n_if = u_int.shape[0], u_if.shape[0]
    neighbours, slots = send_map.shape
    reach = neighbours // 2
    offsets = list(range(-reach, 0)) + list(range(1, reach + 1))
    tables = constants(fourier)
    analysis = tables[4]

    blocks = send_blocks(u_int.T, u_if.T, send_map)
    halos = [passed_along(blocks[j], "dom", offsets[j]) for j in range(neighbours)]
    params = [x.reshape(1, -1) for x in (elem_size, stiffness, yield_stress, relax_rate)]
    stress_end, p_int, p_if, back = element_phase(
        counts, u_int.T, u_if.T, halos, conn.T, params, stress_init, tables
    )
    returned = [passed_along(back[j], "dom", -offsets[j]) for j in range(neighbours)]

    half = n_if // 2
    part_a, part_b = pl.pallas_call(
        functools.partial(interface_kernel, first=n_int),
        out_shape=[jax.ShapeDtypeStruct((half, ROWS), F32), jax.ShapeDtypeStruct((n_if - half, ROWS), F32)],
        name="interface_forces",
    )(p_if, send_map, *returned)

    bits = [1 << b for b in range(lax.axis_size("grp").bit_length() - 1)]
    got_a = got_b = None
    for bit_a, bit_b in zip(bits, bits[::-1]):
        if got_a is not None:
            part_a, part_b = part_a + got_a, part_b + got_b
        got_a, got_b = swapped(part_a, "grp", bit_a), swapped(part_b, "grp", bit_b)

    du_int = pl.pallas_call(
        interior_kernel,
        out_shape=jax.ShapeDtypeStruct((width, n_int), F32),
        scratch_shapes=[pltpu.VMEM((3 * n_int, fourier), F32)],
        cost_estimate=pl.CostEstimate(
            flops=2 * kinv_int.size * fourier, bytes_accessed=2 * kinv_int.size, transcendentals=0
        ),
        name="interior_solve",
    )(p_int, send_map, *returned, load_int.T, analysis, kinv_int).T

    peers = lax.axis_size("dom")
    me = lax.axis_index("dom").astype(jnp.int32).reshape(1)
    levels = peers.bit_length() - 1
    sent, mine = interface_solve(
        me, load_if.T, part_a, got_a, part_b, got_b, analysis, sinv.T, peers, F32
    )
    got = swapped(sent, "dom", 1)
    for level in range(1, levels):
        both = (mine + got).reshape(peers >> (level + 1), 2, *mine.shape[1:])
        mine = both[:, 0]
        got = swapped(both[:, 1], "dom", 1 << level)
    rows = sinv.shape[0] // peers
    du_if = pl.pallas_call(
        last_kernel,
        out_shape=jax.ShapeDtypeStruct((rows // 3, width), F32),
        scratch_shapes=[pltpu.VMEM((rows, fourier), F32)],
        name="interface_result",
    )(mine, got)
    return (du_int, du_if, stress_end)


def solution(mesh):
    return jax.shard_map(
        per_device,
        mesh=mesh,
        in_specs=(
            P(("grp", "dom"), None),
            P("dom", None),
            P(("grp", "dom"), None),
            P("dom", None),
            P(("grp", "dom"), None),
            P(("grp", "dom"), None),
            P(("grp", "dom")),
            P(("grp", "dom")),
            P(("grp", "dom")),
            P(("grp", "dom")),
            P(("grp", "dom")),
            P(None, ("grp", "dom")),
            P(("grp", "dom"), None),
            P("grp", "dom"),
        ),
        out_specs=(P(("grp", "dom"), None), P(("grp", "dom"), None), P(None, ("grp", "dom"))),
        check_vma=False,
    )
```

time: 166 us -> 107 us (0.64); the launches traced: 163 us -> 109 us
  local copies, waits for them, and re-layouts: 42.7 us -> 5.29 us
  starting transfers between devices: 51.1 us -> 36.5 us
  Pallas kernels: 46 us -> 35.3 us
  waiting for transfers between devices: 18.9 us -> 28.1 us
    unnamed x50 -> x22, local copies, waits for them, and re-layouts: 39.5 us -> 3.82 us
    ppermute x8, starting transfers between devices: 42.1 us -> 32.7 us  [passed_along(): lax.ppermute(shard, axis, [(i, (i + by) % peers) for i in range(peers)])]
    ppermute x7, waiting for transfers between devices: 12.2 us -> 20.3 us  [swapped(): return lax.ppermute(shard, axis, [(i, i ^ bit) for i in range(peers)])]
    pallas_call x4 -> x3, Pallas kernels: 25.1 us -> 19.4 us  [the longest x1 10.3 us: interface_solve(): pl.pallas_call(functools.partial(solve_kernel, peers=peers), grid_spec=pl...]
    ppermute x7, starting transfers between devices: 9.09 us -> 3.83 us  [swapped(): return lax.ppermute(shard, axis, [(i, i ^ bit) for i in range(peers)])]
    pallas_call x1, Pallas kernels: 16.8 us -> 11.8 us  [element_phase(): pl.pallas_call(functools.partial(element_kernel, neighbours=neighbours, c...]
    add x2, other arithmetic: 0.04 us -> 1.9 us  [per_device(): part_a, part_b = (part_a + got_a, part_b + got_b)]
  transfers between devices with their start and end apart: 15 -> 15, of which waited for: 7 -> 10; matrix products, arithmetic and copies ran while one was open for 18% -> 2% of each run, Pallas kernels for 9% -> 6%
where the time goes in v2:
time: 107 us; the launch traced here: 109 us
  starting transfers between devices  36.5 us (34%)
  Pallas kernels  35.3 us (33%)
  waiting for transfers between devices  28.1 us (26%)
  local copies, waits for them, and re-layouts  5.29 us (5%)
  other arithmetic  2 us (2%)
  between operations  1.41 us (1%)
    ppermute x8, starting transfers between devices, passed_along(): lax.ppermute(shard, axis, [(i, (i + by) % peers) for i in range(peers)])  32.7 us
    ppermute x7, waiting for transfers between devices, swapped(): return lax.ppermute(shard, axis, [(i, i ^ bit) for i in range(peers)])  20.3 us
    pallas_call x1, Pallas kernels, element_phase(): pl.pallas_call(functools.partial(element_kernel, neighbours=neighbours, c...  11.8 us
    pallas_call x1, Pallas kernels, interface_solve(): pl.pallas_call(functools.partial(solve_kernel, peers=peers), grid_spec=pl...  10.3 us
    ppermute x8, waiting for transfers between devices, passed_along(): lax.ppermute(shard, axis, [(i, (i + by) % peers) for i in range(peers)])  7.72 us
    pallas_call x1, Pallas kernels, per_device(): pl.pallas_call(interior_kernel, out_shape=jax.ShapeDtypeStruct((width, n_...  6.81 us
    ppermute x7, starting transfers between devices, swapped(): return lax.ppermute(shard, axis, [(i, i ^ bit) for i in range(peers)])  3.83 us
    unnamed x22, local copies, waits for them, and re-layouts  3.82 us
  transfers between devices with their start and end apart: 15, of which 10 were waited for; matrix products, arithmetic and copies ran while one was open for 2% of the time, Pallas kernels for 6%

profile of v2, /device:TPU:0, one launch (start us, length us, event | category | flops | bytes accessed | tf_op | source)
XLA Modules:
  0.0 108.5 jit_solution(10986832237725787542)
XLA Ops:
  0.6 2.4 %halo_rows.1 = (bf16[32,192]{1,0:T(8,128)(2,1)}, bf16[32,192]{1,0:T(8,128)(2,1)}, bf16[32,192]{1,0:T(8,128)(2,1)}, bf16[32,192]{1,0:T(8,128)(2,1)}) custom-call(bf16[192,512]{1,0:T(8,128)(2,1)} %bitcast.45, bf16[192,704]{1,0:T(8,128)(2,1)} %bitcast.43, s32[4,32]{1,0:T(4,128)} %map_ref.5), custom_call_target="tpu_custom_call" | custom-call | tf_op jit(solution)/shard_map/halo_rows/pallas_call | solution.py:304
  3.0 5.1 %collective-permute-start = (bf16[32,192]{1,0:T(8,128)(2,1)}, bf16[32,192]{1,0:T(8,128)(2,1)S(1)}, u32[]{:S(2)}, u32[]{:S(2)}) collective-permute-start(bf16[32,192]{1,0:T(8,128)(2,1)} %get-tuple-element.15), channel_id=1, source_target_pairs={{0,6},{1,7},{2,0},{3,1},{4,2},{5,3},{6,4},{7,5},{8,14},{9,15},{10,... | collective-permute-start | bytes 36872 | tf_op jit(solution)/shard_map/ppermute | solution.py:432
  8.1 0.0 collective-permute-start.1
  8.1 0.5 collective-permute-start.2
  8.6 0.7 collective-permute-start.3
  9.9 0.0 collective-permute-done.refs_3_
  9.9 0.0 copy-start.7
  9.9 0.0 collective-permute-done.1.refs_4_
  9.9 0.0 copy-start.8
  10.0 3.3 %collective-permute-done.2.refs_5_ = bf16[32,192]{1,0:T(8,128)(2,1)S(1)} collective-permute-done((bf16[32,192]{1,0:T(8,128)(2,1)}, bf16[32,192]{1,0:T(8,128)(2,1)S(1)}, u32[]{:S(2)}, u32[]{:S(2)}) %collective-permute-start.2) | collective-permute-done | bytes 12320 | tf_op jit(solution)/shard_map/ppermute | solution.py:432
  13.3 0.0 copy-start.9
  13.3 1.1 collective-permute-done.3.refs_6_
  14.3 0.0 copy-start.10
  14.3 0.0 copy-done.7
  14.3 0.0 copy-done.8
  14.3 0.0 copy-done.9
  14.4 0.6 copy-done.10
  14.9 11.8 %elements.1 = (f32[48,2048]{1,0:T(8,128)}, f32[512,128]{1,0:T(8,128)}, f32[704,128]{1,0:T(8,128)}, f32[4,32,128]{2,1,0:T(8,128)}) custom-call(s32[1]{0:T(128)S(6)} %copy.25.refs_0_, bf16[192,512]{1,0:T(8,128)(2,1)} %bitcast.46, bf16[192,704]{1,0:T(8,128)(2,1)} %bitcast.44, bf16[32,192]{1,0:T(8,128)(2,1)} %copy-done.7, bf16[32,192]{1,0:T(8,128)(2,1)} %copy-done.8, ...), custom_call_target="tpu_custom_call" | custom-call | tf_op jit(solution)/shard_map/elements/pallas_call | solution.py:264
  26.7 0.8 slice_bitcast_fusion.4
  27.5 0.0 collective-permute-start.4
  27.6 22.9 %collective-permute-start.5 = (f32[32,128]{1,0:T(8,128)S(1)}, f32[32,128]{1,0:T(8,128)S(1)}, u32[]{:S(2)}, u32[]{:S(2)}) collective-permute-start(f32[32,128]{1,0:T(8,128)S(1)} %get-tuple-element.31), channel_id=1, source_target_pairs={{0,1},{1,2},{2,3},{3,4},{4,5},{5,6},{6,7},{7,0},{8,9},{9,10},{10,1... | collective-permute-start | bytes 49160 | tf_op jit(solution)/shard_map/ppermute | solution.py:432
  50.5 3.1 %collective-permute-start.6 = (f32[32,128]{1,0:T(8,128)S(1)}, f32[32,128]{1,0:T(8,128)S(1)}, u32[]{:S(2)}, u32[]{:S(2)}) collective-permute-start(f32[32,128]{1,0:T(8,128)S(1)} %get-tuple-element.30), channel_id=1, source_target_pairs={{0,7},{1,0},{2,1},{3,2},{4,3},{5,4},{6,5},{7,6},{8,15},{9,8},{10,9... | collective-permute-start | bytes 49160 | tf_op jit(solution)/shard_map/ppermute | solution.py:432
  53.5 0.4 collective-permute-start.7
  53.9 0.0 collective-permute-done.4.refs_0_
  53.9 0.0 copy-start.3
  53.9 1.2 %collective-permute-done.5.refs_1_ = f32[32,128]{1,0:T(8,128)S(1)} collective-permute-done((f32[32,128]{1,0:T(8,128)S(1)}, f32[32,128]{1,0:T(8,128)S(1)}, u32[]{:S(2)}, u32[]{:S(2)}) %collective-permute-start.5) | collective-permute-done | bytes 16416 | tf_op jit(solution)/shard_map/ppermute | solution.py:432
  55.1 0.0 copy-start.4
  55.1 0.0 collective-permute-done.6.refs_2_
  55.1 0.0 copy-start.5
  55.1 2.1 %collective-permute-done.7.refs_3_ = f32[32,128]{1,0:T(8,128)S(1)} collective-permute-done((f32[32,128]{1,0:T(8,128)S(1)}, f32[32,128]{1,0:T(8,128)S(1)}, u32[]{:S(2)}, u32[]{:S(2)}) %collective-permute-start.7) | collective-permute-done | bytes 16416 | tf_op jit(solution)/shard_map/ppermute | solution.py:432
  57.3 0.0 copy-start.6
  57.3 0.0 copy-done.3
  57.3 0.0 copy-done.4
  57.3 0.0 copy-done.5
  57.3 0.6 copy-done.6
  57.9 2.2 %interface_forces.1 = (f32[352,128]{1,0:T(8,128)}, f32[352,128]{1,0:T(8,128)}) custom-call(f32[704,128]{1,0:T(8,128)} %get-tuple-element.21.own_ref, s32[4,32]{1,0:T(4,128)} %map_ref.5, f32[32,128]{1,0:T(8,128)} %copy-done.3, f32[32,128]{1,0:T(8,128)} %copy-done.4, f32[32,128]{1,0:T(8,128)} %copy-done.5, f32[32,128]{1,0:T(8,128)} %copy-done.6), custom_call_target="tpu_custom_call" | custom-call | tf_op jit(solution)/shard_map/interface_forces/pallas_call | solution.py:469
  60.1 0.0 collective-permute-start.10
  60.1 0.0 collective-permute-start.8
  60.1 5.7 %collective-permute-done.10 = f32[352,128]{1,0:T(8,128)S(1)} collective-permute-done((f32[352,128]{1,0:T(8,128)}, f32[352,128]{1,0:T(8,128)S(1)}, u32[]{:S(2)}, u32[]{:S(2)}) %collective-permute-start.10) | collective-permute-done | bytes 180256 | tf_op jit(solution)/shard_map/ppermute | solution.py:427
  65.8 1.0 add.13.own_b
  66.8 0.1 collective-permute-start.11
  66.8 0.0 collective-permute-done.8
  66.9 1.0 add.12.own_a
  67.8 2.6 %collective-permute-start.9 = (f32[352,128]{1,0:T(8,128)S(1)}, f32[352,128]{1,0:T(8,128)S(1)}, u32[]{:S(2)}, u32[]{:S(2)}) collective-permute-start(f32[352,128]{1,0:T(8,128)S(1)} %add.12.own_a), channel_id=1, source_target_pairs={{0,16},{8,24},{16,0},{24,8},{1,17},{9,25},{17,1},{25,9},{2,18},{10... | collective-permute-start | bytes 540680 | tf_op jit(solution)/shard_map/ppermute | solution.py:427
  70.4 1.9 %collective-permute-done.11.got_b = f32[352,128]{1,0:T(8,128)S(1)} collective-permute-done((f32[352,128]{1,0:T(8,128)S(1)}, f32[352,128]{1,0:T(8,128)S(1)}, u32[]{:S(2)}, u32[]{:S(2)}) %collective-permute-start.11) | collective-permute-done | bytes 180256 | tf_op jit(solution)/shard_map/ppermute | solution.py:427
  72.3 1.5 %collective-permute-done.9.got_a = f32[352,128]{1,0:T(8,128)S(1)} collective-permute-done((f32[352,128]{1,0:T(8,128)S(1)}, f32[352,128]{1,0:T(8,128)S(1)}, u32[]{:S(2)}, u32[]{:S(2)}) %collective-permute-start.9) | collective-permute-done | bytes 180256 | tf_op jit(solution)/shard_map/ppermute | solution.py:427
  73.9 0.0 copy-start
  73.9 1.1 copy-done
  74.9 0.0 copy-start.1
  74.9 0.9 copy-done.1
  75.8 10.3 %interface_solve.1 = (f32[4,264,128]{2,1,0:T(8,128)S(1)}, f32[4,264,128]{2,1,0:T(8,128)S(1)}) custom-call(s32[1]{0:T(128)} %bitcast.13.me_ref, f32[192,704]{1,0:T(8,128)S(1)} %bitcast.39, f32[352,128]{1,0:T(8,128)S(1)} %add.12.own_a, f32[352,128]{1,0:T(8,128)S(1)} %collective-permute-done.9.got_a, f32[352,128]{1,0:T(8,128)S(1)} %add.13.own_b, ...), custom_call_target="tpu_custom_call" | custom-call | tf_op jit(solution)/shard_map/interface_solve/pallas_call | solution.py:398
  86.1 0.1 collective-permute-start.12
  86.2 1.9 %collective-permute-done.12 = f32[4,264,128]{2,1,0:T(8,128)S(1)} collective-permute-done((f32[4,264,128]{2,1,0:T(8,128)S(1)}, f32[4,264,128]{2,1,0:T(8,128)S(1)}, u32[]{:S(2)}, u32[]{:S(2)}) %collective-permute-start.12) | collective-permute-done | bytes 540704 | tf_op jit(solution)/shard_map/ppermute | solution.py:427
  88.1 0.1 add.14
  88.2 0.1 collective-permute-start.13
  88.3 8.5 %collective-permute-done.13 = f32[2,264,128]{2,1,0:T(8,128)S(1)} collective-permute-done((f32[2,264,128]{2,1,0:T(8,128)S(1)}, f32[2,264,128]{2,1,0:T(8,128)S(1)}, u32[]{:S(2)}, u32[]{:S(2)}) %collective-permute-start.13) | collective-permute-done | bytes 270368 | tf_op jit(solution)/shard_map/ppermute | solution.py:427
  96.8 0.7 slice_bitcast_fusion.2
  97.5 1.0 collective-permute-start.14
  98.5 6.8 %interior_solve.1 = f32[192,512]{1,0:T(8,128)} custom-call(f32[512,128]{1,0:T(8,128)} %get-tuple-element.19.own_ref, s32[4,32]{1,0:T(4,128)} %map_ref.5, f32[32,128]{1,0:T(8,128)} %copy-done.3, f32[32,128]{1,0:T(8,128)} %copy-done.4, f32[32,128]{1,0:T(8,128)} %copy-done.5, f32[32,128]{1,0:T(8,128)} %copy-done.6, f32[192,512]{1,0:T(8,128)} %bitcast.47, ...), custom_call_target="tpu_custom_call" | custom-call | flops 301989888 | bytes 4718592 | tf_op jit(solution)/shard_map/interior_solve/pallas_call | solution.py:482
  105.3 0.7 collective-permute-done.14.got_ref
  106.1 0.0 copy-start.2
  106.1 0.6 copy-done.2
  106.7 1.8 %interface_result.1 = f32[176,192]{1,0:T(8,128)} custom-call(f32[1,264,128]{2,1,0:T(8,128)} %get-tuple-element.28.mine_ref, f32[1,264,128]{2,1,0:T(8,128)} %copy-done.2), custom_call_target="tpu_custom_call" | custom-call | tf_op jit(solution)/shard_map/interface_result/pallas_call | solution.py:504
  (2 shorter events, 0.1 us)
Async XLA Ops:
  3.0 6.9 %collective-permute-start = (bf16[32,192]{1,0:T(8,128)(2,1)}, bf16[32,192]{1,0:T(8,128)(2,1)S(1)}, u32[]{:S(2)}, u32[]{:S(2)}) collective-permute-start(bf16[32,192]{1,0:T(8,128)(2,1)} %get-tuple-element.15), channel_id=1, source_target_pairs={{0,6},{1,7},{2,0},{3,1},{4,2},{5,3},{6,4},{7,5},{8,14},{9,15},{10,... | collective-permute-start | bytes 36872 | tf_op jit(solution)/shard_map/ppermute | solution.py:432
  8.1 1.9 %collective-permute-start.1 = (bf16[32,192]{1,0:T(8,128)(2,1)}, bf16[32,192]{1,0:T(8,128)(2,1)S(1)}, u32[]{:S(2)}, u32[]{:S(2)}) collective-permute-start(bf16[32,192]{1,0:T(8,128)(2,1)} %get-tuple-element.16), channel_id=1, source_target_pairs={{0,7},{1,0},{2,1},{3,2},{4,3},{5,4},{6,5},{7,6},{8,15},{9,8},{10,9... | collective-permute-start | bytes 36872 | tf_op jit(solution)/shard_map/ppermute | solution.py:432
  8.1 5.2 %collective-permute-start.2 = (bf16[32,192]{1,0:T(8,128)(2,1)}, bf16[32,192]{1,0:T(8,128)(2,1)S(1)}, u32[]{:S(2)}, u32[]{:S(2)}) collective-permute-start(bf16[32,192]{1,0:T(8,128)(2,1)} %get-tuple-element.17), channel_id=1, source_target_pairs={{0,1},{1,2},{2,3},{3,4},{4,5},{5,6},{6,7},{7,0},{8,9},{9,10},{10,1... | collective-permute-start | bytes 36872 | tf_op jit(solution)/shard_map/ppermute | solution.py:432
  8.6 5.7 %collective-permute-start.3 = (bf16[32,192]{1,0:T(8,128)(2,1)}, bf16[32,192]{1,0:T(8,128)(2,1)S(1)}, u32[]{:S(2)}, u32[]{:S(2)}) collective-permute-start(bf16[32,192]{1,0:T(8,128)(2,1)} %get-tuple-element.18), channel_id=1, source_target_pairs={{0,2},{1,3},{2,4},{3,5},{4,6},{5,7},{6,0},{7,1},{8,10},{9,11},{10,... | collective-permute-start | bytes 36872 | tf_op jit(solution)/shard_map/ppermute | solution.py:432
  9.9 4.4 %copy-start.7 = (bf16[32,192]{1,0:T(8,128)(2,1)}, bf16[32,192]{1,0:T(8,128)(2,1)S(1)}, u32[]{:S(2)}) copy-start(bf16[32,192]{1,0:T(8,128)(2,1)S(1)} %collective-permute-done.refs_3_) | copy-start | bytes 36868
  9.9 4.4 %copy-start.8 = (bf16[32,192]{1,0:T(8,128)(2,1)}, bf16[32,192]{1,0:T(8,128)(2,1)S(1)}, u32[]{:S(2)}) copy-start(bf16[32,192]{1,0:T(8,128)(2,1)S(1)} %collective-permute-done.1.refs_4_) | copy-start | bytes 36868
  13.3 1.1 %copy-start.9 = (bf16[32,192]{1,0:T(8,128)(2,1)}, bf16[32,192]{1,0:T(8,128)(2,1)S(1)}, u32[]{:S(2)}) copy-start(bf16[32,192]{1,0:T(8,128)(2,1)S(1)} %collective-permute-done.2.refs_5_) | copy-start | bytes 36868
  14.3 0.6 copy-start.10
  27.5 26.4 %collective-permute-start.4 = (f32[32,128]{1,0:T(8,128)S(1)}, f32[32,128]{1,0:T(8,128)S(1)}, u32[]{:S(2)}, u32[]{:S(2)}) collective-permute-start(f32[32,128]{1,0:T(8,128)S(1)} %get-tuple-element.32), channel_id=1, source_target_pairs={{0,2},{1,3},{2,4},{3,5},{4,6},{5,7},{6,0},{7,1},{8,10},{9,11},{10,... | collective-permute-start | bytes 49160 | tf_op jit(solution)/shard_map/ppermute | solution.py:432
  27.6 27.6 %collective-permute-start.5 = (f32[32,128]{1,0:T(8,128)S(1)}, f32[32,128]{1,0:T(8,128)S(1)}, u32[]{:S(2)}, u32[]{:S(2)}) collective-permute-start(f32[32,128]{1,0:T(8,128)S(1)} %get-tuple-element.31), channel_id=1, source_target_pairs={{0,1},{1,2},{2,3},{3,4},{4,5},{5,6},{6,7},{7,0},{8,9},{9,10},{10,1... | collective-permute-start | bytes 49160 | tf_op jit(solution)/shard_map/ppermute | solution.py:432
  50.5 4.7 %collective-permute-start.6 = (f32[32,128]{1,0:T(8,128)S(1)}, f32[32,128]{1,0:T(8,128)S(1)}, u32[]{:S(2)}, u32[]{:S(2)}) collective-permute-start(f32[32,128]{1,0:T(8,128)S(1)} %get-tuple-element.30), channel_id=1, source_target_pairs={{0,7},{1,0},{2,1},{3,2},{4,3},{5,4},{6,5},{7,6},{8,15},{9,8},{10,9... | collective-permute-start | bytes 49160 | tf_op jit(solution)/shard_map/ppermute | solution.py:432
  53.5 3.7 %collective-permute-start.7 = (f32[32,128]{1,0:T(8,128)S(1)}, f32[32,128]{1,0:T(8,128)S(1)}, u32[]{:S(2)}, u32[]{:S(2)}) collective-permute-start(f32[32,128]{1,0:T(8,128)S(1)} %get-tuple-element.29), channel_id=1, source_target_pairs={{0,6},{1,7},{2,0},{3,1},{4,2},{5,3},{6,4},{7,5},{8,14},{9,15},{10,... | collective-permute-start | bytes 49160 | tf_op jit(solution)/shard_map/ppermute | solution.py:432
  53.9 3.3 %copy-start.3 = (f32[32,128]{1,0:T(8,128)}, f32[32,128]{1,0:T(8,128)S(1)}, u32[]{:S(2)}) copy-start(f32[32,128]{1,0:T(8,128)S(1)} %collective-permute-done.4.refs_0_) | copy-start | bytes 49156
  55.1 2.2 %copy-start.4 = (f32[32,128]{1,0:T(8,128)}, f32[32,128]{1,0:T(8,128)S(1)}, u32[]{:S(2)}) copy-start(f32[32,128]{1,0:T(8,128)S(1)} %collective-permute-done.5.refs_1_) | copy-start | bytes 49156
  55.1 2.2 %copy-start.5 = (f32[32,128]{1,0:T(8,128)}, f32[32,128]{1,0:T(8,128)S(1)}, u32[]{:S(2)}) copy-start(f32[32,128]{1,0:T(8,128)S(1)} %collective-permute-done.6.refs_2_) | copy-start | bytes 49156
  57.3 0.6 copy-start.6
  60.1 5.7 %collective-permute-start.10 = (f32[352,128]{1,0:T(8,128)}, f32[352,128]{1,0:T(8,128)S(1)}, u32[]{:S(2)}, u32[]{:S(2)}) collective-permute-start(f32[352,128]{1,0:T(8,128)} %get-tuple-element.23), channel_id=1, source_target_pairs={{0,16},{8,24},{16,0},{24,8},{1,17},{9,25},{17,1},{25,9},{2,18},{10... | collective-permute-start | bytes 540680 | tf_op jit(solution)/shard_map/ppermute | solution.py:427
  60.1 6.7 %collective-permute-start.8 = (f32[352,128]{1,0:T(8,128)}, f32[352,128]{1,0:T(8,128)S(1)}, u32[]{:S(2)}, u32[]{:S(2)}) collective-permute-start(f32[352,128]{1,0:T(8,128)} %get-tuple-element.22), channel_id=1, source_target_pairs={{0,8},{8,0},{16,24},{24,16},{1,9},{9,1},{17,25},{25,17},{2,10},{10... | collective-permute-start | bytes 540680 | tf_op jit(solution)/shard_map/ppermute | solution.py:427
  66.8 5.6 %collective-permute-start.11 = (f32[352,128]{1,0:T(8,128)S(1)}, f32[352,128]{1,0:T(8,128)S(1)}, u32[]{:S(2)}, u32[]{:S(2)}) collective-permute-start(f32[352,128]{1,0:T(8,128)S(1)} %add.13.own_b), channel_id=1, source_target_pairs={{0,8},{8,0},{16,24},{24,16},{1,9},{9,1},{17,25},{25,17},{2,10},{10... | collective-permute-start | bytes 540680 | tf_op jit(solution)/shard_map/ppermute | solution.py:427
  67.8 6.1 %collective-permute-start.9 = (f32[352,128]{1,0:T(8,128)S(1)}, f32[352,128]{1,0:T(8,128)S(1)}, u32[]{:S(2)}, u32[]{:S(2)}) collective-permute-start(f32[352,128]{1,0:T(8,128)S(1)} %add.12.own_a), channel_id=1, source_target_pairs={{0,16},{8,24},{16,0},{24,8},{1,17},{9,25},{17,1},{25,9},{2,18},{10... | collective-permute-start | bytes 540680 | tf_op jit(solution)/shard_map/ppermute | solution.py:427
  73.9 1.1 copy-start
  74.9 0.9 copy-start.1
  86.1 2.0 %collective-permute-start.12 = (f32[4,264,128]{2,1,0:T(8,128)S(1)}, f32[4,264,128]{2,1,0:T(8,128)S(1)}, u32[]{:S(2)}, u32[]{:S(2)}) collective-permute-start(f32[4,264,128]{2,1,0:T(8,128)S(1)} %get-tuple-element.25), channel_id=1, source_target_pairs={{0,1},{1,0},{2,3},{3,2},{4,5},{5,4},{6,7},{7,6},{8,9},{9,8},{10,11... | collective-permute-start | bytes 1622024 | tf_op jit(solution)/shard_map/ppermute | solution.py:427
  88.2 8.6 %collective-permute-start.13 = (f32[2,264,128]{2,1,0:T(8,128)S(1)}, f32[2,264,128]{2,1,0:T(8,128)S(1)}, u32[]{:S(2)}, u32[]{:S(2)}) collective-permute-start(f32[2,264,128]{2,1,0:T(8,128)S(1)} %slice_bitcast_fusion), channel_id=1, source_target_pairs={{0,2},{1,3},{2,0},{3,1},{4,6},{5,7},{6,4},{7,5},{8,10},{9,11},{10,... | collective-permute-start | bytes 811016 | tf_op jit(solution)/shard_map/ppermute | solution.py:427
  97.5 8.6 %collective-permute-start.14 = (f32[1,264,128]{2,1,0:T(8,128)S(1)}, f32[1,264,128]{2,1,0:T(8,128)S(1)}, u32[]{:S(2)}, u32[]{:S(2)}) collective-permute-start(f32[1,264,128]{2,1,0:T(8,128)S(1)} %get-tuple-element.27), channel_id=1, source_target_pairs={{0,4},{1,5},{2,6},{3,7},{4,0},{5,1},{6,2},{7,3},{8,12},{9,13},{10,... | collective-permute-start | bytes 405512 | tf_op jit(solution)/shard_map/ppermute | solution.py:427
  106.1 0.7 copy-start.2

commit v3 on v2

--- a/solution.py
+++ b/solution.py
@@ -20,6 +20,14 @@
 SLOT = 16
 ROWS = GROUPS * SLOT
 NT = (((1,), (1,)), ((), ()))
+
+
+def lasts(microseconds):
+    return pl.CostEstimate(flops=0, bytes_accessed=int(3e6 * microseconds), transcendentals=0)
+
+
+LIMIT = 38
+SMALL = pltpu.CompilerParams(vmem_limit_bytes=12 << 20)
 BF16 = jnp.bfloat16
 F32 = jnp.float32
 
@@ -96,19 +104,33 @@
     return -(-n // to) * to
 
 
-def element_kernel(*refs, neighbours, chunk, own, half):
-    count_ref, int_ref, if_ref = refs[:3]
-    halo_refs = refs[3 : 3 + neighbours]
-    conn_ref, size_ref, stiff_ref, yield_ref, rate_ref, init_ref = refs[3 + neighbours : 9 + neighbours]
-    high_ref, low_ref, strain_ref, force_ref = refs[9 + neighbours : 13 + neighbours]
-    end_ref, pint_ref, pif_ref, back_ref = refs[13 + neighbours : 17 + neighbours]
-    nodes, onehot, corners, forces, state, total = refs[17 + neighbours :]
+def element_kernel(*refs, neighbours, chunk, own, half, kept):
+    refs = list(refs)
+
+    def take(n):
+        taken, refs[:n] = refs[:n], []
+        return taken
+
+    count_ref, int_ref, if_ref = take(3)
+    halo_refs = take(neighbours)
+    conn_ref, size_ref, stiff_ref, yield_ref, rate_ref, init_ref = take(6)
+    high_ref, low_ref, strain_ref, force_ref = take(4)
+    far_refs = take(kept)
+    end_ref, pint_ref, pif_ref = take(3)
+    back_refs = take(neighbours)
+    near_refs = take(kept)
+    nodes, onehot, corners, forces, state, total, arrived = refs
+    fetches = [
+        pltpu.make_async_copy(far, near, arrived.at[k]) for k, (far, near) in enumerate(zip(far_refs, near_refs))
+    ]
+    for fetch in fetches:
+        fetch.start()
     n_int, n_if, slots = int_ref.shape[1], if_ref.shape[1], halo_refs[0].shape[0]
     halo_at = up(own, 128)
     both = 2 * GROUPS * PART
     chunks = end_ref.shape[1] // chunk
     count = count_ref[0]
-    used = lax.div(count + chunk - 1, chunk)
+    used = jnp.maximum(lax.div(count + chunk - 1, chunk), 1)
 
     nodes[...] = jnp.zeros_like(nodes)
     total[...] = jnp.zeros_like(total)
@@ -244,15 +266,17 @@
 
     pint_ref[...] = result(0, n_int)
     pif_ref[...] = result(n_int, n_if)
-    for slot_index in range(neighbours):
-        back_ref[slot_index] = result(halo_at + slot_index * slots, slots)
+    for slot_index, back_ref in enumerate(back_refs):
+        back_ref[...] = result(halo_at + slot_index * slots, slots)
+    for fetch in fetches:
+        fetch.wait()
 
 
 def whole(shape):
     return pl.BlockSpec(shape, lambda *_: (0,) * len(shape))
 
 
-def element_phase(count, u_int, u_if, halos, conn, params, stress_init, tables, interpret=False):
+def element_phase(count, u_int, u_if, halos, conn, params, stress_init, tables, later=(), interpret=False):
     chunk = 256
     n_int, n_if = u_int.shape[1], u_if.shape[1]
     own = n_int + n_if
@@ -262,9 +286,10 @@
     vmem = pl.BlockSpec(memory_space=pltpu.VMEM)
     inputs = [u_int, u_if, *halos, conn, *params, stress_init, *tables[:4]]
     return pl.pallas_call(
-        functools.partial(element_kernel, neighbours=neighbours, chunk=chunk, own=own, half=half),
-        in_specs=[pl.BlockSpec(memory_space=pltpu.SMEM)] + [vmem] * len(inputs),
-        out_specs=[vmem] * 4,
+        functools.partial(element_kernel, neighbours=neighbours, chunk=chunk, own=own, half=half, kept=len(later)),
+        in_specs=[pl.BlockSpec(memory_space=pltpu.SMEM)] + [vmem] * len(inputs)
+        + [pl.BlockSpec(memory_space=pl.ANY)] * len(later),
+        out_specs=[vmem] * (3 + neighbours + len(later)),
         scratch_shapes=[
             pltpu.VMEM((4 * GROUPS * PART, half), BF16),
             pltpu.VMEM((3, 8, half, chunk), BF16),
@@ -272,17 +297,20 @@
             pltpu.VMEM((2, 8, ROWS, chunk), BF16),
             pltpu.VMEM((stress_init.shape[0], chunk), F32),
             pltpu.VMEM((half, 2 * ROWS), F32),
+            pltpu.SemaphoreType.DMA((max(len(later), 1),)),
         ],
         out_shape=[
             jax.ShapeDtypeStruct(stress_init.shape, F32),
-            jax.ShapeDtypeStruct((n_int, ROWS), F32),
-            jax.ShapeDtypeStruct((n_if, ROWS), F32),
-            jax.ShapeDtypeStruct((neighbours, slots, ROWS), F32),
-        ],
-        compiler_params=pltpu.CompilerParams(vmem_limit_bytes=60 << 20),
+            pltpu.VMEM((n_int, ROWS), F32),
+            pltpu.VMEM((n_if, ROWS), F32),
+        ]
+        + [pltpu.VMEM((slots, ROWS), F32)] * neighbours
+        + [pltpu.VMEM(x.shape, x.dtype) for x in later],
+        compiler_params=pltpu.CompilerParams(vmem_limit_bytes=LIMIT << 20),
+        cost_estimate=lasts(40),
         name="elements",
         interpret=interpret,
-    )(count, *inputs)
+    )(count, *inputs, *later)
 
 
 def send_kernel(int_ref, if_ref, map_ref, *out_refs):
@@ -304,7 +332,7 @@
     return pl.pallas_call(
         send_kernel,
         out_shape=[jax.ShapeDtypeStruct((slots, u_int.shape[0]), BF16)] * neighbours,
-        name="halo_rows",
+        compiler_params=pltpu.CompilerParams(vmem_limit_bytes=60 << 20), cost_estimate=lasts(3), name="halo_rows",
     )(u_int, u_if, send_map)
 
 
@@ -323,11 +351,24 @@
 
 
 def interface_kernel(own_ref, map_ref, *refs, first):
-    returned, (a_ref, b_ref) = refs[:-2], refs[-2:]
+    returned, outs = refs[:-4], refs[-4:]
     value = added_back(own_ref[...], map_ref, returned, first)
-    half = a_ref.shape[0]
-    a_ref[...] = value[:half]
-    b_ref[...] = value[half:]
+    half = outs[0].shape[0]
+    for part, rows in enumerate((value[:half], value[half:])):
+        outs[part][...] = rows
+        outs[2 + part][...] = rows.astype(BF16)
+
+
+def join_kernel(own_a, got_a, own_b, got_b, a_ref, b_ref, sent_a, sent_b):
+    for own, got, ref, sent in ((own_a, got_a, a_ref, sent_a), (own_b, got_b, b_ref, sent_b)):
+        value = own[...] + got[...].astype(F32)
+        ref[...] = value
+        sent[...] = value.astype(BF16)
+
+
+def halves(n_rows):
+    sizes = (n_rows // 2, n_rows - n_rows // 2)
+    return [jax.ShapeDtypeStruct((size, ROWS), kind) for kind in (F32, BF16) for size in sizes]
 
 
 def interleaved(value, scratch):
@@ -344,80 +385,90 @@
     return jnp.concatenate([scratch[pl.ds(comp, nodes, stride=3), :] for comp in range(3)], axis=1)
 
 
-def interior_kernel(own_ref, map_ref, *refs):
-    returned = refs[:-5]
-    load_ref, anal_ref, kinv_ref, du_ref, scratch = refs[-5:]
+def interior_rhs_kernel(own_ref, map_ref, *refs):
+    returned = refs[:-4]
+    load_ref, anal_ref, rhs_ref, scratch = refs[-4:]
     value = added_back(own_ref[...], map_ref, returned, 0)
     force = jnp.dot(value, anal_ref[...], precision=HIGHEST, preferred_element_type=F32)
-    rhs = interleaved(load_ref[...].T - force, scratch).astype(BF16)
-    du = jnp.dot(kinv_ref[...], rhs, preferred_element_type=F32)
+    rhs_ref[...] = interleaved(load_ref[...].T - force, scratch).astype(BF16)
+
+
+def interior_kernel(rhs_ref, kinv_ref, du_ref, scratch):
+    du = jnp.dot(kinv_ref[...], rhs_ref[...], preferred_element_type=F32)
     du_ref[...] = separated(du, scratch).T
 
 
-def solve_kernel(me_ref, load_ref, own_a, got_a, own_b, got_b, anal_ref, sinv_ref, *refs, peers):
-    away_ref, near_ref, rhs, scratch, total, rows = refs
-    index = pl.program_id(0)
-
-    @pl.when(index == 0)
-    def _():
-        value = jnp.concatenate([own_a[...] + got_a[...], own_b[...] + got_b[...]], axis=0)
-        force = jnp.dot(value, anal_ref[...], precision=HIGHEST, preferred_element_type=F32)
-        right = interleaved(load_ref[...].T - force, scratch).T.astype(BF16)
-        depth = rhs.shape[2]
-        for block in range(rhs.shape[0]):
-            rhs[block] = right[:, block * depth : (block + 1) * depth]
-
-    term = jnp.dot(rhs[index], sinv_ref[...], preferred_element_type=F32)
-
-    @pl.when(index == 0)
-    def _():
-        total[...] = term
-
-    @pl.when(index > 0)
-    def _():
-        total[...] += term
-
-    @pl.when(index == pl.num_programs(0) - 1)
-    def _():
-        rows[...] = total[...].T
-        count = rows.shape[0] // peers
-        for j in range(peers):
-            at = (me_ref[0] ^ j) * count
-            upper, lower = rows[pl.ds(at, count // 2), :], rows[pl.ds(at + count // 2, count // 2), :]
-            out_ref = away_ref if j & 1 else near_ref
-            out_ref[j // 2] = jnp.concatenate([upper, lower], axis=1).astype(out_ref.dtype)
-
-
-def interface_solve(me, load, own_a, got_a, own_b, got_b, analysis, sinv, peers, dtype):
-    depth_all, rows = sinv.shape
+def solve_kernel(load_ref, own_a, got_a, own_b, got_b, anal_ref, sinv_ref, *refs, peers):
+    away_ref, near_ref, scratch, total, rows = refs
+    depth_all = sinv_ref.shape[0]
     blocks = next(b for b in (4, 3, 2, 1) if b == 1 or depth_all % (b * 16) == 0)
     depth = depth_all // blocks
+    value = jnp.concatenate([own_a[...] + got_a[...].astype(F32), own_b[...] + got_b[...].astype(F32)], axis=0)
+    force = jnp.dot(value, anal_ref[...], precision=HIGHEST, preferred_element_type=F32)
+    right = interleaved(load_ref[...].T - force, scratch).T.astype(BF16)
+    for k in range(blocks):
+        part = slice(k * depth, (k + 1) * depth)
+        term = jnp.dot(right[:, part], sinv_ref[part, :], preferred_element_type=F32)
+        total[...] = term if k == 0 else total[...] + term
+    rows[...] = total[...].T
+    count = rows.shape[0] // peers
+    me = lax.axis_index("dom")
+    for j in range(peers):
+        at = (me ^ j) * count
+        upper, lower = rows[pl.ds(at, count // 2), :], rows[pl.ds(at + count // 2, count // 2), :]
+        out_ref = away_ref if j & 1 else near_ref
+        out_ref[j // 2] = jnp.concatenate([upper, lower], axis=1).astype(out_ref.dtype)
+
+
+def interface_solve(load, own_a, got_a, own_b, got_b, analysis, sinv, peers):
+    depth, rows = sinv.shape
     fourier = load.shape[0] // 3
     shape = (peers // 2, rows // peers // 2, 2 * fourier)
+    vmem = pl.BlockSpec(memory_space=pltpu.VMEM)
     small = [load, own_a, got_a, own_b, got_b, analysis]
     return pl.pallas_call(
         functools.partial(solve_kernel, peers=peers),
-        grid_spec=pltpu.PrefetchScalarGridSpec(
-            num_scalar_prefetch=1,
-            grid=(blocks,),
-            in_specs=[whole(x.shape) for x in small] + [pl.BlockSpec((depth, rows), lambda k, me: (k, 0))],
-            out_specs=[whole(shape)] * 2,
-            scratch_shapes=[
-                pltpu.VMEM((blocks, fourier, depth), BF16),
-                pltpu.VMEM((depth_all, fourier), F32),
-                pltpu.VMEM((fourier, rows), F32),
-                pltpu.VMEM((rows, fourier), F32),
-            ],
-        ),
-        out_shape=[jax.ShapeDtypeStruct(shape, dtype), jax.ShapeDtypeStruct(shape, F32)],
-        compiler_params=pltpu.CompilerParams(vmem_limit_bytes=40 << 20),
+        in_specs=[vmem] * (len(small) + 1),
+        out_specs=[vmem] * 2,
+        scratch_shapes=[
+            pltpu.VMEM((depth, fourier), F32),
+            pltpu.VMEM((fourier, rows), F32),
+            pltpu.VMEM((rows, fourier), F32),
+        ],
+        out_shape=[jax.ShapeDtypeStruct(shape, BF16), jax.ShapeDtypeStruct(shape, F32)],
+        compiler_params=pltpu.CompilerParams(vmem_limit_bytes=12 << 20),
+        cost_estimate=lasts(10),
         name="interface_solve",
-    )(me, *small, sinv)
-
-
-def last_kernel(mine_ref, got_ref, out_ref, scratch):
-    value = mine_ref[0] + got_ref[0].astype(F32)
-    half = value.shape[0]
+    )(*small, sinv)
+
+
+def split_kernel(mine_ref, got_ref, *outs):
+    keep_ref, sent = outs[0], outs[1:]
+    for j in range(mine_ref.shape[0]):
+        value = mine_ref[j] + got_ref[j].astype(F32)
+        if len(sent) == 1:
+            ref = sent[0] if j & 1 else keep_ref
+            ref[j // 2] = value.astype(ref.dtype)
+        elif j == 0:
+            keep_ref[...] = value
+        else:
+            sent[j - 1][...] = value.astype(BF16)
+
+
+def split(mine, got, apart):
+    count, shape = mine.shape[0], mine.shape[1:]
+    if apart:
+        outs = [jax.ShapeDtypeStruct(shape, F32)] + [jax.ShapeDtypeStruct(shape, BF16)] * (count - 1)
+    else:
+        outs = [jax.ShapeDtypeStruct((count // 2, *shape), kind) for kind in (F32, BF16)]
+    return pl.pallas_call(split_kernel, out_shape=outs, compiler_params=SMALL, cost_estimate=lasts(4), name="correction_sums")(mine, got)
+
+
+def last_kernel(mine_ref, *refs):
+    got_refs, (out_ref, scratch) = refs[:-2], refs[-2:]
+    value = mine_ref[...]
+    for ref in got_refs:
+        value = value + ref[...].astype(F32)
     fourier = value.shape[1] // 2
     out_ref[...] = separated(jnp.concatenate([value[:, :fourier], value[:, fourier:]], axis=0), scratch)
 
@@ -460,53 +511,62 @@
     blocks = send_blocks(u_int.T, u_if.T, send_map)
     halos = [passed_along(blocks[j], "dom", offsets[j]) for j in range(neighbours)]
     params = [x.reshape(1, -1) for x in (elem_size, stiffness, yield_stress, relax_rate)]
-    stress_end, p_int, p_if, back = element_phase(
-        counts, u_int.T, u_if.T, halos, conn.T, params, stress_init, tables
+    later = (sinv.T, kinv_int, load_int.T, load_if.T, analysis, send_map)
+    stress_end, p_int, p_if, *more = element_phase(
+        counts, u_int.T, u_if.T, halos, conn.T, params, stress_init, tables, later
+    )
+    back = more[:neighbours]
+    sinv_t, kinv, load_int_t, load_if_t, analysis, near_map = (
+        pltpu.with_memory_space_constraint(x, pltpu.VMEM) for x in more[neighbours:]
     )
     returned = [passed_along(back[j], "dom", -offsets[j]) for j in range(neighbours)]
 
-    half = n_if // 2
-    part_a, part_b = pl.pallas_call(
-        functools.partial(interface_kernel, first=n_int),
-        out_shape=[jax.ShapeDtypeStruct((half, ROWS), F32), jax.ShapeDtypeStruct((n_if - half, ROWS), F32)],
-        name="interface_forces",
-    )(p_if, send_map, *returned)
+    part_a, part_b, sent_a, sent_b = pl.pallas_call(
+        functools.partial(interface_kernel, first=n_int), out_shape=halves(n_if), compiler_params=SMALL, cost_estimate=lasts(4), name="interface_forces"
+    )(p_if, near_map, *returned)
+
+    rhs_int = pl.pallas_call(
+        interior_rhs_kernel,
+        out_shape=jax.ShapeDtypeStruct((3 * n_int, fourier), BF16),
+        scratch_shapes=[pltpu.VMEM((3 * n_int, fourier), F32)],
+        compiler_params=SMALL, cost_estimate=lasts(12), name="interior_rhs",
+    )(p_int, near_map, *returned, load_int_t, analysis)
 
     bits = [1 << b for b in range(lax.axis_size("grp").bit_length() - 1)]
-    got_a = got_b = None
-    for bit_a, bit_b in zip(bits, bits[::-1]):
-        if got_a is not None:
-            part_a, part_b = part_a + got_a, part_b + got_b
-        got_a, got_b = swapped(part_a, "grp", bit_a), swapped(part_b, "grp", bit_b)
+    for turn, (bit_a, bit_b) in enumerate(zip(bits, bits[::-1])):
+        if turn:
+            part_a, part_b, sent_a, sent_b = pl.pallas_call(
+                join_kernel, out_shape=halves(n_if), compiler_params=SMALL, cost_estimate=lasts(5), name="interface_sums"
+            )(part_a, got_a, part_b, got_b)
+            sent_a, sent_b, rhs_int = lax.optimization_barrier((sent_a, sent_b, rhs_int))
+        got_a, got_b = swapped(sent_a, "grp", bit_a), swapped(sent_b, "grp", bit_b)
 
     du_int = pl.pallas_call(
         interior_kernel,
         out_shape=jax.ShapeDtypeStruct((width, n_int), F32),
         scratch_shapes=[pltpu.VMEM((3 * n_int, fourier), F32)],
-        cost_estimate=pl.CostEstimate(
-            flops=2 * kinv_int.size * fourier, bytes_accessed=2 * kinv_int.size, transcendentals=0
-        ),
-        name="interior_solve",
-    )(p_int, send_map, *returned, load_int.T, analysis, kinv_int).T
+        compiler_params=SMALL, cost_estimate=lasts(6), name="interior_solve",
+    )(rhs_int, kinv).T
 
     peers = lax.axis_size("dom")
-    me = lax.axis_index("dom").astype(jnp.int32).reshape(1)
-    levels = peers.bit_length() - 1
-    sent, mine = interface_solve(
-        me, load_if.T, part_a, got_a, part_b, got_b, analysis, sinv.T, peers, F32
-    )
-    got = swapped(sent, "dom", 1)
-    for level in range(1, levels):
-        both = (mine + got).reshape(peers >> (level + 1), 2, *mine.shape[1:])
-        mine = both[:, 0]
-        got = swapped(both[:, 1], "dom", 1 << level)
+    sent, mine = interface_solve(load_if_t, part_a, got_a, part_b, got_b, analysis, sinv_t, peers)
+    bit = 1
+    while True:
+        got = swapped(sent, "dom", bit)
+        apart = mine.shape[0] <= 4
+        mine, *sent = split(mine, got, apart)
+        bit *= 2
+        if apart:
+            break
+        sent = sent[0]
+    got = [swapped(block, "dom", bit * (j + 1)) for j, block in enumerate(sent)]
     rows = sinv.shape[0] // peers
     du_if = pl.pallas_call(
         last_kernel,
         out_shape=jax.ShapeDtypeStruct((rows // 3, width), F32),
         scratch_shapes=[pltpu.VMEM((rows, fourier), F32)],
-        name="interface_result",
-    )(mine, got)
+        compiler_params=SMALL, cost_estimate=lasts(2), name="interface_result",
+    )(mine, *got)
     return (du_int, du_if, stress_end)
 
 

time: 107 us -> 87.8 us (0.82)
  waiting for transfers between devices: 28.1 us -> 18 us
  Pallas kernels: 35.3 us -> 25.2 us
  starting transfers between devices: 36.5 us -> 43.1 us
  local copies, waits for them, and re-layouts: 5.29 us -> 0.6 us
  other arithmetic: 2 us -> 0 us
    ppermute x7 -> x8, starting transfers between devices: 3.83 us -> 13.4 us  [swapped(): return lax.ppermute(shard, axis, [(i, i ^ bit) for i in range(peers)])]
    ppermute x7 -> x8, waiting for transfers between devices: 20.3 us -> 12.1 us  [swapped(): return lax.ppermute(shard, axis, [(i, i ^ bit) for i in range(peers)])]
    pallas_call x1, Pallas kernels: 6.81 us -> 2.37 us  [per_device(): pl.pallas_call(interior_kernel, out_shape=jax.ShapeDtypeStruct((width, n_...]
    unnamed x22 -> x8, local copies, waits for them, and re-layouts: 3.82 us -> 0.6 us
    ppermute x8, starting transfers between devices: 32.7 us -> 29.8 us  [passed_along(): lax.ppermute(shard, axis, [(i, (i + by) % peers) for i in range(peers)])]
    pallas_call x1 -> x4, Pallas kernels: 10.3 us -> 7.42 us  [the longest x1 5.78 us: interface_solve(): pl.pallas_call(functools.partial(solve_kernel, peers=peers), in_specs=[vm...]
    add x3 -> x0, other arithmetic: 1.96 us -> none  [the longest x2 1.9 us: per_device(): part_a, part_b = (part_a + got_a, part_b + got_b)]
    ppermute x8, waiting for transfers between devices: 7.72 us -> 5.82 us  [passed_along(): lax.ppermute(shard, axis, [(i, (i + by) % peers) for i in range(peers)])]
  transfers between devices with their start and end apart: 15 -> 16, of which waited for: 10 -> 10; matrix products, arithmetic and copies ran while one was open for 2% -> 0% of each run, Pallas kernels for 6% -> 4%
where the time goes in v3:
time: 87.8 us; the launch traced here: 88.3 us
  starting transfers between devices  43.1 us (49%)
  Pallas kernels  25.2 us (29%)
  waiting for transfers between devices  18 us (21%)
  between operations  1.39 us (2%)
    ppermute x8, starting transfers between devices, passed_along(): lax.ppermute(shard, axis, [(i, (i + by) % peers) for i in range(peers)])  29.8 us
    ppermute x8, starting transfers between devices, swapped(): return lax.ppermute(shard, axis, [(i, i ^ bit) for i in range(peers)])  13.4 us
    ppermute x8, waiting for transfers between devices, swapped(): return lax.ppermute(shard, axis, [(i, i ^ bit) for i in range(peers)])  12.1 us
    pallas_call x1, Pallas kernels, element_phase(): pl.pallas_call(functools.partial(element_kernel, neighbours=neighbours, c...  11.7 us
    ppermute x8, waiting for transfers between devices, passed_along(): lax.ppermute(shard, axis, [(i, (i + by) % peers) for i in range(peers)])  5.82 us
    pallas_call x1, Pallas kernels, interface_solve(): pl.pallas_call(functools.partial(solve_kernel, peers=peers), in_specs=[vm...  5.78 us
    pallas_call x1, Pallas kernels, send_blocks(): pl.pallas_call(send_kernel, out_shape=[jax.ShapeDtypeStruct((slots, u_int...  2.37 us
    pallas_call x1, Pallas kernels, per_device(): pl.pallas_call(interior_kernel, out_shape=jax.ShapeDtypeStruct((width, n_...  2.37 us
  transfers between devices with their start and end apart: 16, of which 10 were waited for; matrix products, arithmetic and copies ran while one was open for 0% of the time, Pallas kernels for 4%

profile of v3, /device:TPU:0, one launch (start us, length us, event | category | flops | bytes accessed | tf_op | source)
XLA Modules:
  0.0 88.3 jit_solution(1073280620735294630)
XLA Ops:
  0.6 2.4 %halo_rows.1 = (bf16[32,192]{1,0:T(8,128)(2,1)}, bf16[32,192]{1,0:T(8,128)(2,1)}, bf16[32,192]{1,0:T(8,128)(2,1)}, bf16[32,192]{1,0:T(8,128)(2,1)}) custom-call(bf16[192,512]{1,0:T(8,128)(2,1)} %bitcast.14, bf16[192,704]{1,0:T(8,128)(2,1)} %bitcast.12, s32[4,32]{1,0:T(4,128)} %refs_22_.1), custom_call_target="tpu_custom_call" | custom-call | bytes 9000000 | tf_op jit(solution)/shard_map/halo_rows/pallas_call | solution.py:332
  3.0 5.1 %collective-permute-start = (bf16[32,192]{1,0:T(8,128)(2,1)}, bf16[32,192]{1,0:T(8,128)(2,1)S(1)}, u32[]{:S(2)}, u32[]{:S(2)}) collective-permute-start(bf16[32,192]{1,0:T(8,128)(2,1)} %get-tuple-element.37), channel_id=1, source_target_pairs={{0,6},{1,7},{2,0},{3,1},{4,2},{5,3},{6,4},{7,5},{8,14},{9,15},{10,... | collective-permute-start | bytes 36872 | tf_op jit(solution)/shard_map/ppermute | solution.py:483
  8.1 0.0 collective-permute-start.1
  8.1 0.5 collective-permute-start.2
  8.6 0.7 collective-permute-start.3
  9.9 0.0 collective-permute-done.refs_3_
  9.9 0.0 copy-start
  9.9 0.0 collective-permute-done.1.refs_4_
  10.0 0.0 copy-start.1
  10.0 3.3 %collective-permute-done.2.refs_5_ = bf16[32,192]{1,0:T(8,128)(2,1)S(1)} collective-permute-done((bf16[32,192]{1,0:T(8,128)(2,1)}, bf16[32,192]{1,0:T(8,128)(2,1)S(1)}, u32[]{:S(2)}, u32[]{:S(2)}) %collective-permute-start.2) | collective-permute-done | bytes 12320 | tf_op jit(solution)/shard_map/ppermute | solution.py:483
  13.3 0.0 copy-start.2
  13.3 1.1 %collective-permute-done.3.refs_6_ = bf16[32,192]{1,0:T(8,128)(2,1)S(1)} collective-permute-done((bf16[32,192]{1,0:T(8,128)(2,1)}, bf16[32,192]{1,0:T(8,128)(2,1)S(1)}, u32[]{:S(2)}, u32[]{:S(2)}) %collective-permute-start.3) | collective-permute-done | bytes 12320 | tf_op jit(solution)/shard_map/ppermute | solution.py:483
  14.3 0.0 copy-start.3
  14.3 0.0 copy-done
  14.3 0.0 copy-done.1
  14.3 0.0 copy-done.2
  14.4 0.6 copy-done.3
  14.9 11.7 %elements.1 = (f32[48,2048]{1,0:T(8,128)}, f32[512,128]{1,0:T(8,128)S(1)}, f32[704,128]{1,0:T(8,128)S(1)}, f32[32,128]{1,0:T(8,128)S(1)}, f32[32,128]{1,0:T(8,12...) custom-call(s32[1]{0:T(128)S(6)} %copy.21.refs_0_, ...), custom_call_target="tpu_custom_call" | custom-call | bytes 120000000 | tf_op jit(solution)/shard_map/elements/pallas_call | solution.py:288
  26.6 2.8 %collective-permute-start.4 = (f32[32,128]{1,0:T(8,128)S(1)}, f32[32,128]{1,0:T(8,128)S(1)}, u32[]{:S(2)}, u32[]{:S(2)}) collective-permute-start(f32[32,128]{1,0:T(8,128)S(1)} %get-tuple-element.43), channel_id=1, source_target_pairs={{0,2},{1,3},{2,4},{3,5},{4,6},{5,7},{6,0},{7,1},{8,10},{9,11},{10,... | collective-permute-start | bytes 49160 | tf_op jit(solution)/shard_map/ppermute | solution.py:483
  29.4 14.7 %collective-permute-start.5 = (f32[32,128]{1,0:T(8,128)S(1)}, f32[32,128]{1,0:T(8,128)S(1)}, u32[]{:S(2)}, u32[]{:S(2)}) collective-permute-start(f32[32,128]{1,0:T(8,128)S(1)} %get-tuple-element.44), channel_id=1, source_target_pairs={{0,1},{1,2},{2,3},{3,4},{4,5},{5,6},{6,7},{7,0},{8,9},{9,10},{10,1... | collective-permute-start | bytes 49160 | tf_op jit(solution)/shard_map/ppermute | solution.py:483
  44.1 0.0 collective-permute-start.6
  44.2 6.0 %collective-permute-start.7 = (f32[32,128]{1,0:T(8,128)S(1)}, f32[32,128]{1,0:T(8,128)S(1)}, u32[]{:S(2)}, u32[]{:S(2)}) collective-permute-start(f32[32,128]{1,0:T(8,128)S(1)} %get-tuple-element.46), channel_id=1, source_target_pairs={{0,6},{1,7},{2,0},{3,1},{4,2},{5,3},{6,4},{7,5},{8,14},{9,15},{10,... | collective-permute-start | bytes 49160 | tf_op jit(solution)/shard_map/ppermute | solution.py:483
  50.1 0.0 collective-permute-done.4.refs_0_
  50.1 0.0 collective-permute-done.5.refs_1_
  50.1 0.0 collective-permute-done.6.refs_2_
  50.1 1.4 %collective-permute-done.7.refs_3_ = f32[32,128]{1,0:T(8,128)S(1)} collective-permute-done((f32[32,128]{1,0:T(8,128)S(1)}, f32[32,128]{1,0:T(8,128)S(1)}, u32[]{:S(2)}, u32[]{:S(2)}) %collective-permute-start.7) | collective-permute-done | bytes 16416 | tf_op jit(solution)/shard_map/ppermute | solution.py:483
  51.6 0.5 interface_forces.1
  52.1 7.2 %collective-permute-start.8 = (bf16[352,128]{1,0:T(8,128)(2,1)S(1)}, bf16[352,128]{1,0:T(8,128)(2,1)S(1)}, u32[]{:S(2)}, u32[]{:S(2)}) collective-permute-start(bf16[352,128]{1,0:T(8,128)(2,1)S(1)} %get-tuple-element.48), channel_id=1, source_target_pairs={{0,8},{8,0},{16,24},{24,16},{1,9},{9,1},{17,25},{25,17},{2,10},{10... | collective-permute-start | bytes 270344 | tf_op jit(solution)/shard_map/ppermute | solution.py:478
  59.3 0.7 collective-permute-start.9
  60.0 1.5 %interior_rhs.1.rhs_ref = bf16[1536,64]{1,0:T(8,128)(2,1)S(1)} custom-call(f32[512,128]{1,0:T(8,128)S(1)} %get-tuple-element.53.own_ref, s32[4,32]{1,0:T(4,128)S(1)} %get-tuple-element.42.map_ref, f32[32,128]{1,0:T(8,128)S(1)} %collective-permute-done.4.refs_0_, f32[32,128]{1,0:T(8,128)S(1)} %collective-permute-done.5.refs_1_, ...), custom_call_target="tpu_custom_call" | custom-call | bytes 36000000 | tf_op jit(solution)/shard_map/interior_rhs/pallas_call | solution.py:528
  61.6 0.3 collective-permute-done.8.got_a
  61.8 2.8 %collective-permute-done.9.got_b = bf16[352,128]{1,0:T(8,128)(2,1)S(1)} collective-permute-done((bf16[352,128]{1,0:T(8,128)(2,1)S(1)}, bf16[352,128]{1,0:T(8,128)(2,1)S(1)}, u32[]{:S(2)}, u32[]{:S(2)}) %collective-permute-start.9) | collective-permute-done | bytes 90144 | tf_op jit(solution)/shard_map/ppermute | solution.py:478
  64.7 0.9 %collective-permute-start.10 = (bf16[352,128]{1,0:T(8,128)(2,1)S(1)}, bf16[352,128]{1,0:T(8,128)(2,1)S(1)}, u32[]{:S(2)}, u32[]{:S(2)}) collective-permute-start(bf16[352,128]{1,0:T(8,128)(2,1)S(1)} %get-tuple-element.60), channel_id=1, source_target_pairs={{0,16},{8,24},{16,0},{24,8},{1,17},{9,25},{17,1},{25,9},{2,18},{10... | collective-permute-start | bytes 270344 | tf_op jit(solution)/shard_map/ppermute | solution.py:478
  65.6 0.0 collective-permute-start.11
  65.6 3.6 %collective-permute-done.10.got_a = bf16[352,128]{1,0:T(8,128)(2,1)S(1)} collective-permute-done((bf16[352,128]{1,0:T(8,128)(2,1)S(1)}, bf16[352,128]{1,0:T(8,128)(2,1)S(1)}, u32[]{:S(2)}, u32[]{:S(2)}) %collective-permute-start.10) | collective-permute-done | bytes 90144 | tf_op jit(solution)/shard_map/ppermute | solution.py:478
  69.3 0.9 collective-permute-done.11.got_b
  70.1 5.8 %interface_solve.1 = (bf16[4,264,128]{2,1,0:T(8,128)(2,1)S(1)}, f32[4,264,128]{2,1,0:T(8,128)S(1)}) custom-call(f32[192,704]{1,0:T(8,128)S(1)} %get-tuple-element.58.load_ref, f32[352,128]{1,0:T(8,128)S(1)} %get-tuple-element.59.own_a, bf16[352,128]{1,0:T(8,128)(2,1)S(1)} %collective-permute-done.10.got_a, f32[352,128]{1,0:T(8,128)S(1)} %get-tuple-element.61.own_b, ...), custom_call_target="tpu_custom_call" | custom-call | bytes 30000000 | tf_op jit(solution)/shard_map/interface_solve/pallas_call | solution.py:429
  75.9 0.1 collective-permute-start.12
  76.0 1.5 %collective-permute-done.12.got_ref = bf16[4,264,128]{2,1,0:T(8,128)(2,1)S(1)} collective-permute-done((bf16[4,264,128]{2,1,0:T(8,128)(2,1)S(1)}, bf16[4,264,128]{2,1,0:T(8,128)(2,1)S(1)}, u32[]{:S(2)}, u32[]{:S(2)}) %collective-permute-start.12) | collective-permute-done | bytes 270368 | tf_op jit(solution)/shard_map/ppermute | solution.py:478
  77.5 0.1 correction_sums.1
  77.6 0.1 collective-permute-start.13
  77.7 3.6 %collective-permute-start.14 = (bf16[264,128]{1,0:T(8,128)(2,1)S(1)}, bf16[264,128]{1,0:T(8,128)(2,1)S(1)}, u32[]{:S(2)}, u32[]{:S(2)}) collective-permute-start(bf16[264,128]{1,0:T(8,128)(2,1)S(1)} %get-tuple-element.68), channel_id=1, source_target_pairs={{0,4},{1,5},{2,6},{3,7},{4,0},{5,1},{6,2},{7,3},{8,12},{9,13},{10,... | collective-permute-start | bytes 202760 | tf_op jit(solution)/shard_map/ppermute | solution.py:478
  81.3 0.8 collective-permute-start.15
  82.1 2.4 %interior_solve.1 = f32[192,512]{1,0:T(8,128)} custom-call(bf16[1536,64]{1,0:T(8,128)(2,1)S(1)} %interior_rhs.1.rhs_ref, bf16[1536,1536]{1,0:T(8,128)(2,1)S(1)} %get-tuple-element.57.kinv_ref), custom_call_target="tpu_custom_call" | custom-call | bytes 18000000 | tf_op jit(solution)/shard_map/interior_solve/pallas_call | solution.py:544
  84.4 0.0 collective-permute-done.13.refs_0_
  84.4 1.7 %collective-permute-done.14.refs_1_ = bf16[264,128]{1,0:T(8,128)(2,1)S(1)} collective-permute-done((bf16[264,128]{1,0:T(8,128)(2,1)S(1)}, bf16[264,128]{1,0:T(8,128)(2,1)S(1)}, u32[]{:S(2)}, u32[]{:S(2)}) %collective-permute-start.14) | collective-permute-done | bytes 67616 | tf_op jit(solution)/shard_map/ppermute | solution.py:478
  86.1 1.3 %collective-permute-done.15.refs_2_ = bf16[264,128]{1,0:T(8,128)(2,1)S(1)} collective-permute-done((bf16[264,128]{1,0:T(8,128)(2,1)S(1)}, bf16[264,128]{1,0:T(8,128)(2,1)S(1)}, u32[]{:S(2)}, u32[]{:S(2)}) %collective-permute-start.15) | collective-permute-done | bytes 67616 | tf_op jit(solution)/shard_map/ppermute | solution.py:478
  87.5 0.9 interface_result.1
  (1 shorter events, 0.0 us)
Async XLA Ops:
  3.0 6.9 %collective-permute-start = (bf16[32,192]{1,0:T(8,128)(2,1)}, bf16[32,192]{1,0:T(8,128)(2,1)S(1)}, u32[]{:S(2)}, u32[]{:S(2)}) collective-permute-start(bf16[32,192]{1,0:T(8,128)(2,1)} %get-tuple-element.37), channel_id=1, source_target_pairs={{0,6},{1,7},{2,0},{3,1},{4,2},{5,3},{6,4},{7,5},{8,14},{9,15},{10,... | collective-permute-start | bytes 36872 | tf_op jit(solution)/shard_map/ppermute | solution.py:483
  8.1 1.9 %collective-permute-start.1 = (bf16[32,192]{1,0:T(8,128)(2,1)}, bf16[32,192]{1,0:T(8,128)(2,1)S(1)}, u32[]{:S(2)}, u32[]{:S(2)}) collective-permute-start(bf16[32,192]{1,0:T(8,128)(2,1)} %get-tuple-element.38), channel_id=1, source_target_pairs={{0,7},{1,0},{2,1},{3,2},{4,3},{5,4},{6,5},{7,6},{8,15},{9,8},{10,9... | collective-permute-start | bytes 36872 | tf_op jit(solution)/shard_map/ppermute | solution.py:483
  8.1 5.2 %collective-permute-start.2 = (bf16[32,192]{1,0:T(8,128)(2,1)}, bf16[32,192]{1,0:T(8,128)(2,1)S(1)}, u32[]{:S(2)}, u32[]{:S(2)}) collective-permute-start(bf16[32,192]{1,0:T(8,128)(2,1)} %get-tuple-element.39), channel_id=1, source_target_pairs={{0,1},{1,2},{2,3},{3,4},{4,5},{5,6},{6,7},{7,0},{8,9},{9,10},{10,1... | collective-permute-start | bytes 36872 | tf_op jit(solution)/shard_map/ppermute | solution.py:483
  8.6 5.7 %collective-permute-start.3 = (bf16[32,192]{1,0:T(8,128)(2,1)}, bf16[32,192]{1,0:T(8,128)(2,1)S(1)}, u32[]{:S(2)}, u32[]{:S(2)}) collective-permute-start(bf16[32,192]{1,0:T(8,128)(2,1)} %get-tuple-element.40), channel_id=1, source_target_pairs={{0,2},{1,3},{2,4},{3,5},{4,6},{5,7},{6,0},{7,1},{8,10},{9,11},{10,... | collective-permute-start | bytes 36872 | tf_op jit(solution)/shard_map/ppermute | solution.py:483
  9.9 4.4 %copy-start = (bf16[32,192]{1,0:T(8,128)(2,1)}, bf16[32,192]{1,0:T(8,128)(2,1)S(1)}, u32[]{:S(2)}) copy-start(bf16[32,192]{1,0:T(8,128)(2,1)S(1)} %collective-permute-done.refs_3_) | copy-start | bytes 36868
  10.0 4.4 %copy-start.1 = (bf16[32,192]{1,0:T(8,128)(2,1)}, bf16[32,192]{1,0:T(8,128)(2,1)S(1)}, u32[]{:S(2)}) copy-start(bf16[32,192]{1,0:T(8,128)(2,1)S(1)} %collective-permute-done.1.refs_4_) | copy-start | bytes 36868
  13.3 1.1 %copy-start.2 = (bf16[32,192]{1,0:T(8,128)(2,1)}, bf16[32,192]{1,0:T(8,128)(2,1)S(1)}, u32[]{:S(2)}) copy-start(bf16[32,192]{1,0:T(8,128)(2,1)S(1)} %collective-permute-done.2.refs_5_) | copy-start | bytes 36868
  14.3 0.6 copy-start.3
  26.6 23.5 %collective-permute-start.4 = (f32[32,128]{1,0:T(8,128)S(1)}, f32[32,128]{1,0:T(8,128)S(1)}, u32[]{:S(2)}, u32[]{:S(2)}) collective-permute-start(f32[32,128]{1,0:T(8,128)S(1)} %get-tuple-element.43), channel_id=1, source_target_pairs={{0,2},{1,3},{2,4},{3,5},{4,6},{5,7},{6,0},{7,1},{8,10},{9,11},{10,... | collective-permute-start | bytes 49160 | tf_op jit(solution)/shard_map/ppermute | solution.py:483
  29.4 20.7 %collective-permute-start.5 = (f32[32,128]{1,0:T(8,128)S(1)}, f32[32,128]{1,0:T(8,128)S(1)}, u32[]{:S(2)}, u32[]{:S(2)}) collective-permute-start(f32[32,128]{1,0:T(8,128)S(1)} %get-tuple-element.44), channel_id=1, source_target_pairs={{0,1},{1,2},{2,3},{3,4},{4,5},{5,6},{6,7},{7,0},{8,9},{9,10},{10,1... | collective-permute-start | bytes 49160 | tf_op jit(solution)/shard_map/ppermute | solution.py:483
  44.1 6.0 %collective-permute-start.6 = (f32[32,128]{1,0:T(8,128)S(1)}, f32[32,128]{1,0:T(8,128)S(1)}, u32[]{:S(2)}, u32[]{:S(2)}) collective-permute-start(f32[32,128]{1,0:T(8,128)S(1)} %get-tuple-element.45), channel_id=1, source_target_pairs={{0,7},{1,0},{2,1},{3,2},{4,3},{5,4},{6,5},{7,6},{8,15},{9,8},{10,9... | collective-permute-start | bytes 49160 | tf_op jit(solution)/shard_map/ppermute | solution.py:483
  44.2 7.4 %collective-permute-start.7 = (f32[32,128]{1,0:T(8,128)S(1)}, f32[32,128]{1,0:T(8,128)S(1)}, u32[]{:S(2)}, u32[]{:S(2)}) collective-permute-start(f32[32,128]{1,0:T(8,128)S(1)} %get-tuple-element.46), channel_id=1, source_target_pairs={{0,6},{1,7},{2,0},{3,1},{4,2},{5,3},{6,4},{7,5},{8,14},{9,15},{10,... | collective-permute-start | bytes 49160 | tf_op jit(solution)/shard_map/ppermute | solution.py:483
  52.1 9.7 %collective-permute-start.8 = (bf16[352,128]{1,0:T(8,128)(2,1)S(1)}, bf16[352,128]{1,0:T(8,128)(2,1)S(1)}, u32[]{:S(2)}, u32[]{:S(2)}) collective-permute-start(bf16[352,128]{1,0:T(8,128)(2,1)S(1)} %get-tuple-element.48), channel_id=1, source_target_pairs={{0,8},{8,0},{16,24},{24,16},{1,9},{9,1},{17,25},{25,17},{2,10},{10... | collective-permute-start | bytes 270344 | tf_op jit(solution)/shard_map/ppermute | solution.py:478
  59.3 5.3 %collective-permute-start.9 = (bf16[352,128]{1,0:T(8,128)(2,1)S(1)}, bf16[352,128]{1,0:T(8,128)(2,1)S(1)}, u32[]{:S(2)}, u32[]{:S(2)}) collective-permute-start(bf16[352,128]{1,0:T(8,128)(2,1)S(1)} %get-tuple-element.50), channel_id=1, source_target_pairs={{0,16},{8,24},{16,0},{24,8},{1,17},{9,25},{17,1},{25,9},{2,18},{10... | collective-permute-start | bytes 270344 | tf_op jit(solution)/shard_map/ppermute | solution.py:478
  64.7 4.6 %collective-permute-start.10 = (bf16[352,128]{1,0:T(8,128)(2,1)S(1)}, bf16[352,128]{1,0:T(8,128)(2,1)S(1)}, u32[]{:S(2)}, u32[]{:S(2)}) collective-permute-start(bf16[352,128]{1,0:T(8,128)(2,1)S(1)} %get-tuple-element.60), channel_id=1, source_target_pairs={{0,16},{8,24},{16,0},{24,8},{1,17},{9,25},{17,1},{25,9},{2,18},{10... | collective-permute-start | bytes 270344 | tf_op jit(solution)/shard_map/ppermute | solution.py:478
  65.6 4.5 %collective-permute-start.11 = (bf16[352,128]{1,0:T(8,128)(2,1)S(1)}, bf16[352,128]{1,0:T(8,128)(2,1)S(1)}, u32[]{:S(2)}, u32[]{:S(2)}) collective-permute-start(bf16[352,128]{1,0:T(8,128)(2,1)S(1)} %get-tuple-element.62), channel_id=1, source_target_pairs={{0,8},{8,0},{16,24},{24,16},{1,9},{9,1},{17,25},{25,17},{2,10},{10... | collective-permute-start | bytes 270344 | tf_op jit(solution)/shard_map/ppermute | solution.py:478
  75.9 1.6 %collective-permute-start.12 = (bf16[4,264,128]{2,1,0:T(8,128)(2,1)S(1)}, bf16[4,264,128]{2,1,0:T(8,128)(2,1)S(1)}, u32[]{:S(2)}, u32[]{:S(2)}) collective-permute-start(bf16[4,264,128]{2,1,0:T(8,128)(2,1)S(1)} %get-tuple-element.65), channel_id=1, source_target_pairs={{0,1},{1,0},{2,3},{3,2},{4,5},{5,4},{6,7},{7,6},{8,9},{9,8},{10,11... | collective-permute-start | bytes 811016 | tf_op jit(solution)/shard_map/ppermute | solution.py:478
  77.6 6.8 %collective-permute-start.13 = (bf16[264,128]{1,0:T(8,128)(2,1)S(1)}, bf16[264,128]{1,0:T(8,128)(2,1)S(1)}, u32[]{:S(2)}, u32[]{:S(2)}) collective-permute-start(bf16[264,128]{1,0:T(8,128)(2,1)S(1)} %get-tuple-element.67), channel_id=1, source_target_pairs={{0,2},{1,3},{2,0},{3,1},{4,6},{5,7},{6,4},{7,5},{8,10},{9,11},{10,... | collective-permute-start | bytes 202760 | tf_op jit(solution)/shard_map/ppermute | solution.py:478
  77.7 8.4 %collective-permute-start.14 = (bf16[264,128]{1,0:T(8,128)(2,1)S(1)}, bf16[264,128]{1,0:T(8,128)(2,1)S(1)}, u32[]{:S(2)}, u32[]{:S(2)}) collective-permute-start(bf16[264,128]{1,0:T(8,128)(2,1)S(1)} %get-tuple-element.68), channel_id=1, source_target_pairs={{0,4},{1,5},{2,6},{3,7},{4,0},{5,1},{6,2},{7,3},{8,12},{9,13},{10,... | collective-permute-start | bytes 202760 | tf_op jit(solution)/shard_map/ppermute | solution.py:478
  81.3 6.2 %collective-permute-start.15 = (bf16[264,128]{1,0:T(8,128)(2,1)S(1)}, bf16[264,128]{1,0:T(8,128)(2,1)S(1)}, u32[]{:S(2)}, u32[]{:S(2)}) collective-permute-start(bf16[264,128]{1,0:T(8,128)(2,1)S(1)} %get-tuple-element.69), channel_id=1, source_target_pairs={{0,6},{1,7},{2,4},{3,5},{4,2},{5,3},{6,0},{7,1},{8,14},{9,15},{10,... | collective-permute-start | bytes 202760 | tf_op jit(solution)/shard_map/ppermute | solution.py:478

commit v4 on v3

--- a/solution.py
+++ b/solution.py
@@ -26,7 +26,7 @@
     return pl.CostEstimate(flops=0, bytes_accessed=int(3e6 * microseconds), transcendentals=0)
 
 
-LIMIT = 38
+LIMIT = 34
 SMALL = pltpu.CompilerParams(vmem_limit_bytes=12 << 20)
 BF16 = jnp.bfloat16
 F32 = jnp.float32
@@ -104,6 +104,62 @@
     return -(-n // to) * to
 
 
+def node_values(rows, dims, high_ref, low_ref):
+    value = lax.dot_general(high_ref[...], rows, dims, preferred_element_type=F32)
+    value = value + lax.dot_general(low_ref[...], rows, dims, preferred_element_type=F32)
+    upper = value.astype(BF16).astype(F32)
+    row = lax.broadcasted_iota(jnp.int32, (value.shape[0], 1), 0)
+    return jnp.where(lax.rem(row, 2 * PART) < PART, upper, value - upper).astype(BF16)
+
+
+def put_nodes(nodes, start, value):
+    both, half, length = nodes.shape[0] // 2, nodes.shape[1], value.shape[1]
+    cut = min(max(half - start, 0), length)
+    if cut:
+        nodes[:both, start : start + cut] = value[:, :cut]
+    if cut < length:
+        at = start + cut - half
+        nodes[both:, at : at + length - cut] = value[:, cut:]
+
+
+def prepare_kernel(int_ref, if_ref, *refs):
+    kept = len(refs) // 2 - 1
+    far_refs, nodes, near_refs, arrived = refs[:kept], refs[kept], refs[kept + 1 : -1], refs[-1]
+    fetches = [
+        pltpu.make_async_copy(far, near, arrived.at[k]) for k, (far, near) in enumerate(zip(far_refs, near_refs))
+    ]
+    for fetch in fetches:
+        fetch.start()
+    nodes[...] = jnp.zeros_like(nodes)
+    for fetch in fetches[:2]:
+        fetch.wait()
+    high_ref, low_ref = near_refs[:2]
+    dims = (((1,), (0,)), ((), ()))
+    put_nodes(nodes, 0, node_values(int_ref[...], dims, high_ref, low_ref))
+    put_nodes(nodes, int_ref.shape[1], node_values(if_ref[...], dims, high_ref, low_ref))
+    for fetch in fetches[2:]:
+        fetch.wait()
+
+
+def half_of(own, halo):
+    return up(up(own, 128) + up(halo, 128), 256) // 2
+
+
+def prepare(u_int, u_if, halo, arrays):
+    half = up(half_of(u_int.shape[1] + u_if.shape[1], halo), 128)
+    vmem = pl.BlockSpec(memory_space=pltpu.VMEM)
+    return pl.pallas_call(
+        prepare_kernel,
+        in_specs=[vmem] * 2 + [pl.BlockSpec(memory_space=pl.ANY)] * len(arrays),
+        out_specs=[vmem] * (1 + len(arrays)),
+        scratch_shapes=[pltpu.SemaphoreType.DMA((len(arrays),))],
+        out_shape=[pltpu.VMEM((4 * GROUPS * PART, half), BF16)] + [pltpu.VMEM(x.shape, x.dtype) for x in arrays],
+        compiler_params=pltpu.CompilerParams(vmem_limit_bytes=56 << 20),
+        cost_estimate=lasts(5),
+        name="own_nodes",
+    )(u_int, u_if, *arrays)
+
+
 def element_kernel(*refs, neighbours, chunk, own, half, kept):
     refs = list(refs)
 
@@ -111,7 +167,7 @@
         taken, refs[:n] = refs[:n], []
         return taken
 
-    count_ref, int_ref, if_ref = take(3)
+    count_ref, base_ref = take(2)
     halo_refs = take(neighbours)
     conn_ref, size_ref, stiff_ref, yield_ref, rate_ref, init_ref = take(6)
     high_ref, low_ref, strain_ref, force_ref = take(4)
@@ -125,35 +181,17 @@
     ]
     for fetch in fetches:
         fetch.start()
-    n_int, n_if, slots = int_ref.shape[1], if_ref.shape[1], halo_refs[0].shape[0]
+    n_int, n_if, slots = pint_ref.shape[0], pif_ref.shape[0], halo_refs[0].shape[0]
     halo_at = up(own, 128)
     both = 2 * GROUPS * PART
     chunks = end_ref.shape[1] // chunk
     count = count_ref[0]
     used = jnp.maximum(lax.div(count + chunk - 1, chunk), 1)
 
-    nodes[...] = jnp.zeros_like(nodes)
     total[...] = jnp.zeros_like(total)
+    nodes[...] = base_ref[...]
     halo = jnp.concatenate([ref[...].astype(F32) for ref in halo_refs], axis=0).astype(BF16)
-    is_high = lax.rem(lax.broadcasted_iota(jnp.int32, (both, 1), 0), 2 * PART) < PART
-    pieces = (
-        (0, int_ref[...], (((1,), (0,)), ((), ()))),
-        (n_int, if_ref[...], (((1,), (0,)), ((), ()))),
-        (halo_at, halo, NT),
-    )
-    spans = []
-    for start, rows, dims in pieces:
-        value = lax.dot_general(high_ref[...], rows, dims, preferred_element_type=F32)
-        value = value + lax.dot_general(low_ref[...], rows, dims, preferred_element_type=F32)
-        upper = value.astype(BF16).astype(F32)
-        value = jnp.where(is_high, upper, value - upper).astype(BF16)
-        length = value.shape[1]
-        cut = min(max(half - start, 0), length)
-        if cut:
-            nodes[:both, start : start + cut] = value[:, :cut]
-        if cut < length:
-            at = start + cut - half
-            nodes[both:, at : at + length - cut] = value[:, cut:]
+    put_nodes(nodes, halo_at, node_values(halo, NT, high_ref, low_ref))
 
     def columns(c):
         return pl.ds(pl.multiple_of(c * chunk, chunk), chunk)
@@ -215,7 +253,7 @@
         part = jnp.concatenate([jnp.where(upper, 0.0, part), jnp.where(upper, part, 0.0)], axis=0).astype(BF16)
         total[...] += lax.dot_general(onehot[lax.rem(c, 3), corner], part, NT, preferred_element_type=F32)
 
-    turns = 4
+    turns = 8
 
     def stage(c, first, middle, last):
         if middle:
@@ -276,15 +314,14 @@
     return pl.BlockSpec(shape, lambda *_: (0,) * len(shape))
 
 
-def element_phase(count, u_int, u_if, halos, conn, params, stress_init, tables, later=(), interpret=False):
+def element_phase(count, nodes, halos, sizes, conn, params, stress_init, tables, later=()):
     chunk = 256
-    n_int, n_if = u_int.shape[1], u_if.shape[1]
+    n_int, n_if = sizes
     own = n_int + n_if
     neighbours, slots = len(halos), halos[0].shape[0]
-    half = up(up(own, 128) + neighbours * slots, 256) // 2
-    half = up(half, 128)
+    half = nodes.shape[1]
     vmem = pl.BlockSpec(memory_space=pltpu.VMEM)
-    inputs = [u_int, u_if, *halos, conn, *params, stress_init, *tables[:4]]
+    inputs = [nodes, *halos, conn, *params, stress_init, *tables]
     return pl.pallas_call(
         functools.partial(element_kernel, neighbours=neighbours, chunk=chunk, own=own, half=half, kept=len(later)),
         in_specs=[pl.BlockSpec(memory_space=pltpu.SMEM)] + [vmem] * len(inputs)
@@ -309,7 +346,6 @@
         compiler_params=pltpu.CompilerParams(vmem_limit_bytes=LIMIT << 20),
         cost_estimate=lasts(40),
         name="elements",
-        interpret=interpret,
     )(count, *inputs, *later)
 
 
@@ -512,8 +548,20 @@
     halos = [passed_along(blocks[j], "dom", offsets[j]) for j in range(neighbours)]
     params = [x.reshape(1, -1) for x in (elem_size, stiffness, yield_stress, relax_rate)]
     later = (sinv.T, kinv_int, load_int.T, load_if.T, analysis, send_map)
+    nodes, synth_high, synth_low, strain, force, near_conn, init, *params = (
+        pltpu.with_memory_space_constraint(x, pltpu.VMEM)
+        for x in prepare(u_int.T, u_if.T, neighbours * slots, [*tables[:4], conn.T, stress_init, *params])
+    )
     stress_end, p_int, p_if, *more = element_phase(
-        counts, u_int.T, u_if.T, halos, conn.T, params, stress_init, tables, later
+        counts,
+        nodes,
+        halos,
+        (n_int, n_if),
+        near_conn,
+        params,
+        init,
+        (synth_high, synth_low, strain, force),
+        later,
     )
     back = more[:neighbours]
     sinv_t, kinv, load_int_t, load_if_t, analysis, near_map = (

time: 87.8 us -> 83.2 us (0.948)
  Pallas kernels: 25.2 us -> 33.6 us
  starting transfers between devices: 43.1 us -> 35.2 us
  waiting for transfers between devices: 18 us -> 13.6 us
    ppermute x8, starting transfers between devices: 29.8 us -> 11.9 us  [passed_along(): lax.ppermute(shard, axis, [(i, (i + by) % peers) for i in range(peers)])]
    ppermute x8, starting transfers between devices: 13.4 us -> 23.3 us  [swapped(): return lax.ppermute(shard, axis, [(i, i ^ bit) for i in range(peers)])]
    pallas_call x1, Pallas kernels: 11.7 us -> 17.5 us  [element_phase(): pl.pallas_call(functools.partial(element_kernel, neighbours=neighbours, c...]
    pallas_call x0 -> x1, Pallas kernels: none -> 2.55 us  [prepare(): pl.pallas_call(prepare_kernel, in_specs=[vmem] * 2 + [pl.BlockSpec(memory...]
    ppermute x8, waiting for transfers between devices: 5.82 us -> 3.59 us  [passed_along(): lax.ppermute(shard, axis, [(i, (i + by) % peers) for i in range(peers)])]
    ppermute x8, waiting for transfers between devices: 12.1 us -> 10 us  [swapped(): return lax.ppermute(shard, axis, [(i, i ^ bit) for i in range(peers)])]
  transfers between devices with their start and end apart: 16 -> 16, of which waited for: 10 -> 9; matrix products, arithmetic and copies ran while one was open for 0% -> 0% of each run, Pallas kernels for 4% -> 8%
where the time goes in v4:
time: 83.2 us; the launch traced here: 84.4 us
  starting transfers between devices  35.2 us (42%)
  Pallas kernels  33.6 us (40%)
  waiting for transfers between devices  13.6 us (16%)
  between operations  1.41 us (2%)
    ppermute x8, starting transfers between devices, swapped(): return lax.ppermute(shard, axis, [(i, i ^ bit) for i in range(peers)])  23.3 us
    pallas_call x1, Pallas kernels, element_phase(): pl.pallas_call(functools.partial(element_kernel, neighbours=neighbours, c...  17.5 us
    ppermute x8, starting transfers between devices, passed_along(): lax.ppermute(shard, axis, [(i, (i + by) % peers) for i in range(peers)])  11.9 us
    ppermute x8, waiting for transfers between devices, swapped(): return lax.ppermute(shard, axis, [(i, i ^ bit) for i in range(peers)])  10 us
    pallas_call x1, Pallas kernels, interface_solve(): pl.pallas_call(functools.partial(solve_kernel, peers=peers), in_specs=[vm...  5.77 us
    ppermute x8, waiting for transfers between devices, passed_along(): lax.ppermute(shard, axis, [(i, (i + by) % peers) for i in range(peers)])  3.59 us
    pallas_call x1, Pallas kernels, prepare(): pl.pallas_call(prepare_kernel, in_specs=[vmem] * 2 + [pl.BlockSpec(memory...  2.55 us
    pallas_call x1, Pallas kernels, send_blocks(): pl.pallas_call(send_kernel, out_shape=[jax.ShapeDtypeStruct((slots, u_int...  2.37 us
  transfers between devices with their start and end apart: 16, of which 9 were waited for; matrix products, arithmetic and copies ran while one was open for 0% of the time, Pallas kernels for 8%

profile of v4, /device:TPU:0, one launch (start us, length us, event | category | flops | bytes accessed | tf_op | source)
XLA Modules:
  0.0 84.4 jit_solution(4841241743984486406)
XLA Ops:
  0.6 2.4 %halo_rows.1 = (bf16[32,192]{1,0:T(8,128)(2,1)}, bf16[32,192]{1,0:T(8,128)(2,1)}, bf16[32,192]{1,0:T(8,128)(2,1)}, bf16[32,192]{1,0:T(8,128)(2,1)}) custom-call(bf16[192,512]{1,0:T(8,128)(2,1)} %bitcast.14, bf16[192,704]{1,0:T(8,128)(2,1)} %bitcast.12, s32[4,32]{1,0:T(4,128)} %refs_21_.1), custom_call_target="tpu_custom_call" | custom-call | bytes 9000000 | tf_op jit(solution)/shard_map/halo_rows/pallas_call | solution.py:368
  3.0 5.1 %collective-permute-start = (bf16[32,192]{1,0:T(8,128)(2,1)}, bf16[32,192]{1,0:T(8,128)(2,1)S(1)}, u32[]{:S(2)}, u32[]{:S(2)}) collective-permute-start(bf16[32,192]{1,0:T(8,128)(2,1)} %get-tuple-element.49), channel_id=1, source_target_pairs={{0,6},{1,7},{2,0},{3,1},{4,2},{5,3},{6,4},{7,5},{8,14},{9,15},{10,... | collective-permute-start | bytes 36872 | tf_op jit(solution)/shard_map/ppermute | solution.py:519
  8.1 0.0 collective-permute-start.1
  8.1 0.5 collective-permute-start.2
  8.6 0.7 collective-permute-start.3
  9.9 2.6 %own_nodes.1 = (bf16[384,768]{1,0:T(8,128)(2,1)S(1)}, bf16[192,192]{1,0:T(8,128)(2,1)S(1)}, bf16[192,192]{1,0:T(8,128)(2,1)S(1)}, bf16[192,192]{1,0:T(8,128)(2,1...) custom-call(bf16[192,512]{1,0:T(8,128)(2,1)} %bitcast.15, ...), custom_call_target="tpu_custom_call" | custom-call | bytes 15000000 | tf_op jit(solution)/shard_map/own_nodes/pallas_call | solution.py:151
  12.5 0.0 collective-permute-done.refs_2_
  12.5 0.0 copy-start
  12.5 0.0 collective-permute-done.1.refs_3_
  12.5 0.0 copy-start.1
  12.5 0.7 collective-permute-done.2.refs_4_
  13.3 0.0 copy-start.2
  13.3 1.1 %collective-permute-done.3.refs_5_ = bf16[32,192]{1,0:T(8,128)(2,1)S(1)} collective-permute-done((bf16[32,192]{1,0:T(8,128)(2,1)}, bf16[32,192]{1,0:T(8,128)(2,1)S(1)}, u32[]{:S(2)}, u32[]{:S(2)}) %collective-permute-start.3) | collective-permute-done | bytes 12320 | tf_op jit(solution)/shard_map/ppermute | solution.py:519
  14.3 0.0 copy-start.3
  14.3 0.0 copy-done
  14.3 0.0 copy-done.1
  14.3 0.0 copy-done.2
  14.4 0.6 copy-done.3
  14.9 17.5 %elements.1 = (f32[48,2048]{1,0:T(8,128)}, f32[512,128]{1,0:T(8,128)S(1)}, f32[704,128]{1,0:T(8,128)S(1)}, f32[32,128]{1,0:T(8,128)S(1)}, f32[32,128]{1,0:T(8,12...) custom-call(s32[1]{0:T(128)S(6)} %copy.21.refs_0_, ...), custom_call_target="tpu_custom_call" | custom-call | bytes 120000000 | tf_op jit(solution)/shard_map/elements/pallas_call | solution.py:325
  32.4 0.1 collective-permute-start.4
  32.5 0.1 collective-permute-start.5
  32.6 3.5 %collective-permute-start.6 = (f32[32,128]{1,0:T(8,128)S(1)}, f32[32,128]{1,0:T(8,128)S(1)}, u32[]{:S(2)}, u32[]{:S(2)}) collective-permute-start(f32[32,128]{1,0:T(8,128)S(1)} %get-tuple-element.67), channel_id=1, source_target_pairs={{0,7},{1,0},{2,1},{3,2},{4,3},{5,4},{6,5},{7,6},{8,15},{9,8},{10,9... | collective-permute-start | bytes 49160 | tf_op jit(solution)/shard_map/ppermute | solution.py:519
  36.1 2.0 %collective-permute-start.7 = (f32[32,128]{1,0:T(8,128)S(1)}, f32[32,128]{1,0:T(8,128)S(1)}, u32[]{:S(2)}, u32[]{:S(2)}) collective-permute-start(f32[32,128]{1,0:T(8,128)S(1)} %get-tuple-element.68), channel_id=1, source_target_pairs={{0,6},{1,7},{2,0},{3,1},{4,2},{5,3},{6,4},{7,5},{8,14},{9,15},{10,... | collective-permute-start | bytes 49160 | tf_op jit(solution)/shard_map/ppermute | solution.py:519
  38.0 0.1 collective-permute-done.4.refs_0_
  38.1 0.0 collective-permute-done.5.refs_1_
  38.1 0.0 collective-permute-done.6.refs_2_
  38.1 1.7 %collective-permute-done.7.refs_3_ = f32[32,128]{1,0:T(8,128)S(1)} collective-permute-done((f32[32,128]{1,0:T(8,128)S(1)}, f32[32,128]{1,0:T(8,128)S(1)}, u32[]{:S(2)}, u32[]{:S(2)}) %collective-permute-start.7) | collective-permute-done | bytes 16416 | tf_op jit(solution)/shard_map/ppermute | solution.py:519
  39.8 0.5 interface_forces.1
  40.3 14.8 %collective-permute-start.8 = (bf16[352,128]{1,0:T(8,128)(2,1)S(1)}, bf16[352,128]{1,0:T(8,128)(2,1)S(1)}, u32[]{:S(2)}, u32[]{:S(2)}) collective-permute-start(bf16[352,128]{1,0:T(8,128)(2,1)S(1)} %get-tuple-element.70), channel_id=1, source_target_pairs={{0,8},{8,0},{16,24},{24,16},{1,9},{9,1},{17,25},{25,17},{2,10},{10... | collective-permute-start | bytes 270344 | tf_op jit(solution)/shard_map/ppermute | solution.py:514
  55.2 1.9 %collective-permute-start.9 = (bf16[352,128]{1,0:T(8,128)(2,1)S(1)}, bf16[352,128]{1,0:T(8,128)(2,1)S(1)}, u32[]{:S(2)}, u32[]{:S(2)}) collective-permute-start(bf16[352,128]{1,0:T(8,128)(2,1)S(1)} %get-tuple-element.72), channel_id=1, source_target_pairs={{0,16},{8,24},{16,0},{24,8},{1,17},{9,25},{17,1},{25,9},{2,18},{10... | collective-permute-start | bytes 270344 | tf_op jit(solution)/shard_map/ppermute | solution.py:514
  57.1 1.5 %interior_rhs.1.rhs_ref = bf16[1536,64]{1,0:T(8,128)(2,1)S(1)} custom-call(f32[512,128]{1,0:T(8,128)S(1)} %get-tuple-element.75.own_ref, s32[4,32]{1,0:T(4,128)S(1)} %get-tuple-element.64.map_ref, f32[32,128]{1,0:T(8,128)S(1)} %collective-permute-done.4.refs_0_, f32[32,128]{1,0:T(8,128)S(1)} %collective-permute-done.5.refs_1_, ...), custom_call_target="tpu_custom_call" | custom-call | bytes 36000000 | tf_op jit(solution)/shard_map/interior_rhs/pallas_call | solution.py:576
  58.6 0.0 collective-permute-done.8.got_a
  58.6 1.9 %collective-permute-done.9.got_b = bf16[352,128]{1,0:T(8,128)(2,1)S(1)} collective-permute-done((bf16[352,128]{1,0:T(8,128)(2,1)S(1)}, bf16[352,128]{1,0:T(8,128)(2,1)S(1)}, u32[]{:S(2)}, u32[]{:S(2)}) %collective-permute-start.9) | collective-permute-done | bytes 90144 | tf_op jit(solution)/shard_map/ppermute | solution.py:514
  60.6 2.1 %collective-permute-start.10 = (bf16[352,128]{1,0:T(8,128)(2,1)S(1)}, bf16[352,128]{1,0:T(8,128)(2,1)S(1)}, u32[]{:S(2)}, u32[]{:S(2)}) collective-permute-start(bf16[352,128]{1,0:T(8,128)(2,1)S(1)} %get-tuple-element.82), channel_id=1, source_target_pairs={{0,16},{8,24},{16,0},{24,8},{1,17},{9,25},{17,1},{25,9},{2,18},{10... | collective-permute-start | bytes 270344 | tf_op jit(solution)/shard_map/ppermute | solution.py:514
  62.7 0.0 collective-permute-start.11
  62.7 2.5 %collective-permute-done.10.got_a = bf16[352,128]{1,0:T(8,128)(2,1)S(1)} collective-permute-done((bf16[352,128]{1,0:T(8,128)(2,1)S(1)}, bf16[352,128]{1,0:T(8,128)(2,1)S(1)}, u32[]{:S(2)}, u32[]{:S(2)}) %collective-permute-start.10) | collective-permute-done | bytes 90144 | tf_op jit(solution)/shard_map/ppermute | solution.py:514
  65.2 2.0 %collective-permute-done.11.got_b = bf16[352,128]{1,0:T(8,128)(2,1)S(1)} collective-permute-done((bf16[352,128]{1,0:T(8,128)(2,1)S(1)}, bf16[352,128]{1,0:T(8,128)(2,1)S(1)}, u32[]{:S(2)}, u32[]{:S(2)}) %collective-permute-start.11) | collective-permute-done | bytes 90144 | tf_op jit(solution)/shard_map/ppermute | solution.py:514
  67.2 5.8 %interface_solve.1 = (bf16[4,264,128]{2,1,0:T(8,128)(2,1)S(1)}, f32[4,264,128]{2,1,0:T(8,128)S(1)}) custom-call(f32[192,704]{1,0:T(8,128)S(1)} %get-tuple-element.80.load_ref, f32[352,128]{1,0:T(8,128)S(1)} %get-tuple-element.81.own_a, bf16[352,128]{1,0:T(8,128)(2,1)S(1)} %collective-permute-done.10.got_a, f32[352,128]{1,0:T(8,128)S(1)} %get-tuple-element.83.own_b, ...), custom_call_target="tpu_custom_call" | custom-call | bytes 30000000 | tf_op jit(solution)/shard_map/interface_solve/pallas_call | solution.py:465
  73.0 0.1 collective-permute-start.12
  73.1 1.5 %collective-permute-done.12.got_ref = bf16[4,264,128]{2,1,0:T(8,128)(2,1)S(1)} collective-permute-done((bf16[4,264,128]{2,1,0:T(8,128)(2,1)S(1)}, bf16[4,264,128]{2,1,0:T(8,128)(2,1)S(1)}, u32[]{:S(2)}, u32[]{:S(2)}) %collective-permute-start.12) | collective-permute-done | bytes 270368 | tf_op jit(solution)/shard_map/ppermute | solution.py:514
  74.6 0.1 correction_sums.1
  74.7 0.1 collective-permute-start.13
  74.7 1.8 %collective-permute-start.14 = (bf16[264,128]{1,0:T(8,128)(2,1)S(1)}, bf16[264,128]{1,0:T(8,128)(2,1)S(1)}, u32[]{:S(2)}, u32[]{:S(2)}) collective-permute-start(bf16[264,128]{1,0:T(8,128)(2,1)S(1)} %get-tuple-element.90), channel_id=1, source_target_pairs={{0,4},{1,5},{2,6},{3,7},{4,0},{5,1},{6,2},{7,3},{8,12},{9,13},{10,... | collective-permute-start | bytes 202760 | tf_op jit(solution)/shard_map/ppermute | solution.py:514
  76.5 2.6 %collective-permute-start.15 = (bf16[264,128]{1,0:T(8,128)(2,1)S(1)}, bf16[264,128]{1,0:T(8,128)(2,1)S(1)}, u32[]{:S(2)}, u32[]{:S(2)}) collective-permute-start(bf16[264,128]{1,0:T(8,128)(2,1)S(1)} %get-tuple-element.91), channel_id=1, source_target_pairs={{0,6},{1,7},{2,4},{3,5},{4,2},{5,3},{6,0},{7,1},{8,14},{9,15},{10,... | collective-permute-start | bytes 202760 | tf_op jit(solution)/shard_map/ppermute | solution.py:514
  79.1 2.4 %interior_solve.1 = f32[192,512]{1,0:T(8,128)} custom-call(bf16[1536,64]{1,0:T(8,128)(2,1)S(1)} %interior_rhs.1.rhs_ref, bf16[1536,1536]{1,0:T(8,128)(2,1)S(1)} %get-tuple-element.79.kinv_ref), custom_call_target="tpu_custom_call" | custom-call | bytes 18000000 | tf_op jit(solution)/shard_map/interior_solve/pallas_call | solution.py:592
  81.5 0.0 collective-permute-done.13.refs_0_
  81.5 2.0 %collective-permute-done.14.refs_1_ = bf16[264,128]{1,0:T(8,128)(2,1)S(1)} collective-permute-done((bf16[264,128]{1,0:T(8,128)(2,1)S(1)}, bf16[264,128]{1,0:T(8,128)(2,1)S(1)}, u32[]{:S(2)}, u32[]{:S(2)}) %collective-permute-start.14) | collective-permute-done | bytes 67616 | tf_op jit(solution)/shard_map/ppermute | solution.py:514
  83.5 0.0 collective-permute-done.15.refs_2_
  83.5 0.9 %interface_result.1 = f32[176,192]{1,0:T(8,128)} custom-call(f32[264,128]{1,0:T(8,128)S(1)} %get-tuple-element.88.mine_ref, bf16[264,128]{1,0:T(8,128)(2,1)S(1)} %collective-permute-done.13.refs_0_, bf16[264,128]{1,0:T(8,128)(2,1)S(1)} %collective-permute-done.14.refs_1_, bf16[264,128]{1,0:T(8,128)(2,1)S(1)} %collective-permute-done.15.refs_2_), custom_call_target="tpu_custom_call" | custom-call | bytes 6000000 | tf_op jit(solution)/shard_map/interface_result/pallas_call | solution.py:612
  (1 shorter events, 0.0 us)
Async XLA Ops:
  3.0 9.5 %collective-permute-start = (bf16[32,192]{1,0:T(8,128)(2,1)}, bf16[32,192]{1,0:T(8,128)(2,1)S(1)}, u32[]{:S(2)}, u32[]{:S(2)}) collective-permute-start(bf16[32,192]{1,0:T(8,128)(2,1)} %get-tuple-element.49), channel_id=1, source_target_pairs={{0,6},{1,7},{2,0},{3,1},{4,2},{5,3},{6,4},{7,5},{8,14},{9,15},{10,... | collective-permute-start | bytes 36872 | tf_op jit(solution)/shard_map/ppermute | solution.py:519
  8.1 4.4 %collective-permute-start.1 = (bf16[32,192]{1,0:T(8,128)(2,1)}, bf16[32,192]{1,0:T(8,128)(2,1)S(1)}, u32[]{:S(2)}, u32[]{:S(2)}) collective-permute-start(bf16[32,192]{1,0:T(8,128)(2,1)} %get-tuple-element.50), channel_id=1, source_target_pairs={{0,7},{1,0},{2,1},{3,2},{4,3},{5,4},{6,5},{7,6},{8,15},{9,8},{10,9... | collective-permute-start | bytes 36872 | tf_op jit(solution)/shard_map/ppermute | solution.py:519
  8.1 5.2 %collective-permute-start.2 = (bf16[32,192]{1,0:T(8,128)(2,1)}, bf16[32,192]{1,0:T(8,128)(2,1)S(1)}, u32[]{:S(2)}, u32[]{:S(2)}) collective-permute-start(bf16[32,192]{1,0:T(8,128)(2,1)} %get-tuple-element.51), channel_id=1, source_target_pairs={{0,1},{1,2},{2,3},{3,4},{4,5},{5,6},{6,7},{7,0},{8,9},{9,10},{10,1... | collective-permute-start | bytes 36872 | tf_op jit(solution)/shard_map/ppermute | solution.py:519
  8.6 5.7 %collective-permute-start.3 = (bf16[32,192]{1,0:T(8,128)(2,1)}, bf16[32,192]{1,0:T(8,128)(2,1)S(1)}, u32[]{:S(2)}, u32[]{:S(2)}) collective-permute-start(bf16[32,192]{1,0:T(8,128)(2,1)} %get-tuple-element.52), channel_id=1, source_target_pairs={{0,2},{1,3},{2,4},{3,5},{4,6},{5,7},{6,0},{7,1},{8,10},{9,11},{10,... | collective-permute-start | bytes 36872 | tf_op jit(solution)/shard_map/ppermute | solution.py:519
  12.5 1.9 %copy-start = (bf16[32,192]{1,0:T(8,128)(2,1)}, bf16[32,192]{1,0:T(8,128)(2,1)S(1)}, u32[]{:S(2)}) copy-start(bf16[32,192]{1,0:T(8,128)(2,1)S(1)} %collective-permute-done.refs_2_) | copy-start | bytes 36868
  12.5 1.8 %copy-start.1 = (bf16[32,192]{1,0:T(8,128)(2,1)}, bf16[32,192]{1,0:T(8,128)(2,1)S(1)}, u32[]{:S(2)}) copy-start(bf16[32,192]{1,0:T(8,128)(2,1)S(1)} %collective-permute-done.1.refs_3_) | copy-start | bytes 36868
  13.3 1.1 %copy-start.2 = (bf16[32,192]{1,0:T(8,128)(2,1)}, bf16[32,192]{1,0:T(8,128)(2,1)S(1)}, u32[]{:S(2)}) copy-start(bf16[32,192]{1,0:T(8,128)(2,1)S(1)} %collective-permute-done.2.refs_4_) | copy-start | bytes 36868
  14.3 0.6 copy-start.3
  32.4 5.7 %collective-permute-start.4 = (f32[32,128]{1,0:T(8,128)S(1)}, f32[32,128]{1,0:T(8,128)S(1)}, u32[]{:S(2)}, u32[]{:S(2)}) collective-permute-start(f32[32,128]{1,0:T(8,128)S(1)} %get-tuple-element.65), channel_id=1, source_target_pairs={{0,2},{1,3},{2,4},{3,5},{4,6},{5,7},{6,0},{7,1},{8,10},{9,11},{10,... | collective-permute-start | bytes 49160 | tf_op jit(solution)/shard_map/ppermute | solution.py:519
  32.5 5.6 %collective-permute-start.5 = (f32[32,128]{1,0:T(8,128)S(1)}, f32[32,128]{1,0:T(8,128)S(1)}, u32[]{:S(2)}, u32[]{:S(2)}) collective-permute-start(f32[32,128]{1,0:T(8,128)S(1)} %get-tuple-element.66), channel_id=1, source_target_pairs={{0,1},{1,2},{2,3},{3,4},{4,5},{5,6},{6,7},{7,0},{8,9},{9,10},{10,1... | collective-permute-start | bytes 49160 | tf_op jit(solution)/shard_map/ppermute | solution.py:519
  32.6 5.6 %collective-permute-start.6 = (f32[32,128]{1,0:T(8,128)S(1)}, f32[32,128]{1,0:T(8,128)S(1)}, u32[]{:S(2)}, u32[]{:S(2)}) collective-permute-start(f32[32,128]{1,0:T(8,128)S(1)} %get-tuple-element.67), channel_id=1, source_target_pairs={{0,7},{1,0},{2,1},{3,2},{4,3},{5,4},{6,5},{7,6},{8,15},{9,8},{10,9... | collective-permute-start | bytes 49160 | tf_op jit(solution)/shard_map/ppermute | solution.py:519
  36.1 3.7 %collective-permute-start.7 = (f32[32,128]{1,0:T(8,128)S(1)}, f32[32,128]{1,0:T(8,128)S(1)}, u32[]{:S(2)}, u32[]{:S(2)}) collective-permute-start(f32[32,128]{1,0:T(8,128)S(1)} %get-tuple-element.68), channel_id=1, source_target_pairs={{0,6},{1,7},{2,0},{3,1},{4,2},{5,3},{6,4},{7,5},{8,14},{9,15},{10,... | collective-permute-start | bytes 49160 | tf_op jit(solution)/shard_map/ppermute | solution.py:519
  40.3 18.3 %collective-permute-start.8 = (bf16[352,128]{1,0:T(8,128)(2,1)S(1)}, bf16[352,128]{1,0:T(8,128)(2,1)S(1)}, u32[]{:S(2)}, u32[]{:S(2)}) collective-permute-start(bf16[352,128]{1,0:T(8,128)(2,1)S(1)} %get-tuple-element.70), channel_id=1, source_target_pairs={{0,8},{8,0},{16,24},{24,16},{1,9},{9,1},{17,25},{25,17},{2,10},{10... | collective-permute-start | bytes 270344 | tf_op jit(solution)/shard_map/ppermute | solution.py:514
  55.2 5.4 %collective-permute-start.9 = (bf16[352,128]{1,0:T(8,128)(2,1)S(1)}, bf16[352,128]{1,0:T(8,128)(2,1)S(1)}, u32[]{:S(2)}, u32[]{:S(2)}) collective-permute-start(bf16[352,128]{1,0:T(8,128)(2,1)S(1)} %get-tuple-element.72), channel_id=1, source_target_pairs={{0,16},{8,24},{16,0},{24,8},{1,17},{9,25},{17,1},{25,9},{2,18},{10... | collective-permute-start | bytes 270344 | tf_op jit(solution)/shard_map/ppermute | solution.py:514
  60.6 4.6 %collective-permute-start.10 = (bf16[352,128]{1,0:T(8,128)(2,1)S(1)}, bf16[352,128]{1,0:T(8,128)(2,1)S(1)}, u32[]{:S(2)}, u32[]{:S(2)}) collective-permute-start(bf16[352,128]{1,0:T(8,128)(2,1)S(1)} %get-tuple-element.82), channel_id=1, source_target_pairs={{0,16},{8,24},{16,0},{24,8},{1,17},{9,25},{17,1},{25,9},{2,18},{10... | collective-permute-start | bytes 270344 | tf_op jit(solution)/shard_map/ppermute | solution.py:514
  62.7 4.5 %collective-permute-start.11 = (bf16[352,128]{1,0:T(8,128)(2,1)S(1)}, bf16[352,128]{1,0:T(8,128)(2,1)S(1)}, u32[]{:S(2)}, u32[]{:S(2)}) collective-permute-start(bf16[352,128]{1,0:T(8,128)(2,1)S(1)} %get-tuple-element.84), channel_id=1, source_target_pairs={{0,8},{8,0},{16,24},{24,16},{1,9},{9,1},{17,25},{25,17},{2,10},{10... | collective-permute-start | bytes 270344 | tf_op jit(solution)/shard_map/ppermute | solution.py:514
  73.0 1.6 %collective-permute-start.12 = (bf16[4,264,128]{2,1,0:T(8,128)(2,1)S(1)}, bf16[4,264,128]{2,1,0:T(8,128)(2,1)S(1)}, u32[]{:S(2)}, u32[]{:S(2)}) collective-permute-start(bf16[4,264,128]{2,1,0:T(8,128)(2,1)S(1)} %get-tuple-element.87), channel_id=1, source_target_pairs={{0,1},{1,0},{2,3},{3,2},{4,5},{5,4},{6,7},{7,6},{8,9},{9,8},{10,11... | collective-permute-start | bytes 811016 | tf_op jit(solution)/shard_map/ppermute | solution.py:514
  74.7 6.8 %collective-permute-start.13 = (bf16[264,128]{1,0:T(8,128)(2,1)S(1)}, bf16[264,128]{1,0:T(8,128)(2,1)S(1)}, u32[]{:S(2)}, u32[]{:S(2)}) collective-permute-start(bf16[264,128]{1,0:T(8,128)(2,1)S(1)} %get-tuple-element.89), channel_id=1, source_target_pairs={{0,2},{1,3},{2,0},{3,1},{4,6},{5,7},{6,4},{7,5},{8,10},{9,11},{10,... | collective-permute-start | bytes 202760 | tf_op jit(solution)/shard_map/ppermute | solution.py:514
  74.7 8.8 %collective-permute-start.14 = (bf16[264,128]{1,0:T(8,128)(2,1)S(1)}, bf16[264,128]{1,0:T(8,128)(2,1)S(1)}, u32[]{:S(2)}, u32[]{:S(2)}) collective-permute-start(bf16[264,128]{1,0:T(8,128)(2,1)S(1)} %get-tuple-element.90), channel_id=1, source_target_pairs={{0,4},{1,5},{2,6},{3,7},{4,0},{5,1},{6,2},{7,3},{8,12},{9,13},{10,... | collective-permute-start | bytes 202760 | tf_op jit(solution)/shard_map/ppermute | solution.py:514
  76.5 7.0 %collective-permute-start.15 = (bf16[264,128]{1,0:T(8,128)(2,1)S(1)}, bf16[264,128]{1,0:T(8,128)(2,1)S(1)}, u32[]{:S(2)}, u32[]{:S(2)}) collective-permute-start(bf16[264,128]{1,0:T(8,128)(2,1)S(1)} %get-tuple-element.91), channel_id=1, source_target_pairs={{0,6},{1,7},{2,4},{3,5},{4,2},{5,3},{6,0},{7,1},{8,14},{9,15},{10,... | collective-permute-start | bytes 202760 | tf_op jit(solution)/shard_map/ppermute | solution.py:514

commit v5 on v4

--- a/solution.py
+++ b/solution.py
@@ -26,7 +26,7 @@
     return pl.CostEstimate(flops=0, bytes_accessed=int(3e6 * microseconds), transcendentals=0)
 
 
-LIMIT = 34
+LIMIT = 30
 SMALL = pltpu.CompilerParams(vmem_limit_bytes=12 << 20)
 BF16 = jnp.bfloat16
 F32 = jnp.float32
@@ -97,6 +97,7 @@
         jnp.asarray(strain.reshape(STEPS * 48, 16 * PART)).astype(BF16),
         jnp.asarray(force.reshape(8 * SLOT, STEPS * 48)).astype(BF16),
         jnp.asarray(anal.reshape(ROWS, 3 * fourier), F32),
+        jnp.asarray(anal[:, :PART].reshape(GROUPS * PART, 3 * fourier), F32),
     )
 
 
@@ -386,25 +387,31 @@
     return own
 
 
+def without_gaps(value):
+    width = GROUPS * PART
+    row = lax.broadcasted_iota(jnp.int32, (ROWS, width), 0)
+    column = lax.broadcasted_iota(jnp.int32, (ROWS, width), 1)
+    chosen = row == lax.div(column, PART) * SLOT + lax.rem(column, PART)
+    value = jnp.dot(value.astype(BF16), jnp.where(chosen, 1.0, 0.0).astype(BF16), preferred_element_type=F32)
+    tall = value.shape[0] // 4 * 3
+    rest = jnp.concatenate([value[tall:, k * width // 3 : (k + 1) * width // 3] for k in range(3)], axis=0)
+    return jnp.concatenate([value[:tall], rest], axis=1)
+
+
+def with_rows_back(value):
+    width = GROUPS * PART
+    rest = value[:, width:]
+    short = rest.shape[0] // 3
+    rest = jnp.concatenate([rest[k * short : (k + 1) * short] for k in range(3)], axis=1)
+    return jnp.concatenate([value[:, :width], rest], axis=0)
+
+
 def interface_kernel(own_ref, map_ref, *refs, first):
-    returned, outs = refs[:-4], refs[-4:]
+    returned, (own_out, sent_out) = refs[:-2], refs[-2:]
     value = added_back(own_ref[...], map_ref, returned, first)
-    half = outs[0].shape[0]
-    for part, rows in enumerate((value[:half], value[half:])):
-        outs[part][...] = rows
-        outs[2 + part][...] = rows.astype(BF16)
-
-
-def join_kernel(own_a, got_a, own_b, got_b, a_ref, b_ref, sent_a, sent_b):
-    for own, got, ref, sent in ((own_a, got_a, a_ref, sent_a), (own_b, got_b, b_ref, sent_b)):
-        value = own[...] + got[...].astype(F32)
-        ref[...] = value
-        sent[...] = value.astype(BF16)
-
-
-def halves(n_rows):
-    sizes = (n_rows // 2, n_rows - n_rows // 2)
-    return [jax.ShapeDtypeStruct((size, ROWS), kind) for kind in (F32, BF16) for size in sizes]
+    upper = without_gaps(value)
+    own_out[...] = upper + without_gaps(value - value.astype(BF16).astype(F32))
+    sent_out[...] = upper.astype(BF16)
 
 
 def interleaved(value, scratch):
@@ -434,13 +441,15 @@
     du_ref[...] = separated(du, scratch).T
 
 
-def solve_kernel(load_ref, own_a, got_a, own_b, got_b, anal_ref, sinv_ref, *refs, peers):
-    away_ref, near_ref, scratch, total, rows = refs
+def solve_kernel(load_ref, anal_ref, own_ref, *refs, peers):
+    got_refs, (sinv_ref, away_ref, near_ref, scratch, total, rows) = refs[:-6], refs[-6:]
     depth_all = sinv_ref.shape[0]
     blocks = next(b for b in (4, 3, 2, 1) if b == 1 or depth_all % (b * 16) == 0)
     depth = depth_all // blocks
-    value = jnp.concatenate([own_a[...] + got_a[...].astype(F32), own_b[...] + got_b[...].astype(F32)], axis=0)
-    force = jnp.dot(value, anal_ref[...], precision=HIGHEST, preferred_element_type=F32)
+    value = own_ref[...]
+    for ref in got_refs:
+        value = value + ref[...].astype(F32)
+    force = jnp.dot(with_rows_back(value), anal_ref[...], precision=HIGHEST, preferred_element_type=F32)
     right = interleaved(load_ref[...].T - force, scratch).T.astype(BF16)
     for k in range(blocks):
         part = slice(k * depth, (k + 1) * depth)
@@ -456,12 +465,12 @@
         out_ref[j // 2] = jnp.concatenate([upper, lower], axis=1).astype(out_ref.dtype)
 
 
-def interface_solve(load, own_a, got_a, own_b, got_b, analysis, sinv, peers):
+def interface_solve(load, analysis, own, got, sinv, peers):
     depth, rows = sinv.shape
     fourier = load.shape[0] // 3
     shape = (peers // 2, rows // peers // 2, 2 * fourier)
     vmem = pl.BlockSpec(memory_space=pltpu.VMEM)
-    small = [load, own_a, got_a, own_b, got_b, analysis]
+    small = [load, analysis, own, *got]
     return pl.pallas_call(
         functools.partial(solve_kernel, peers=peers),
         in_specs=[vmem] * (len(small) + 1),
@@ -547,7 +556,7 @@
     blocks = send_blocks(u_int.T, u_if.T, send_map)
     halos = [passed_along(blocks[j], "dom", offsets[j]) for j in range(neighbours)]
     params = [x.reshape(1, -1) for x in (elem_size, stiffness, yield_stress, relax_rate)]
-    later = (sinv.T, kinv_int, load_int.T, load_if.T, analysis, send_map)
+    later = (sinv.T, kinv_int, load_int.T, load_if.T, analysis, send_map, tables[5])
     nodes, synth_high, synth_low, strain, force, near_conn, init, *params = (
         pltpu.with_memory_space_constraint(x, pltpu.VMEM)
         for x in prepare(u_int.T, u_if.T, neighbours * slots, [*tables[:4], conn.T, stress_init, *params])
@@ -564,14 +573,20 @@
         later,
     )
     back = more[:neighbours]
-    sinv_t, kinv, load_int_t, load_if_t, analysis, near_map = (
+    sinv_t, kinv, load_int_t, load_if_t, analysis, near_map, compact = (
         pltpu.with_memory_space_constraint(x, pltpu.VMEM) for x in more[neighbours:]
     )
     returned = [passed_along(back[j], "dom", -offsets[j]) for j in range(neighbours)]
 
-    part_a, part_b, sent_a, sent_b = pl.pallas_call(
-        functools.partial(interface_kernel, first=n_int), out_shape=halves(n_if), compiler_params=SMALL, cost_estimate=lasts(4), name="interface_forces"
+    packed = (n_if // 4 * 3, GROUPS * PART // 3 * 4)
+    own_force, sent_force = pl.pallas_call(
+        functools.partial(interface_kernel, first=n_int),
+        out_shape=[jax.ShapeDtypeStruct(packed, kind) for kind in (F32, BF16)],
+        compiler_params=SMALL,
+        cost_estimate=lasts(1),
+        name="interface_forces",
     )(p_if, near_map, *returned)
+    got_force = [swapped(sent_force, "grp", other) for other in range(1, lax.axis_size("grp"))]
 
     rhs_int = pl.pallas_call(
         interior_rhs_kernel,
@@ -580,15 +595,6 @@
         compiler_params=SMALL, cost_estimate=lasts(12), name="interior_rhs",
     )(p_int, near_map, *returned, load_int_t, analysis)
 
-    bits = [1 << b for b in range(lax.axis_size("grp").bit_length() - 1)]
-    for turn, (bit_a, bit_b) in enumerate(zip(bits, bits[::-1])):
-        if turn:
-            part_a, part_b, sent_a, sent_b = pl.pallas_call(
-                join_kernel, out_shape=halves(n_if), compiler_params=SMALL, cost_estimate=lasts(5), name="interface_sums"
-            )(part_a, got_a, part_b, got_b)
-            sent_a, sent_b, rhs_int = lax.optimization_barrier((sent_a, sent_b, rhs_int))
-        got_a, got_b = swapped(sent_a, "grp", bit_a), swapped(sent_b, "grp", bit_b)
-
     du_int = pl.pallas_call(
         interior_kernel,
         out_shape=jax.ShapeDtypeStruct((width, n_int), F32),
@@ -597,7 +603,7 @@
     )(rhs_int, kinv).T
 
     peers = lax.axis_size("dom")
-    sent, mine = interface_solve(load_if_t, part_a, got_a, part_b, got_b, analysis, sinv_t, peers)
+    sent, mine = interface_solve(load_if_t, compact, own_force, got_force, sinv_t, peers)
     bit = 1
     while True:
         got = swapped(sent, "dom", bit)

time: 83.2 us -> 80.1 us (0.963); the launches traced: 84.4 us -> 79.8 us
  Pallas kernels: 33.6 us -> 30.3 us
  waiting for transfers between devices: 13.6 us -> 11.6 us
    pallas_call x1, Pallas kernels: 17.5 us -> 13.8 us  [element_phase(): pl.pallas_call(functools.partial(element_kernel, neighbours=neighbours, c...]
    ppermute x8 -> x7, waiting for transfers between devices: 10 us -> 7.72 us  [swapped(): return lax.ppermute(shard, axis, [(i, i ^ bit) for i in range(peers)])]
    ppermute x8, starting transfers between devices: 11.9 us -> 13.1 us  [passed_along(): lax.ppermute(shard, axis, [(i, (i + by) % peers) for i in range(peers)])]
    ppermute x8 -> x7, starting transfers between devices: 23.3 us -> 22.7 us  [swapped(): return lax.ppermute(shard, axis, [(i, i ^ bit) for i in range(peers)])]
  transfers between devices with their start and end apart: 16 -> 15, of which waited for: 9 -> 8; matrix products, arithmetic and copies ran while one was open for 0% -> 0% of each run, Pallas kernels for 8% -> 8%
where the time goes in v5:
time: 80.1 us; the launch traced here: 79.8 us
  starting transfers between devices  35.8 us (45%)
  Pallas kernels  30.3 us (38%)
  waiting for transfers between devices  11.6 us (14%)
  between operations  1.4 us (2%)
    ppermute x7, starting transfers between devices, swapped(): return lax.ppermute(shard, axis, [(i, i ^ bit) for i in range(peers)])  22.7 us
    pallas_call x1, Pallas kernels, element_phase(): pl.pallas_call(functools.partial(element_kernel, neighbours=neighbours, c...  13.8 us
    ppermute x8, starting transfers between devices, passed_along(): lax.ppermute(shard, axis, [(i, (i + by) % peers) for i in range(peers)])  13.1 us
    ppermute x7, waiting for transfers between devices, swapped(): return lax.ppermute(shard, axis, [(i, i ^ bit) for i in range(peers)])  7.72 us
    pallas_call x1, Pallas kernels, interface_solve(): pl.pallas_call(functools.partial(solve_kernel, peers=peers), in_specs=[vm...  5.7 us
    ppermute x8, waiting for transfers between devices, passed_along(): lax.ppermute(shard, axis, [(i, (i + by) % peers) for i in range(peers)])  3.93 us
    pallas_call x1, Pallas kernels, prepare(): pl.pallas_call(prepare_kernel, in_specs=[vmem] * 2 + [pl.BlockSpec(memory...  2.55 us
    pallas_call x1, Pallas kernels, per_device(): pl.pallas_call(interior_kernel, out_shape=jax.ShapeDtypeStruct((width, n_...  2.38 us
  transfers between devices with their start and end apart: 15, of which 8 were waited for; matrix products, arithmetic and copies ran while one was open for 0% of the time, Pallas kernels for 8%

profile of v5, /device:TPU:0, one launch (start us, length us, event | category | flops | bytes accessed | tf_op | source)
XLA Modules:
  0.0 79.8 jit_solution(10757245793251118535)
XLA Ops:
  0.6 2.4 %halo_rows.1 = (bf16[32,192]{1,0:T(8,128)(2,1)}, bf16[32,192]{1,0:T(8,128)(2,1)}, bf16[32,192]{1,0:T(8,128)(2,1)}, bf16[32,192]{1,0:T(8,128)(2,1)}) custom-call(bf16[192,512]{1,0:T(8,128)(2,1)} %bitcast.14, bf16[192,704]{1,0:T(8,128)(2,1)} %bitcast.12, s32[4,32]{1,0:T(4,128)} %refs_21_.1), custom_call_target="tpu_custom_call" | custom-call | bytes 9000000 | tf_op jit(solution)/shard_map/halo_rows/pallas_call | solution.py:369
  3.0 5.1 %collective-permute-start = (bf16[32,192]{1,0:T(8,128)(2,1)}, bf16[32,192]{1,0:T(8,128)(2,1)S(1)}, u32[]{:S(2)}, u32[]{:S(2)}) collective-permute-start(bf16[32,192]{1,0:T(8,128)(2,1)} %get-tuple-element.41), channel_id=1, source_target_pairs={{0,6},{1,7},{2,0},{3,1},{4,2},{5,3},{6,4},{7,5},{8,14},{9,15},{10,... | collective-permute-start | bytes 36872 | tf_op jit(solution)/shard_map/ppermute | solution.py:528
  8.1 0.0 collective-permute-start.1
  8.1 0.5 collective-permute-start.2
  8.6 0.7 collective-permute-start.3
  9.9 2.6 %own_nodes.1 = (bf16[384,768]{1,0:T(8,128)(2,1)S(1)}, bf16[192,192]{1,0:T(8,128)(2,1)S(1)}, bf16[192,192]{1,0:T(8,128)(2,1)S(1)}, bf16[192,192]{1,0:T(8,128)(2,1...) custom-call(bf16[192,512]{1,0:T(8,128)(2,1)} %bitcast.15, ...), custom_call_target="tpu_custom_call" | custom-call | bytes 15000000 | tf_op jit(solution)/shard_map/own_nodes/pallas_call | solution.py:152
  12.5 0.0 collective-permute-done.refs_2_
  12.5 0.0 copy-start
  12.5 0.0 collective-permute-done.1.refs_3_
  12.5 0.0 copy-start.1
  12.5 0.7 collective-permute-done.2.refs_4_
  13.3 0.0 copy-start.2
  13.3 1.1 %collective-permute-done.3.refs_5_ = bf16[32,192]{1,0:T(8,128)(2,1)S(1)} collective-permute-done((bf16[32,192]{1,0:T(8,128)(2,1)}, bf16[32,192]{1,0:T(8,128)(2,1)S(1)}, u32[]{:S(2)}, u32[]{:S(2)}) %collective-permute-start.3) | collective-permute-done | bytes 12320 | tf_op jit(solution)/shard_map/ppermute | solution.py:528
  14.3 0.0 copy-start.3
  14.3 0.0 copy-done
  14.3 0.0 copy-done.1
  14.3 0.0 copy-done.2
  14.4 0.6 copy-done.3
  14.9 13.8 %elements.1 = (f32[48,2048]{1,0:T(8,128)}, f32[512,128]{1,0:T(8,128)S(1)}, f32[704,128]{1,0:T(8,128)S(1)}, f32[32,128]{1,0:T(8,128)S(1)}, f32[32,128]{1,0:T(8,12...) custom-call(s32[1]{0:T(128)S(6)} %copy.22.refs_0_, ...), custom_call_target="tpu_custom_call" | custom-call | bytes 120000000 | tf_op jit(solution)/shard_map/elements/pallas_call | solution.py:326
  28.8 0.1 collective-permute-start.4
  28.8 0.1 collective-permute-start.5
  28.9 5.1 %collective-permute-start.6 = (f32[32,128]{1,0:T(8,128)S(1)}, f32[32,128]{1,0:T(8,128)S(1)}, u32[]{:S(2)}, u32[]{:S(2)}) collective-permute-start(f32[32,128]{1,0:T(8,128)S(1)} %get-tuple-element.59), channel_id=1, source_target_pairs={{0,7},{1,0},{2,1},{3,2},{4,3},{5,4},{6,5},{7,6},{8,15},{9,8},{10,9... | collective-permute-start | bytes 49160 | tf_op jit(solution)/shard_map/ppermute | solution.py:528
  34.0 1.6 %collective-permute-start.7 = (f32[32,128]{1,0:T(8,128)S(1)}, f32[32,128]{1,0:T(8,128)S(1)}, u32[]{:S(2)}, u32[]{:S(2)}) collective-permute-start(f32[32,128]{1,0:T(8,128)S(1)} %get-tuple-element.60), channel_id=1, source_target_pairs={{0,6},{1,7},{2,0},{3,1},{4,2},{5,3},{6,4},{7,5},{8,14},{9,15},{10,... | collective-permute-start | bytes 49160 | tf_op jit(solution)/shard_map/ppermute | solution.py:528
  35.6 0.0 collective-permute-done.4.refs_0_
  35.6 0.0 collective-permute-done.5.refs_1_
  35.6 0.0 collective-permute-done.6.refs_2_
  35.7 2.1 %collective-permute-done.7.refs_3_ = f32[32,128]{1,0:T(8,128)S(1)} collective-permute-done((f32[32,128]{1,0:T(8,128)S(1)}, f32[32,128]{1,0:T(8,128)S(1)}, u32[]{:S(2)}, u32[]{:S(2)}) %collective-permute-start.7) | collective-permute-done | bytes 16416 | tf_op jit(solution)/shard_map/ppermute | solution.py:528
  37.8 1.0 %interface_forces.1 = (f32[528,128]{1,0:T(8,128)S(1)}, bf16[528,128]{1,0:T(8,128)(2,1)S(1)}) custom-call(f32[704,128]{1,0:T(8,128)S(1)} %get-tuple-element.66.own_ref, s32[4,32]{1,0:T(4,128)S(1)} %get-tuple-element.56.map_ref, f32[32,128]{1,0:T(8,128)S(1)} %collective-permute-done.4.refs_0_, f32[32,128]{1,0:T(8,128)S(1)} %collective-permute-done.5.refs_1_, ...), custom_call_target="tpu_custom_call" | custom-call | bytes 3000000 | tf_op jit(solution)/shard_map/interface_forces/pallas_call | solution.py:582
  38.8 15.3 %collective-permute-start.10 = (bf16[528,128]{1,0:T(8,128)(2,1)S(1)}, bf16[528,128]{1,0:T(8,128)(2,1)S(1)}, u32[]{:S(2)}, u32[]{:S(2)}) collective-permute-start(bf16[528,128]{1,0:T(8,128)(2,1)S(1)} %get-tuple-element.68), channel_id=1, source_target_pairs={{0,24},{8,16},{16,8},{24,0},{1,25},{9,17},{17,9},{25,1},{2,26},{10... | collective-permute-start | bytes 405512 | tf_op jit(solution)/shard_map/ppermute | solution.py:523
  54.1 2.9 %collective-permute-start.9 = (bf16[528,128]{1,0:T(8,128)(2,1)S(1)}, bf16[528,128]{1,0:T(8,128)(2,1)S(1)}, u32[]{:S(2)}, u32[]{:S(2)}) collective-permute-start(bf16[528,128]{1,0:T(8,128)(2,1)S(1)} %get-tuple-element.68), channel_id=1, source_target_pairs={{0,16},{8,24},{16,0},{24,8},{1,17},{9,25},{17,1},{25,9},{2,18},{10... | collective-permute-start | bytes 405512 | tf_op jit(solution)/shard_map/ppermute | solution.py:523
  57.0 0.0 collective-permute-start.8
  57.0 0.9 %collective-permute-done.10.refs_2_ = bf16[528,128]{1,0:T(8,128)(2,1)S(1)} collective-permute-done((bf16[528,128]{1,0:T(8,128)(2,1)S(1)}, bf16[528,128]{1,0:T(8,128)(2,1)S(1)}, u32[]{:S(2)}, u32[]{:S(2)}) %collective-permute-start.10) | collective-permute-done | bytes 135200 | tf_op jit(solution)/shard_map/ppermute | solution.py:523
  57.9 2.1 %collective-permute-done.9.refs_1_ = bf16[528,128]{1,0:T(8,128)(2,1)S(1)} collective-permute-done((bf16[528,128]{1,0:T(8,128)(2,1)S(1)}, bf16[528,128]{1,0:T(8,128)(2,1)S(1)}, u32[]{:S(2)}, u32[]{:S(2)}) %collective-permute-start.9) | collective-permute-done | bytes 135200 | tf_op jit(solution)/shard_map/ppermute | solution.py:523
  60.0 2.0 %collective-permute-done.8.refs_0_ = bf16[528,128]{1,0:T(8,128)(2,1)S(1)} collective-permute-done((bf16[528,128]{1,0:T(8,128)(2,1)S(1)}, bf16[528,128]{1,0:T(8,128)(2,1)S(1)}, u32[]{:S(2)}, u32[]{:S(2)}) %collective-permute-start.8) | collective-permute-done | bytes 135200 | tf_op jit(solution)/shard_map/ppermute | solution.py:523
  62.0 5.7 %interface_solve.1 = (bf16[4,264,128]{2,1,0:T(8,128)(2,1)S(1)}, f32[4,264,128]{2,1,0:T(8,128)S(1)}) custom-call(f32[192,704]{1,0:T(8,128)S(1)} %get-tuple-element.64.load_ref, f32[96,192]{1,0:T(8,128)S(1)} %get-tuple-element.65.anal_ref, f32[528,128]{1,0:T(8,128)S(1)} %get-tuple-element.67.own_ref, bf16[528,128]{1,0:T(8,128)(2,1)S(1)} %collective-permute-done.8.refs_0_, ...), custom_call_target="tpu_custom_call" | custom-call | bytes 30000000 | tf_op jit(solution)/shard_map/interface_solve/pallas_call | solution.py:474
  67.7 0.1 collective-permute-start.11
  67.8 1.5 %collective-permute-done.11.got_ref = bf16[4,264,128]{2,1,0:T(8,128)(2,1)S(1)} collective-permute-done((bf16[4,264,128]{2,1,0:T(8,128)(2,1)S(1)}, bf16[4,264,128]{2,1,0:T(8,128)(2,1)S(1)}, u32[]{:S(2)}, u32[]{:S(2)}) %collective-permute-start.11) | collective-permute-done | bytes 270368 | tf_op jit(solution)/shard_map/ppermute | solution.py:523
  69.3 0.1 correction_sums.1
  69.4 0.1 collective-permute-start.12
  69.5 3.2 %collective-permute-start.13 = (bf16[264,128]{1,0:T(8,128)(2,1)S(1)}, bf16[264,128]{1,0:T(8,128)(2,1)S(1)}, u32[]{:S(2)}, u32[]{:S(2)}) collective-permute-start(bf16[264,128]{1,0:T(8,128)(2,1)S(1)} %get-tuple-element.74), channel_id=1, source_target_pairs={{0,4},{1,5},{2,6},{3,7},{4,0},{5,1},{6,2},{7,3},{8,12},{9,13},{10,... | collective-permute-start | bytes 202760 | tf_op jit(solution)/shard_map/ppermute | solution.py:523
  72.7 1.1 %collective-permute-start.14 = (bf16[264,128]{1,0:T(8,128)(2,1)S(1)}, bf16[264,128]{1,0:T(8,128)(2,1)S(1)}, u32[]{:S(2)}, u32[]{:S(2)}) collective-permute-start(bf16[264,128]{1,0:T(8,128)(2,1)S(1)} %get-tuple-element.75), channel_id=1, source_target_pairs={{0,6},{1,7},{2,4},{3,5},{4,2},{5,3},{6,0},{7,1},{8,14},{9,15},{10,... | collective-permute-start | bytes 202760 | tf_op jit(solution)/shard_map/ppermute | solution.py:523
  73.8 1.5 %interior_rhs.1.rhs_ref = bf16[1536,64]{1,0:T(8,128)(2,1)S(1)} custom-call(f32[512,128]{1,0:T(8,128)S(1)} %get-tuple-element.55.own_ref, s32[4,32]{1,0:T(4,128)S(1)} %get-tuple-element.56.map_ref, f32[32,128]{1,0:T(8,128)S(1)} %collective-permute-done.4.refs_0_, f32[32,128]{1,0:T(8,128)S(1)} %collective-permute-done.5.refs_1_, ...), custom_call_target="tpu_custom_call" | custom-call | bytes 36000000 | tf_op jit(solution)/shard_map/interior_rhs/pallas_call | solution.py:591
  75.4 2.4 %interior_solve.1 = f32[192,512]{1,0:T(8,128)} custom-call(bf16[1536,64]{1,0:T(8,128)(2,1)S(1)} %interior_rhs.1.rhs_ref, bf16[1536,1536]{1,0:T(8,128)(2,1)S(1)} %get-tuple-element.63.kinv_ref), custom_call_target="tpu_custom_call" | custom-call | bytes 18000000 | tf_op jit(solution)/shard_map/interior_solve/pallas_call | solution.py:598
  77.7 0.0 collective-permute-done.12.refs_0_
  77.7 0.0 collective-permute-done.13.refs_1_
  77.8 1.2 %collective-permute-done.14.refs_2_ = bf16[264,128]{1,0:T(8,128)(2,1)S(1)} collective-permute-done((bf16[264,128]{1,0:T(8,128)(2,1)S(1)}, bf16[264,128]{1,0:T(8,128)(2,1)S(1)}, u32[]{:S(2)}, u32[]{:S(2)}) %collective-permute-start.14) | collective-permute-done | bytes 67616 | tf_op jit(solution)/shard_map/ppermute | solution.py:523
  78.9 0.9 %interface_result.1 = f32[176,192]{1,0:T(8,128)} custom-call(f32[264,128]{1,0:T(8,128)S(1)} %get-tuple-element.72.mine_ref, bf16[264,128]{1,0:T(8,128)(2,1)S(1)} %collective-permute-done.12.refs_0_, bf16[264,128]{1,0:T(8,128)(2,1)S(1)} %collective-permute-done.13.refs_1_, bf16[264,128]{1,0:T(8,128)(2,1)S(1)} %collective-permute-done.14.refs_2_), custom_call_target="tpu_custom_call" | custom-call | bytes 6000000 | tf_op jit(solution)/shard_map/interface_result/pallas_call | solution.py:618
Async XLA Ops:
  3.0 9.5 %collective-permute-start = (bf16[32,192]{1,0:T(8,128)(2,1)}, bf16[32,192]{1,0:T(8,128)(2,1)S(1)}, u32[]{:S(2)}, u32[]{:S(2)}) collective-permute-start(bf16[32,192]{1,0:T(8,128)(2,1)} %get-tuple-element.41), channel_id=1, source_target_pairs={{0,6},{1,7},{2,0},{3,1},{4,2},{5,3},{6,4},{7,5},{8,14},{9,15},{10,... | collective-permute-start | bytes 36872 | tf_op jit(solution)/shard_map/ppermute | solution.py:528
  8.1 4.4 %collective-permute-start.1 = (bf16[32,192]{1,0:T(8,128)(2,1)}, bf16[32,192]{1,0:T(8,128)(2,1)S(1)}, u32[]{:S(2)}, u32[]{:S(2)}) collective-permute-start(bf16[32,192]{1,0:T(8,128)(2,1)} %get-tuple-element.42), channel_id=1, source_target_pairs={{0,7},{1,0},{2,1},{3,2},{4,3},{5,4},{6,5},{7,6},{8,15},{9,8},{10,9... | collective-permute-start | bytes 36872 | tf_op jit(solution)/shard_map/ppermute | solution.py:528
  8.1 5.2 %collective-permute-start.2 = (bf16[32,192]{1,0:T(8,128)(2,1)}, bf16[32,192]{1,0:T(8,128)(2,1)S(1)}, u32[]{:S(2)}, u32[]{:S(2)}) collective-permute-start(bf16[32,192]{1,0:T(8,128)(2,1)} %get-tuple-element.43), channel_id=1, source_target_pairs={{0,1},{1,2},{2,3},{3,4},{4,5},{5,6},{6,7},{7,0},{8,9},{9,10},{10,1... | collective-permute-start | bytes 36872 | tf_op jit(solution)/shard_map/ppermute | solution.py:528
  8.6 5.7 %collective-permute-start.3 = (bf16[32,192]{1,0:T(8,128)(2,1)}, bf16[32,192]{1,0:T(8,128)(2,1)S(1)}, u32[]{:S(2)}, u32[]{:S(2)}) collective-permute-start(bf16[32,192]{1,0:T(8,128)(2,1)} %get-tuple-element.44), channel_id=1, source_target_pairs={{0,2},{1,3},{2,4},{3,5},{4,6},{5,7},{6,0},{7,1},{8,10},{9,11},{10,... | collective-permute-start | bytes 36872 | tf_op jit(solution)/shard_map/ppermute | solution.py:528
  12.5 1.9 %copy-start = (bf16[32,192]{1,0:T(8,128)(2,1)}, bf16[32,192]{1,0:T(8,128)(2,1)S(1)}, u32[]{:S(2)}) copy-start(bf16[32,192]{1,0:T(8,128)(2,1)S(1)} %collective-permute-done.refs_2_) | copy-start | bytes 36868
  12.5 1.8 %copy-start.1 = (bf16[32,192]{1,0:T(8,128)(2,1)}, bf16[32,192]{1,0:T(8,128)(2,1)S(1)}, u32[]{:S(2)}) copy-start(bf16[32,192]{1,0:T(8,128)(2,1)S(1)} %collective-permute-done.1.refs_3_) | copy-start | bytes 36868
  13.3 1.1 %copy-start.2 = (bf16[32,192]{1,0:T(8,128)(2,1)}, bf16[32,192]{1,0:T(8,128)(2,1)S(1)}, u32[]{:S(2)}) copy-start(bf16[32,192]{1,0:T(8,128)(2,1)S(1)} %collective-permute-done.2.refs_4_) | copy-start | bytes 36868
  14.3 0.6 copy-start.3
  28.8 6.9 %collective-permute-start.4 = (f32[32,128]{1,0:T(8,128)S(1)}, f32[32,128]{1,0:T(8,128)S(1)}, u32[]{:S(2)}, u32[]{:S(2)}) collective-permute-start(f32[32,128]{1,0:T(8,128)S(1)} %get-tuple-element.57), channel_id=1, source_target_pairs={{0,2},{1,3},{2,4},{3,5},{4,6},{5,7},{6,0},{7,1},{8,10},{9,11},{10,... | collective-permute-start | bytes 49160 | tf_op jit(solution)/shard_map/ppermute | solution.py:528
  28.8 6.8 %collective-permute-start.5 = (f32[32,128]{1,0:T(8,128)S(1)}, f32[32,128]{1,0:T(8,128)S(1)}, u32[]{:S(2)}, u32[]{:S(2)}) collective-permute-start(f32[32,128]{1,0:T(8,128)S(1)} %get-tuple-element.58), channel_id=1, source_target_pairs={{0,1},{1,2},{2,3},{3,4},{4,5},{5,6},{6,7},{7,0},{8,9},{9,10},{10,1... | collective-permute-start | bytes 49160 | tf_op jit(solution)/shard_map/ppermute | solution.py:528
  28.9 6.7 %collective-permute-start.6 = (f32[32,128]{1,0:T(8,128)S(1)}, f32[32,128]{1,0:T(8,128)S(1)}, u32[]{:S(2)}, u32[]{:S(2)}) collective-permute-start(f32[32,128]{1,0:T(8,128)S(1)} %get-tuple-element.59), channel_id=1, source_target_pairs={{0,7},{1,0},{2,1},{3,2},{4,3},{5,4},{6,5},{7,6},{8,15},{9,8},{10,9... | collective-permute-start | bytes 49160 | tf_op jit(solution)/shard_map/ppermute | solution.py:528
  34.0 3.7 %collective-permute-start.7 = (f32[32,128]{1,0:T(8,128)S(1)}, f32[32,128]{1,0:T(8,128)S(1)}, u32[]{:S(2)}, u32[]{:S(2)}) collective-permute-start(f32[32,128]{1,0:T(8,128)S(1)} %get-tuple-element.60), channel_id=1, source_target_pairs={{0,6},{1,7},{2,0},{3,1},{4,2},{5,3},{6,4},{7,5},{8,14},{9,15},{10,... | collective-permute-start | bytes 49160 | tf_op jit(solution)/shard_map/ppermute | solution.py:528
  38.8 19.1 %collective-permute-start.10 = (bf16[528,128]{1,0:T(8,128)(2,1)S(1)}, bf16[528,128]{1,0:T(8,128)(2,1)S(1)}, u32[]{:S(2)}, u32[]{:S(2)}) collective-permute-start(bf16[528,128]{1,0:T(8,128)(2,1)S(1)} %get-tuple-element.68), channel_id=1, source_target_pairs={{0,24},{8,16},{16,8},{24,0},{1,25},{9,17},{17,9},{25,1},{2,26},{10... | collective-permute-start | bytes 405512 | tf_op jit(solution)/shard_map/ppermute | solution.py:523
  54.1 5.9 %collective-permute-start.9 = (bf16[528,128]{1,0:T(8,128)(2,1)S(1)}, bf16[528,128]{1,0:T(8,128)(2,1)S(1)}, u32[]{:S(2)}, u32[]{:S(2)}) collective-permute-start(bf16[528,128]{1,0:T(8,128)(2,1)S(1)} %get-tuple-element.68), channel_id=1, source_target_pairs={{0,16},{8,24},{16,0},{24,8},{1,17},{9,25},{17,1},{25,9},{2,18},{10... | collective-permute-start | bytes 405512 | tf_op jit(solution)/shard_map/ppermute | solution.py:523
  57.0 5.0 %collective-permute-start.8 = (bf16[528,128]{1,0:T(8,128)(2,1)S(1)}, bf16[528,128]{1,0:T(8,128)(2,1)S(1)}, u32[]{:S(2)}, u32[]{:S(2)}) collective-permute-start(bf16[528,128]{1,0:T(8,128)(2,1)S(1)} %get-tuple-element.68), channel_id=1, source_target_pairs={{0,8},{8,0},{16,24},{24,16},{1,9},{9,1},{17,25},{25,17},{2,10},{10... | collective-permute-start | bytes 405512 | tf_op jit(solution)/shard_map/ppermute | solution.py:523
  67.7 1.6 %collective-permute-start.11 = (bf16[4,264,128]{2,1,0:T(8,128)(2,1)S(1)}, bf16[4,264,128]{2,1,0:T(8,128)(2,1)S(1)}, u32[]{:S(2)}, u32[]{:S(2)}) collective-permute-start(bf16[4,264,128]{2,1,0:T(8,128)(2,1)S(1)} %get-tuple-element.71), channel_id=1, source_target_pairs={{0,1},{1,0},{2,3},{3,2},{4,5},{5,4},{6,7},{7,6},{8,9},{9,8},{10,11... | collective-permute-start | bytes 811016 | tf_op jit(solution)/shard_map/ppermute | solution.py:523
  69.4 8.4 %collective-permute-start.12 = (bf16[264,128]{1,0:T(8,128)(2,1)S(1)}, bf16[264,128]{1,0:T(8,128)(2,1)S(1)}, u32[]{:S(2)}, u32[]{:S(2)}) collective-permute-start(bf16[264,128]{1,0:T(8,128)(2,1)S(1)} %get-tuple-element.73), channel_id=1, source_target_pairs={{0,2},{1,3},{2,0},{3,1},{4,6},{5,7},{6,4},{7,5},{8,10},{9,11},{10,... | collective-permute-start | bytes 202760 | tf_op jit(solution)/shard_map/ppermute | solution.py:523
  69.5 8.2 %collective-permute-start.13 = (bf16[264,128]{1,0:T(8,128)(2,1)S(1)}, bf16[264,128]{1,0:T(8,128)(2,1)S(1)}, u32[]{:S(2)}, u32[]{:S(2)}) collective-permute-start(bf16[264,128]{1,0:T(8,128)(2,1)S(1)} %get-tuple-element.74), channel_id=1, source_target_pairs={{0,4},{1,5},{2,6},{3,7},{4,0},{5,1},{6,2},{7,3},{8,12},{9,13},{10,... | collective-permute-start | bytes 202760 | tf_op jit(solution)/shard_map/ppermute | solution.py:523
  72.7 6.2 %collective-permute-start.14 = (bf16[264,128]{1,0:T(8,128)(2,1)S(1)}, bf16[264,128]{1,0:T(8,128)(2,1)S(1)}, u32[]{:S(2)}, u32[]{:S(2)}) collective-permute-start(bf16[264,128]{1,0:T(8,128)(2,1)S(1)} %get-tuple-element.75), channel_id=1, source_target_pairs={{0,6},{1,7},{2,4},{3,5},{4,2},{5,3},{6,0},{7,1},{8,14},{9,15},{10,... | collective-permute-start | bytes 202760 | tf_op jit(solution)/shard_map/ppermute | solution.py:523
